TPU v7x, 32 devices: a whole 2x2x4 slice. The times are simulated.
32 devices in a mesh: row: 16 (over z, y, core), col: 2 (over x).
Axes of the slice: x: 2, y: 2, z: 4, core: 2. Of those that a mesh axis runs over, the one named last changes fastest.
Arguments:
- tokens: bfloat16 [18464, 1024], P('row', 'col'), may hold values from -6 to 6
- first_gain: float32 [1024], P(('row', 'col')), may hold values from 0.5 to 1.5
- first_shift: float32 [1024], P(('row', 'col')), may hold values from -1.75 to 1.75
- mixer_weight: float32 [1024, 3, 1024], P('row', None, 'col'), may hold values from -0.1875 to 0.1875
- mixer_bias: float32 [2, 1024], P(None, ('row', 'col')), may hold values from -1.75 to 1.75
- merge_weight: float32 [1024, 1024], P('col', 'row'), may hold values from -2 to 2
- merge_bias: float32 [1024], P(('row', 'col')), may hold values from -1.75 to 1.75
- second_gain: float32 [1024], P(('row', 'col')), may hold values from 0.5 to 1.5
- second_shift: float32 [1024], P(('row', 'col')), may hold values from -1.75 to 1.75
- expand_weight: float32 [1024, 4096], P('row', 'col'), may hold values from -0.1875 to 0.1875
- expand_bias: float32 [4096], P(('row', 'col')), may hold values from -1.75 to 1.75
- reduce_weight: float32 [4096, 1024], P('col', 'row'), may hold values from -0.09375 to 0.09375
- reduce_bias: float32 [1024], P(('row', 'col')), may hold values from -1.75 to 1.75
- cotangent: bfloat16 [18464, 1024], P('row', 'col'), may hold values from -6 to 6
Outputs:
- layer_output: bfloat16 [18464, 1024], P('row', 'col')
- tokens_gradient: float32 [18464, 1024], P('row', 'col')
- first_gain_gradient: float32 [1024], P(('row', 'col'))
- first_shift_gradient: float32 [1024], P(('row', 'col'))
- mixer_weight_gradient: float32 [1024, 3, 1024], P('row', None, 'col')
- mixer_bias_gradient: float32 [2, 1024], P(None, ('row', 'col'))
- merge_weight_gradient: float32 [1024, 1024], P('col', 'row')
- merge_bias_gradient: float32 [1024], P(('row', 'col'))
- second_gain_gradient: float32 [1024], P(('row', 'col'))
- second_shift_gradient: float32 [1024], P(('row', 'col'))
- expand_weight_gradient: float32 [1024, 4096], P('row', 'col')
- expand_bias_gradient: float32 [4096], P(('row', 'col'))
- reduce_weight_gradient: float32 [4096, 1024], P('col', 'row')
- reduce_bias_gradient: float32 [1024], P(('row', 'col'))
All inputs are finite; a program needn't handle non-finite values.
Results may differ from a plain program's by a relative error of at most 0.02.
Values may be sent and summed in bfloat16 or wider, within the bound.
A program may use at most 128 MiB of HBM per device.

v0:
```python
import jax
import jax.numpy as jnp
from jax import lax
from jax.sharding import PartitionSpec as P

HEAD_DIM = 64
SEQ = 577


EPSILON = 1e-05
SLOPE = 1.702


def quick_gelu(inputs):
    return inputs * jax.nn.sigmoid(SLOPE * inputs)


def gelu_slope(inputs):
    sigmoid_value = jax.nn.sigmoid(SLOPE * inputs)
    return sigmoid_value + SLOPE * inputs * sigmoid_value * (1.0 - sigmoid_value)


def own_columns(values, start, width):
    return lax.dynamic_slice_in_dim(values, start, width, values.ndim - 1)


def normalize(values, gain_row, shift_row):
    feature_count = values.shape[-1]
    row_mean = jnp.sum(values, -1, keepdims=True) / feature_count
    square = jnp.sum(values * values, -1, keepdims=True) / feature_count
    inverse = lax.rsqrt(square - row_mean * row_mean + EPSILON)
    scaled = (values - row_mean) * inverse
    return (scaled, inverse, scaled * gain_row + shift_row)


def column_sum(partial_value):
    return lax.psum_scatter(
        partial_value.astype(jnp.bfloat16), "col", scatter_dimension=1, tiled=True
    ).astype(jnp.float32)


def feature_totals(first_sum, second_sum):
    return lax.psum((first_sum, second_sum), "col")


def normed_gather(piece):
    return lax.all_gather(piece, "col", axis=1, tiled=True)


def shared_back(upstream, scaled, inverse, gain_row, feature_count):
    scaled_grad = upstream * gain_row
    totals = feature_totals(jnp.sum(scaled_grad, -1), jnp.sum(scaled_grad * scaled, -1))
    first_mean = totals[0][:, None] / feature_count
    second_mean = totals[1][:, None] / feature_count
    return inverse * (scaled_grad - first_mean - scaled * second_mean)


def fetch_weights(masters):
    return (
        lax.all_gather(masters[0], "row", axis=0, tiled=True),
        lax.all_gather(masters[1], "row", axis=1, tiled=True),
        lax.all_gather(masters[2], "row", axis=0, tiled=True),
        lax.all_gather(masters[3], "row", axis=1, tiled=True),
    )


def attend_forward(parts):
    queries, key_rows, values = parts
    score_scale = queries.shape[-1] ** (-0.5)
    scores = (
        jnp.einsum("qhd,khd->hqk", queries, key_rows, preferred_element_type=jnp.float32)
        * score_scale
    )
    score_top = jnp.max(scores, -1, keepdims=True)
    exponent = jnp.exp(scores - score_top)
    row_total = jnp.sum(exponent, -1, keepdims=True)
    weights = (exponent / row_total).astype(jnp.bfloat16)
    mixture = jnp.einsum("hqk,khd->qhd", weights, values, preferred_element_type=jnp.float32)
    return (mixture.astype(jnp.bfloat16), (score_top + jnp.log(row_total))[..., 0])


def attend_back(parts):
    queries, key_rows, values, log_total, upstream = parts
    score_scale = queries.shape[-1] ** (-0.5)
    scores = (
        jnp.einsum("qhd,khd->hqk", queries, key_rows, preferred_element_type=jnp.float32)
        * score_scale
    )
    probability = jnp.exp(scores - log_total[..., None])
    rounded = probability.astype(jnp.bfloat16)
    pulled = jnp.einsum("qhd,khd->hqk", upstream, values, preferred_element_type=jnp.float32)
    centre = jnp.sum(probability * pulled, -1, keepdims=True)
    score_grad = (probability * (pulled - centre)).astype(jnp.bfloat16)
    query_grad = (
        jnp.einsum("hqk,khd->qhd", score_grad, key_rows, preferred_element_type=jnp.float32)
        * score_scale
    )
    key_grad = (
        jnp.einsum("hqk,qhd->khd", score_grad, queries, preferred_element_type=jnp.float32)
        * score_scale
    )
    value_grad = jnp.einsum("hqk,qhd->khd", rounded, upstream, preferred_element_type=jnp.float32)
    return (query_grad, key_grad, value_grad)


def shards(
    tokens,
    first_gain,
    first_shift,
    mixer_weight,
    mixer_bias,
    merge_weight,
    merge_bias,
    second_gain,
    second_shift,
    expand_weight,
    expand_bias,
    reduce_weight,
    reduce_bias,
    cotangent,
):
    col_index = lax.axis_index("col")
    piece_width = tokens.shape[1]
    hidden_width = expand_weight.shape[1]
    start = col_index * piece_width
    hidden_start = col_index * hidden_width
    vector_pieces = jnp.stack(
        [
            first_gain,
            first_shift,
            mixer_bias[0],
            mixer_bias[1],
            merge_bias,
            second_gain,
            second_shift,
            reduce_bias,
        ]
    ).astype(jnp.bfloat16)
    vectors_low, expand_shift_low = (
        lax.all_gather(vector_pieces, ("row", "col"), axis=1, tiled=True),
        lax.all_gather(expand_bias.astype(jnp.bfloat16), ("row", "col"), axis=0, tiled=True),
    )
    vectors = vectors_low.astype(jnp.float32)
    feature_count = vectors.shape[1]
    first_gain_row, first_shift_row = (vectors[0], vectors[1])
    query_bias = own_columns(vectors[2], start, piece_width)
    value_bias = own_columns(vectors[3], start, piece_width)
    merge_shift = vectors[4]
    second_gain_row, second_shift_row = (vectors[5], vectors[6])
    reduce_shift = own_columns(vectors[7], start, piece_width)
    expand_shift = own_columns(expand_shift_low.astype(jnp.float32), hidden_start, hidden_width)
    masters = (
        mixer_weight.astype(jnp.bfloat16),
        merge_weight.astype(jnp.bfloat16),
        expand_weight.astype(jnp.bfloat16),
        reduce_weight.astype(jnp.bfloat16),
    )
    mixer_local, merger, expander, reducer = fetch_weights(masters)
    inputs_whole, upstream_whole = (
        lax.all_gather(tokens, "col", axis=1, tiled=True),
        lax.all_gather(cotangent, "col", axis=1, tiled=True),
    )
    inputs = inputs_whole.astype(jnp.float32)
    row_count = inputs.shape[0]
    first_scaled, first_inverse, first_normed = normalize(inputs, first_gain_row, first_shift_row)
    first_low = first_normed.astype(jnp.bfloat16)
    projected = jnp.einsum(
        "rd,dtc->rtc", first_low, mixer_local, preferred_element_type=jnp.float32
    )
    projected = projected + jnp.stack([query_bias, jnp.zeros_like(query_bias), value_bias])
    projected_low = projected.astype(jnp.bfloat16)
    head_shape = (row_count // SEQ, SEQ, piece_width // HEAD_DIM, HEAD_DIM)
    queries = projected_low[:, 0].reshape(head_shape)
    key_rows = projected_low[:, 1].reshape(head_shape)
    values = projected_low[:, 2].reshape(head_shape)
    attended, log_total = lax.map(attend_forward, (queries, key_rows, values))
    attended = attended.reshape(row_count, piece_width)
    merged_part = jnp.dot(attended, merger, preferred_element_type=jnp.float32)
    hidden_own = (
        own_columns(inputs, start, piece_width)
        + column_sum(merged_part)
        + own_columns(merge_shift, start, piece_width)
    )
    totals = feature_totals(jnp.sum(hidden_own, -1), jnp.sum(hidden_own * hidden_own, -1))
    row_mean = totals[0][:, None] / feature_count
    square = totals[1][:, None] / feature_count
    second_inverse = lax.rsqrt(square - row_mean * row_mean + EPSILON)
    second_scaled = (hidden_own - row_mean) * second_inverse
    second_gain_own = own_columns(second_gain_row, start, piece_width)
    second_piece = second_scaled * second_gain_own + own_columns(
        second_shift_row, start, piece_width
    )
    second_low = normed_gather(second_piece.astype(jnp.bfloat16))
    expanded = jnp.dot(second_low, expander, preferred_element_type=jnp.float32) + expand_shift
    activated = quick_gelu(expanded).astype(jnp.bfloat16)
    reduced = column_sum(jnp.dot(activated, reducer, preferred_element_type=jnp.float32))
    layer_output = (hidden_own + reduced + reduce_shift).astype(jnp.bfloat16)
    masters_again = lax.optimization_barrier((masters, layer_output))[0]
    mixer_local, merger, expander, reducer = fetch_weights(masters_again)
    upstream_own = cotangent.astype(jnp.float32)
    reducer_grad = jnp.einsum(
        "rf,rd->fd", activated, upstream_whole, preferred_element_type=jnp.float32
    )
    activated_grad = jnp.einsum(
        "rd,fd->rf", upstream_whole, reducer, preferred_element_type=jnp.float32
    )
    expanded_grad = (activated_grad * gelu_slope(expanded)).astype(jnp.bfloat16)
    expander_grad = jnp.einsum(
        "rd,rf->df", second_low, expanded_grad, preferred_element_type=jnp.float32
    )
    expand_shift_grad = jnp.sum(expanded_grad.astype(jnp.float32), 0)
    second_part = jnp.einsum(
        "rf,df->rd", expanded_grad, expander, preferred_element_type=jnp.float32
    )
    second_grad = column_sum(second_part)
    hidden_part = shared_back(
        second_grad, second_scaled, second_inverse, second_gain_own, feature_count
    )
    hidden_grad = upstream_own + hidden_part
    second_gain_grad = jnp.sum(second_grad * second_scaled, 0)
    second_shift_grad = jnp.sum(second_grad, 0)
    hidden_low = normed_gather(hidden_grad.astype(jnp.bfloat16))
    merger_grad = jnp.einsum("rc,rd->cd", attended, hidden_low, preferred_element_type=jnp.float32)
    attended_grad = jnp.einsum(
        "rd,cd->rc", hidden_low, merger, preferred_element_type=jnp.float32
    ).astype(jnp.bfloat16)
    query_grad, key_grad, value_grad = lax.map(
        attend_back, (queries, key_rows, values, log_total, attended_grad.reshape(head_shape))
    )
    projected_grad = jnp.stack(
        [
            query_grad.reshape(row_count, piece_width),
            key_grad.reshape(row_count, piece_width),
            value_grad.reshape(row_count, piece_width),
        ],
        1,
    ).astype(jnp.bfloat16)
    mixer_grad = jnp.einsum(
        "rd,rtc->dtc", first_low, projected_grad, preferred_element_type=jnp.float32
    )
    bias_sums = jnp.sum(projected_grad.astype(jnp.float32), 0)
    first_part = jnp.einsum(
        "rtc,dtc->rd", projected_grad, mixer_local, preferred_element_type=jnp.float32
    )
    first_grad = column_sum(first_part)
    first_scaled_own = own_columns(first_scaled, start, piece_width)
    input_part = shared_back(
        first_grad,
        first_scaled_own,
        first_inverse,
        own_columns(first_gain_row, start, piece_width),
        feature_count,
    )
    tokens_gradient = hidden_grad + input_part
    own_vector_grads = jnp.stack(
        [
            jnp.sum(first_grad * first_scaled_own, 0),
            jnp.sum(first_grad, 0),
            bias_sums[0],
            bias_sums[2],
            jnp.sum(hidden_grad, 0),
            second_gain_grad,
            second_shift_grad,
            jnp.sum(upstream_own, 0),
        ]
    )
    vector_whole = lax.dynamic_update_slice(
        jnp.zeros((8, feature_count), jnp.float32), own_vector_grads, (jnp.int32(0), start)
    )
    expand_whole = lax.dynamic_update_slice(
        jnp.zeros((hidden_width * lax.axis_size("col"),), jnp.float32),
        expand_shift_grad,
        (hidden_start,),
    )
    vector_total, expand_bias_total = (
        lax.psum_scatter(vector_whole, ("row", "col"), scatter_dimension=1, tiled=True),
        lax.psum_scatter(expand_whole, ("row", "col"), scatter_dimension=0, tiled=True),
    )
    mixer_total, merge_total, expand_total, reduce_total = (
        lax.psum_scatter(
            mixer_grad.astype(jnp.bfloat16), "row", scatter_dimension=0, tiled=True
        ).astype(jnp.float32),
        lax.psum_scatter(
            merger_grad.astype(jnp.bfloat16), "row", scatter_dimension=1, tiled=True
        ).astype(jnp.float32),
        lax.psum_scatter(
            expander_grad.astype(jnp.bfloat16), "row", scatter_dimension=0, tiled=True
        ).astype(jnp.float32),
        lax.psum_scatter(
            reducer_grad.astype(jnp.bfloat16), "row", scatter_dimension=1, tiled=True
        ).astype(jnp.float32),
    )
    return (
        layer_output,
        tokens_gradient,
        vector_total[0],
        vector_total[1],
        mixer_total,
        jnp.stack([vector_total[2], vector_total[3]]),
        merge_total,
        vector_total[4],
        vector_total[5],
        vector_total[6],
        expand_total,
        expand_bias_total,
        reduce_total,
        vector_total[7],
    )


def solution(mesh):
    return jax.shard_map(
        shards,
        mesh=mesh,
        in_specs=(
            P("row", "col"),
            P(("row", "col")),
            P(("row", "col")),
            P("row", None, "col"),
            P(None, ("row", "col")),
            P("col", "row"),
            P(("row", "col")),
            P(("row", "col")),
            P(("row", "col")),
            P("row", "col"),
            P(("row", "col")),
            P("col", "row"),
            P(("row", "col")),
            P("row", "col"),
        ),
        out_specs=(
            P("row", "col"),
            P("row", "col"),
            P(("row", "col")),
            P(("row", "col")),
            P("row", None, "col"),
            P(None, ("row", "col")),
            P("col", "row"),
            P(("row", "col")),
            P(("row", "col")),
            P(("row", "col")),
            P("row", "col"),
            P(("row", "col")),
            P("col", "row"),
            P(("row", "col")),
        ),
        check_vma=False,
    )
```

profile of v0, /device:TPU:28, one launch (start us, length us, event | category | flops | bytes accessed | tf_op | source)
XLA Modules:
  0.0 1154.1 jit_solution(11184303092411313592)
XLA Ops:
  14.1 59.2 %all-gather = bf16[32,32,8]{1,2,0:T(8,128)(2,1)S(1)} all-gather(bf16[1,32,8]{1,2,0:T(8,128)(2,1)S(1)} %bitcast.211), channel_id=1, replica_groups=mesh['row'=16,'col'=2] {'row','col'}, dimensions={0}, use_global_device_ids=true | all-gather | bytes 16896 | tf_op jit(solution)/shard_map/all_gather | solution.py:140
  76.9 16.3 %all-gather.17.cloned.1.call-done = bf16[1024,3,512]{2,0,1:T(8,128)(2,1)} async-done(((bf16[64,3,512]{2,0,1:T(8,128)(2,1)}), bf16[1024,3,512]{2,0,1:T(8,128)(2,1)}) %all-gather.17.cloned.1.call-update) | async-done | bytes 3145744 | tf_op jit(solution)/shard_map/all_gather | solution.py:60
  93.2 6.7 add_convert_fusion
  103.8 3.3 copy.75
  109.7 3.3 copy.74
  113.0 4.1 reshape.126
  117.1 4.1 copy.73
  121.2 16.9 %while.26 = (s32[]{:T(128)}, bf16[2,577,8,64]{1,3,2,0:T(8,128)(2,1)}, f32[2,8,577]{2,1,0:T(8,128)S(1)}, bf16[2,577,8,64]{1,3,2,0:T(8,128)(2,1)}, bf16[2,577,8,64...) while((s32[]{:T(128)}, bf16[2,577,8,64]{1,3,2,0:T(8,128)(2,1)}, ...), condition=%wide.region_5.6_spmd, body=%wide.region_2.5_spmd.sunk | while | flops 706100224 | bytes 50229580 | solution.py:176
  125.9 2.9 fusion.118
  134.1 2.9 fusion.118
  138.1 3.7 copy.76
  141.8 4.0 reshape.110
  145.8 4.7 convolution_convert_fusion.4
  152.4 4.5 convert_element_type.122
  156.8 29.7 %reduce-scatter.12.cloned.1.call-done = bf16[1154,512]{1,0:T(8,128)(2,1)} async-done(((bf16[1154,1024]{1,0:T(8,128)(2,1)}), bf16[1154,512]{1,0:T(8,128)(2,1)}) %reduce-scatter.12.cloned.1.call-update) | async-done | bytes 1181712 | tf_op jit(solution)/shard_map/reduce_scatter | solution.py:37
  186.5 3.8 fusion.71
  190.3 7.1 all-reduce.3
  197.5 3.2 add_convert_fusion.3
  201.6 57.2 %all-gather.1 = bf16[32,1,128]{2,1,0:T(2,128)(2,1)S(1)} all-gather(bf16[1,1,128]{2,1,0:T(2,128)(2,1)S(1)} %convert_bitcast_fusion), channel_id=1, replica_groups=mesh['row'=16,'col'=2] {'row','col'}, dimensions={0}, use_global_device_ids=true | all-gather | bytes 8448 | tf_op jit(solution)/shard_map/all_gather | solution.py:141
  258.9 17.5 %all-gather.21.cloned.1.call-done = bf16[1154,1024]{1,0:T(8,128)(2,1)} async-done(((bf16[1154,512]{1,0:T(8,128)(2,1)}), bf16[1154,1024]{1,0:T(8,128)(2,1)}) %all-gather.21.cloned.1.call-update) | async-done | bytes 2363408 | tf_op jit(solution)/shard_map/all_gather | solution.py:47
  276.4 12.0 %multiply_convert_fusion.1 = (bf16[1154,2048]{1,0:T(8,128)(2,1)}, f32[1154,2048]{1,0:T(8,128)}) fusion(f32[2048]{0:T(1024)S(1)} %dynamic_slice.62, bf16[1154,1024]{1,0:T(8,128)(2,1)} %all-gather.21.cloned.1.call-done, bf16[1024,2048]{1,0:T(8,128)(2,1)} %all-gather.23.cloned.1.call-done), kind=kOutput, calls=%fused_computation.60 | convolution fusion | flops 4856770560 | bytes 20746240 | tf_op jit(solution)/shard_map/dot_general | solution.py:194
  288.4 38.8 %all-gather.25.cloned.1.call-done = bf16[2048,1024]{0,1:T(8,128)(2,1)} async-done(((bf16[2048,64]{0,1:T(8,128)(2,1)}), bf16[2048,1024]{0,1:T(8,128)(2,1)}) %all-gather.25.cloned.1.call-update) | async-done | bytes 4194320 | tf_op jit(solution)/shard_map/all_gather | solution.py:63
  327.1 9.4 convolution_convert_fusion.3
  337.4 35.2 %reduce-scatter.14.cloned.1.call-done = bf16[1154,512]{1,0:T(8,128)(2,1)} async-done(((bf16[1154,1024]{1,0:T(8,128)(2,1)}), bf16[1154,512]{1,0:T(8,128)(2,1)}) %reduce-scatter.14.cloned.1.call-update) | async-done | bytes 1181712 | tf_op jit(solution)/shard_map/reduce_scatter | solution.py:37
  372.6 3.4 add_convert_fusion.2
  376.8 33.6 %all-gather.29.cloned.1.call-done = bf16[1154,1024]{1,0:T(8,128)(2,1)} async-done(((bf16[1154,512]{1,0:T(8,128)(2,1)}), bf16[1154,1024]{1,0:T(8,128)(2,1)}) %all-gather.29.cloned.1.call-update) | async-done | bytes 2363408 | tf_op jit(solution)/shard_map/all_gather | solution.py:161
  410.4 50.6 %all-gather.27.cloned.1.call-done = bf16[2048,1024]{0,1:T(8,128)(2,1)} async-done(((bf16[2048,64]{0,1:T(8,128)(2,1)}), bf16[2048,1024]{0,1:T(8,128)(2,1)}) %all-gather.27.cloned.1.call-update) | async-done | bytes 4194320 | tf_op jit(solution)/shard_map/all_gather | solution.py:63
  461.0 14.2 %convert_reduce_fusion = (f32[2048]{0:T(1024)}, bf16[1154,2048]{1,0:T(8,128)(2,1)}) fusion(f32[1154,2048]{1,0:T(8,128)} %get-tuple-element.234, bf16[2048,1024]{0,1:T(8,128)(2,1)} %all-gather.27.cloned.1.call-done, bf16[1154,1024]{1,0:T(8,128)(2,1)} %all-gather.29.cloned.1.call-done), kind=kOutput, calls=%fused_computation.59 | convolution fusion | flops 4868585472 | bytes 20746240 | tf_op jit(solution)/shard_map/rd,fd->rf/dot_general | solution.py:204
  475.2 37.5 %all-gather.31.cloned.1.call-done = bf16[1024,2048]{1,0:T(8,128)(2,1)} async-done(((bf16[64,2048]{1,0:T(8,128)(2,1)}), bf16[1024,2048]{1,0:T(8,128)(2,1)}) %all-gather.31.cloned.1.call-update) | async-done | bytes 4194320 | tf_op jit(solution)/shard_map/all_gather | solution.py:62
  512.7 9.5 convolution_convert_fusion.2
  523.0 35.3 %reduce-scatter.16.cloned.1.call-done = bf16[1154,512]{1,0:T(8,128)(2,1)} async-done(((bf16[1154,1024]{1,0:T(8,128)(2,1)}), bf16[1154,512]{1,0:T(8,128)(2,1)}) %reduce-scatter.16.cloned.1.call-update) | async-done | bytes 1181712 | tf_op jit(solution)/shard_map/reduce_scatter | solution.py:37
  558.3 3.9 fusion.66
  562.1 7.1 all-reduce.2
  569.3 3.5 fusion.72
  576.1 9.7 convolution_convert_fusion
  586.3 9.7 convolution_convert_fusion.1
  597.0 38.6 %all-gather.33.cloned.1.call-done = bf16[1154,1024]{1,0:T(8,128)(2,1)} async-done(((bf16[1154,512]{1,0:T(8,128)(2,1)}), bf16[1154,1024]{1,0:T(8,128)(2,1)}) %all-gather.33.cloned.1.call-update) | async-done | bytes 2363408 | tf_op jit(solution)/shard_map/all_gather | solution.py:47
  635.5 4.4 convolution_convert_fusion.5
  639.9 4.1 reshape.120
  644.0 4.1 copy.80
  648.1 41.6 %while.27 = (s32[]{:T(128)}, bf16[2,577,8,64]{1,3,2,0:T(8,128)(2,1)}, bf16[2,577,8,64]{1,3,2,0:T(8,128)(2,1)}, bf16[2,577,8,64]{1,3,2,0:T(8,128)(2,1)}, bf16[2,5...) while((s32[]{:T(128)}, ...), condition=%wide.region_19.20_spmd, body=%wide.region_17.19_spmd.sunk | while | flops 1737143808 | bytes 129908368 | solution.py:227
  652.4 5.7 multiply_reduce_fusion.7
  658.2 6.3 multiply_convert_fusion.3
  673.1 5.8 multiply_reduce_fusion.7
  678.9 6.4 multiply_convert_fusion.3
  689.7 3.3 copy.96
  695.6 3.5 copy.94
  701.7 3.3 copy.95
  705.1 2.8 reshape.122
  710.2 4.6 convolution_convert_fusion.7
  715.0 2.8 constant_dynamic-update-slice_fusion.1
  720.2 8.1 convolution_convert_fusion.6
  728.4 8.5 bitcast_convert_fusion
  737.0 2.8 subtract_multiply_fusion
  739.8 16.5 %reduce-scatter.26.cloned.1.call-done = bf16[2048,64]{0,1:T(8,128)(2,1)} async-done(((bf16[2048,1024]{0,1:T(8,128)(2,1)}), bf16[2048,64]{0,1:T(8,128)(2,1)}) %reduce-scatter.26.cloned.1.call-update) | async-done | bytes 262160 | tf_op jit(solution)/shard_map/reduce_scatter | solution.py:289
  758.3 42.0 %all-reduce = f32[4096]{0:T(1024)S(1)} all-reduce(f32[4096]{0:T(1024)S(1)} %dynamic_update_slice.25), channel_id=10, replica_groups=mesh['row'=16,'col'=2] {'row','col'}, use_global_device_ids=true, to_apply=%region_37.38.clone | all-reduce | flops 4096 | bytes 32768
  800.9 31.5 %reduce-scatter.24.cloned.1.call-done = bf16[64,2048]{1,0:T(8,128)(2,1)} async-done(((bf16[1024,2048]{1,0:T(8,128)(2,1)}), bf16[64,2048]{1,0:T(8,128)(2,1)}) %reduce-scatter.24.cloned.1.call-update) | async-done | bytes 262160 | tf_op jit(solution)/shard_map/reduce_scatter | solution.py:286
  836.8 56.1 %reduce-scatter.22.cloned.1.call-done = bf16[512,64]{0,1:T(8,128)(2,1)} async-done(((bf16[512,1024]{0,1:T(8,128)(2,1)}), bf16[512,64]{0,1:T(8,128)(2,1)}) %reduce-scatter.22.cloned.1.call-update) | async-done | bytes 65552 | tf_op jit(solution)/shard_map/reduce_scatter | solution.py:283
  894.3 67.6 %reduce-scatter.20.cloned.1.call-done = bf16[64,3,512]{2,0,1:T(8,128)(2,1)} async-done(((bf16[1024,3,512]{2,0,1:T(8,128)(2,1)}), bf16[64,3,512]{2,0,1:T(8,128)(2,1)}) %reduce-scatter.20.cloned.1.call-update) | async-done | bytes 196624 | tf_op jit(solution)/shard_map/reduce_scatter | solution.py:280
  963.6 36.3 %reduce-scatter.18.cloned.1.call-done = bf16[1154,512]{1,0:T(8,128)(2,1)} async-done(((bf16[1154,1024]{1,0:T(8,128)(2,1)}), bf16[1154,512]{1,0:T(8,128)(2,1)}) %reduce-scatter.18.cloned.1.call-update) | async-done | bytes 1181712 | tf_op jit(solution)/shard_map/reduce_scatter | solution.py:37
  999.9 3.0 fusion.67
  1002.9 7.1 all-reduce.1
  1011.2 3.6 fusion.61
  1014.9 126.2 %reduce-scatter.28.cloned.1.call-done = f32[32,8]{1,0:T(8,128)} async-done(((f32[1024,8]{1,0:T(8,128)}), f32[32,8]{1,0:T(8,128)}) %reduce-scatter.28.cloned.1.call-update) | async-done | bytes 1040
  (215 shorter events, 81.5 us)
Async XLA Ops:
  7.2 67.1 %all-gather.15.cloned.1.call-start = ((), (), s32[]{:S(2)}) async-start(), calls=%async_computation.9 | async-start | bytes 3563520 | tf_op jit(solution)/shard_map/all_gather | solution.py:160
  7.9 85.2 %all-gather.17.cloned.1.call-start = ((), (), s32[]{:S(2)}) async-start(), calls=%async_computation.10 | async-start | bytes 3342336 | tf_op jit(solution)/shard_map/all_gather | solution.py:60
  9.7 136.1 %all-gather.19.cloned.1.call-start = ((), (), s32[]{:S(2)}) async-start(), calls=%async_computation.11 | async-start | bytes 1114112 | tf_op jit(solution)/shard_map/all_gather | solution.py:61
  11.3 175.2 %reduce-scatter.12.cloned.1.call-start = ((), (), s32[]{:S(2)}) async-start(), calls=%async_computation.12 | async-start | bytes 3563520 | tf_op jit(solution)/shard_map/reduce_scatter | solution.py:37
  74.1 19.1 %copy-start.21 = (f32[1,1024]{1,0:T(1,128)}, f32[1,1024]{1,0:T(1,128)S(1)}, u32[]{:S(2)}) copy-start(f32[1,1024]{1,0:T(1,128)S(1)} %get-tuple-element.220) | copy-start | bytes 12292
  74.1 19.1 %copy-start.29 = (f32[1,1024]{1,0:T(1,128)}, f32[1,1024]{1,0:T(1,128)S(1)}, u32[]{:S(2)}) copy-start(f32[1,1024]{1,0:T(1,128)S(1)} %get-tuple-element.219) | copy-start | bytes 12292
  74.2 18.9 %copy-start.1 = (bf16[1154,1024]{1,0:T(8,128)(2,1)S(1)}, bf16[1154,1024]{1,0:T(8,128)(2,1)}, u32[]{:S(2)}) copy-start(bf16[1154,1024]{1,0:T(8,128)(2,1)} %all-gather.15.cloned.1.call-done) | copy-start | bytes 7090180
  76.8 16.3 %copy-start.17 = (f32[1154]{0:T(1024)}, f32[1154]{0:T(1024)S(1)}, u32[]{:S(2)}) copy-start(f32[1154]{0:T(1024)S(1)} %get-tuple-element.232) | copy-start | bytes 13852
  76.9 16.3 %copy-start.19 = (f32[1154]{0:T(1024)}, f32[1154]{0:T(1024)S(1)}, u32[]{:S(2)}) copy-start(f32[1154]{0:T(1024)S(1)} %get-tuple-element.231) | copy-start | bytes 13852
  123.8 2.1 copy-start.5
  123.8 2.1 copy-start.7
  128.8 1.1 copy-start.8
  132.0 2.1 copy-start.5
  132.0 2.1 copy-start.7
  137.0 1.1 copy-start.8
  150.5 1.0 copy-start.15
  150.5 108.4 %all-gather.23.cloned.1.call-start = ((), (), s32[]{:S(2)}) async-start(), calls=%async_computation.14 | async-start | bytes 4456448 | tf_op jit(solution)/shard_map/all_gather | solution.py:62
  152.3 124.1 %all-gather.21.cloned.1.call-start = ((), (), s32[]{:S(2)}) async-start(), calls=%async_computation.13 | async-start | bytes 3563520 | tf_op jit(solution)/shard_map/all_gather | solution.py:47
  197.4 3.3 copy-start.16
  197.5 4.2 copy-start.31
  200.7 126.4 %all-gather.25.cloned.1.call-start = ((), (), s32[]{:S(2)}) async-start(), calls=%async_computation.15 | async-start | bytes 4456448 | tf_op jit(solution)/shard_map/all_gather | solution.py:63
  201.6 171.0 %reduce-scatter.14.cloned.1.call-start = ((), (), s32[]{:S(2)}) async-start(), calls=%async_computation.16 | async-start | bytes 3563520 | tf_op jit(solution)/shard_map/reduce_scatter | solution.py:37
  336.6 0.8 copy-start.23
  336.6 73.9 %all-gather.29.cloned.1.call-start = ((), (), s32[]{:S(2)}) async-start(), calls=%async_computation.18 | async-start | bytes 3563520 | tf_op jit(solution)/shard_map/all_gather | solution.py:161
  337.3 123.7 %all-gather.27.cloned.1.call-start = ((), (), s32[]{:S(2)}) async-start(), calls=%async_computation.17 | async-start | bytes 4456448 | tf_op jit(solution)/shard_map/all_gather | solution.py:63
  376.0 136.7 %all-gather.31.cloned.1.call-start = ((), (), s32[]{:S(2)}) async-start(), calls=%async_computation.19 | async-start | bytes 4456448 | tf_op jit(solution)/shard_map/all_gather | solution.py:62
  376.8 181.5 %reduce-scatter.16.cloned.1.call-start = ((), (), s32[]{:S(2)}) async-start(), calls=%async_computation.20 | async-start | bytes 3563520 | tf_op jit(solution)/shard_map/reduce_scatter | solution.py:37
  522.2 74.8 %all-gather.35.cloned.1.call-start = ((), (), s32[]{:S(2)}) async-start(), calls=%async_computation.22 | async-start | bytes 1114112 | tf_op jit(solution)/shard_map/all_gather | solution.py:61
  523.0 112.6 %all-gather.33.cloned.1.call-start = ((), (), s32[]{:S(2)}) async-start(), calls=%async_computation.21 | async-start | bytes 3563520 | tf_op jit(solution)/shard_map/all_gather | solution.py:47
  572.8 1.4 copy-start.3
  575.5 152.9 %all-gather.37.cloned.1.call-start = ((), (), s32[]{:S(2)}) async-start(), calls=%async_computation.23 | async-start | bytes 3342336 | tf_op jit(solution)/shard_map/all_gather | solution.py:60
  576.1 180.2 %reduce-scatter.26.cloned.1.call-start = ((), (), s32[]{:S(2)}) async-start(), calls=%async_computation.28 | async-start | bytes 4456448 | tf_op jit(solution)/shard_map/reduce_scatter | solution.py:289
  585.8 246.6 %reduce-scatter.24.cloned.1.call-start = ((), (), s32[]{:S(2)}) async-start(), calls=%async_computation.27 | async-start | bytes 4456448 | tf_op jit(solution)/shard_map/reduce_scatter | solution.py:286
  596.1 296.8 %reduce-scatter.22.cloned.1.call-start = ((), (), s32[]{:S(2)}) async-start(), calls=%async_computation.26 | async-start | bytes 1114112 | tf_op jit(solution)/shard_map/reduce_scatter | solution.py:283
  648.1 2.1 copy-start
  648.1 2.1 copy-start.9
  650.2 2.2 copy-start.6
  652.4 5.7 copy-start.10
  658.2 6.4 copy-start.11
  664.5 1.9 copy-start.13
  666.5 1.2 copy-start.12
  667.7 1.1 copy-start.14
  668.8 2.1 copy-start
  668.8 2.1 copy-start.9
  670.9 2.2 copy-start.6
  673.1 5.8 copy-start.10
  678.9 6.5 copy-start.11
  685.4 1.9 copy-start.13
  687.3 1.2 copy-start.12
  688.5 1.1 copy-start.14
  714.9 5.3 copy-start.2
  714.9 5.3 copy-start.18
  714.9 5.3 copy-start.20
  714.9 5.2 copy-start.22
  714.9 5.2 copy-start.30
  714.9 247.0 %reduce-scatter.20.cloned.1.call-start = ((), (), s32[]{:S(2)}) async-start(), calls=%async_computation.25 | async-start | bytes 3342336 | tf_op jit(solution)/shard_map/reduce_scatter | solution.py:280
  728.3 271.6 %reduce-scatter.18.cloned.1.call-start = ((), (), s32[]{:S(2)}) async-start(), calls=%async_computation.24 | async-start | bytes 3563520 | tf_op jit(solution)/shard_map/reduce_scatter | solution.py:37
  736.9 404.2 %reduce-scatter.28.cloned.1.call-start = ((), (), s32[]{:S(2)}) async-start(), calls=%async_computation.29 | async-start | bytes 540672
  737.0 21.1 %copy-start.28 = (f32[2048]{0:T(1024)S(1)}, f32[2048]{0:T(1024)}, u32[]{:S(2)}) copy-start(f32[2048]{0:T(1024)} %get-tuple-element.235) | copy-start | bytes 24580
  836.7 173.4 %copy-start.24 = (f32[512]{0:T(512)S(1)}, f32[512]{0:T(512)}, u32[]{:S(2)}) copy-start(f32[512]{0:T(512)} %get-tuple-element.156) | copy-start | bytes 6148
  836.7 173.4 %copy-start.25 = (f32[512]{0:T(512)S(1)}, f32[512]{0:T(512)}, u32[]{:S(2)}) copy-start(f32[512]{0:T(512)} %get-tuple-element.164) | copy-start | bytes 6148
  836.7 173.4 %copy-start.26 = (f32[512]{0:T(512)S(1)}, f32[512]{0:T(512)}, u32[]{:S(2)}) copy-start(f32[512]{0:T(512)} %get-tuple-element.202) | copy-start | bytes 6148
  836.7 173.4 %copy-start.27 = (f32[512]{0:T(512)S(1)}, f32[512]{0:T(512)}, u32[]{:S(2)}) copy-start(f32[512]{0:T(512)} %get-tuple-element.212) | copy-start | bytes 6148
  999.9 11.3 copy-start.4
Sparse Core Ops, SparseCore 0:
  9.5 37.8 all-gather.14
  50.2 42.9 all-gather.16
  95.9 36.8 all-gather.18
  150.6 35.8 reduce-scatter.11
  189.1 48.0 all-gather.22
  239.1 37.1 all-gather.20
  279.1 47.9 all-gather.24
  336.7 35.8 reduce-scatter.13
  374.2 36.2 all-gather.28
  413.0 47.9 all-gather.26
  463.8 48.9 all-gather.30
  522.3 35.8 reduce-scatter.15
  561.0 35.9 all-gather.34
  598.3 37.1 all-gather.32
  638.1 42.9 all-gather.36
  684.8 71.4 reduce-scatter.25
  760.0 72.3 reduce-scatter.23
  835.9 56.9 reduce-scatter.21
  896.6 65.2 reduce-scatter.19
  964.0 35.8 reduce-scatter.17
  1011.3 129.6 reduce-scatter.27
where the time goes:
time: 1170 us; the launch traced here: 1150 us
  waiting for transfers between devices  672 us (57%)
  blocking collectives  180 us (15%)
  matrix products  138 us (12%)
  local copies, waits for them, and re-layouts  78.5 us (7%)
  other arithmetic  69.3 us (6%)
  between operations  15.1 us (1%)
    reduce_scatter x4, waiting for transfers between devices, column_sum(): lax.psum_scatter(partial_value.astype(jnp.bfloat16), 'col', scatter_dimen...  137 us
    unnamed x22, waiting for transfers between devices  130 us
    all_gather x2, waiting for transfers between devices, fetch_weights(): lax.all_gather(masters[3], 'row', axis=1, tiled=True)  89.4 us
    reduce_scatter x1, waiting for transfers between devices, shards(): lax.psum_scatter(mixer_grad.astype(jnp.bfloat16), 'row', scatter_dimensio...  67.6 us
    all_gather x1, blocking collectives, shards(): lax.all_gather(vector_pieces, ('row', 'col'), axis=1, tiled=True)  59.2 us
    all_gather x1, blocking collectives, shards(): lax.all_gather(expand_bias.astype(jnp.bfloat16), ('row', 'col'), axis=0,...  57.2 us
    all_gather x2, waiting for transfers between devices, normed_gather(): return lax.all_gather(piece, 'col', axis=1, tiled=True)  56.1 us
    reduce_scatter x1, waiting for transfers between devices, shards(): lax.psum_scatter(merger_grad.astype(jnp.bfloat16), 'row', scatter_dimensi...  56.1 us
  transfers between devices with their start and end apart: 21, of which 17 were waited for; matrix products, arithmetic and copies ran while one was open for 21% of the time, Pallas kernels for 0%

commit v1 on v0

--- a/solution.py
+++ b/solution.py
@@ -1,6 +1,8 @@
 import jax
 import jax.numpy as jnp
 from jax import lax
+from jax.experimental import pallas as pl
+from jax.experimental.pallas import tpu as pltpu
 from jax.sharding import PartitionSpec as P
 
 HEAD_DIM = 64
@@ -103,7 +105,7 @@
     return (query_grad, key_grad, value_grad)
 
 
-def shards(
+def split_shards(
     tokens,
     first_gain,
     first_shift,
@@ -308,9 +310,313 @@
     )
 
 
+GROUP = 128
+BOTH = ("col", "row")
+
+
+def attention_forward_kernel(projected_ref, attended_ref):
+    for head in range(GROUP // HEAD_DIM):
+        at = head * HEAD_DIM
+        queries = projected_ref[0, :, at : at + HEAD_DIM] * jnp.bfloat16(HEAD_DIM**-0.5)
+        key_rows = projected_ref[0, :, GROUP + at : GROUP + at + HEAD_DIM]
+        values = projected_ref[0, :, 2 * GROUP + at : 2 * GROUP + at + HEAD_DIM]
+        scores = lax.dot_general(
+            key_rows, queries, (((1,), (1,)), ((), ())), preferred_element_type=jnp.float32
+        )
+        exponent = jnp.exp(scores - jnp.max(scores, 0, keepdims=True))
+        weights = exponent * (1.0 / jnp.sum(exponent, 0, keepdims=True))
+        mixture = lax.dot_general(
+            values,
+            weights.astype(jnp.bfloat16),
+            (((0,), (0,)), ((), ())),
+            preferred_element_type=jnp.float32,
+        )
+        attended_ref[0, :, at : at + HEAD_DIM] = mixture.T.astype(jnp.bfloat16)
+
+
+def attention_back_kernel(projected_ref, upstream_ref, grad_ref):
+    for head in range(GROUP // HEAD_DIM):
+        at = head * HEAD_DIM
+        queries = projected_ref[0, :, at : at + HEAD_DIM] * jnp.bfloat16(HEAD_DIM**-0.5)
+        key_rows = projected_ref[0, :, GROUP + at : GROUP + at + HEAD_DIM]
+        values = projected_ref[0, :, 2 * GROUP + at : 2 * GROUP + at + HEAD_DIM]
+        upstream = upstream_ref[0, :, at : at + HEAD_DIM]
+        scores = lax.dot_general(
+            key_rows, queries, (((1,), (1,)), ((), ())), preferred_element_type=jnp.float32
+        )
+        exponent = jnp.exp(scores - jnp.max(scores, 0, keepdims=True))
+        weights = exponent * (1.0 / jnp.sum(exponent, 0, keepdims=True))
+        pulled = lax.dot_general(
+            values, upstream, (((1,), (1,)), ((), ())), preferred_element_type=jnp.float32
+        )
+        centre = jnp.sum(weights * pulled, 0, keepdims=True)
+        score_grad = (weights * (pulled - centre)).astype(jnp.bfloat16)
+        value_grad = jnp.dot(
+            weights.astype(jnp.bfloat16), upstream, preferred_element_type=jnp.float32
+        )
+        key_grad = jnp.dot(score_grad, queries, preferred_element_type=jnp.float32)
+        query_grad = lax.dot_general(
+            key_rows, score_grad, (((0,), (0,)), ((), ())), preferred_element_type=jnp.float32
+        )
+        query_grad = query_grad.T * HEAD_DIM**-0.5
+        grad_ref[0, :, at : at + HEAD_DIM] = query_grad.astype(jnp.bfloat16)
+        grad_ref[0, :, GROUP + at : GROUP + at + HEAD_DIM] = key_grad.astype(jnp.bfloat16)
+        grad_ref[0, :, 2 * GROUP + at : 2 * GROUP + at + HEAD_DIM] = value_grad.astype(
+            jnp.bfloat16
+        )
+
+
+def attention_forward(projected):
+    halves, rows, width = projected.shape
+    groups = width // (3 * GROUP)
+    return pl.pallas_call(
+        attention_forward_kernel,
+        grid=(halves, groups),
+        in_specs=[pl.BlockSpec((1, rows, 3 * GROUP), lambda h, g: (h, 0, g))],
+        out_specs=pl.BlockSpec((1, rows, GROUP), lambda h, g: (h, 0, g)),
+        out_shape=jax.ShapeDtypeStruct((halves, rows, groups * GROUP), jnp.bfloat16),
+        name="attention_forward",
+    )(projected)
+
+
+def attention_back(projected, upstream):
+    halves, rows, width = projected.shape
+    groups = width // (3 * GROUP)
+    return pl.pallas_call(
+        attention_back_kernel,
+        grid=(halves, groups),
+        in_specs=[
+            pl.BlockSpec((1, rows, 3 * GROUP), lambda h, g: (h, 0, g)),
+            pl.BlockSpec((1, rows, GROUP), lambda h, g: (h, 0, g)),
+        ],
+        out_specs=pl.BlockSpec((1, rows, 3 * GROUP), lambda h, g: (h, 0, g)),
+        out_shape=jax.ShapeDtypeStruct(projected.shape, jnp.bfloat16),
+        name="attention_back",
+    )(projected, upstream)
+
+
+def to_image(piece):
+    col = lax.axis_index("col")
+    rows = piece.shape[0] // 2
+    kept = lax.dynamic_slice_in_dim(piece, col * rows, rows, 0)
+    sent = lax.dynamic_slice_in_dim(piece, (1 - col) * rows, rows, 0)
+    other = lax.ppermute(sent, "col", [(0, 1), (1, 0)])
+    return jnp.where(
+        col == 0, jnp.concatenate([kept, other], 1), jnp.concatenate([other, kept], 1)
+    )
+
+
+def from_image(whole):
+    col = lax.axis_index("col")
+    width = whole.shape[1] // 2
+    kept = lax.dynamic_slice_in_dim(whole, col * width, width, 1)
+    sent = lax.dynamic_slice_in_dim(whole, (1 - col) * width, width, 1)
+    other = lax.ppermute(sent, "col", [(0, 1), (1, 0)])
+    return jnp.where(
+        col == 0, jnp.concatenate([kept, other], 0), jnp.concatenate([other, kept], 0)
+    )
+
+
+def gather_blocks(block):
+    whole = lax.all_gather(block, BOTH, axis=0, tiled=True)
+    return whole.reshape(2, whole.shape[0] // 2, block.shape[1])
+
+
+def scatter_blocks(halves):
+    flat = jnp.concatenate(halves, 0)
+    return lax.psum_scatter(flat, BOTH, scatter_dimension=0, tiled=True).astype(jnp.float32)
+
+
+def product(left, right, left_at, right_at):
+    return lax.dot_general(
+        left, right, (((left_at,), (right_at,)), ((), ())), preferred_element_type=jnp.float32
+    )
+
+
+def norm_back(upstream, scaled, inverse, gain_row):
+    scaled_grad = upstream * gain_row
+    first_mean = jnp.mean(scaled_grad, -1, keepdims=True)
+    second_mean = jnp.mean(scaled_grad * scaled, -1, keepdims=True)
+    return inverse * (scaled_grad - first_mean - scaled * second_mean)
+
+
+def group_order(block):
+    rows = block.shape[0]
+    return block.reshape(rows, 3, -1, GROUP).transpose(0, 2, 1, 3).reshape(rows, -1)
+
+
+def part_order(block):
+    rows = block.shape[0]
+    return block.reshape(rows, -1, 3, GROUP).transpose(0, 2, 1, 3).reshape(rows, 3, -1)
+
+
+def image_shards(
+    tokens,
+    first_gain,
+    first_shift,
+    mixer_weight,
+    mixer_bias,
+    merge_weight,
+    merge_bias,
+    second_gain,
+    second_shift,
+    expand_weight,
+    expand_bias,
+    reduce_weight,
+    reduce_bias,
+    cotangent,
+):
+    low = jnp.bfloat16
+    cols = lax.axis_size("col")
+    rows = lax.axis_size("row")
+    piece = first_gain.shape[0]
+    hidden_piece = expand_bias.shape[0]
+    block_rows = mixer_weight.shape[0]
+    vectors = jnp.concatenate(
+        [
+            jnp.stack(
+                [
+                    first_gain,
+                    first_shift,
+                    mixer_bias[0],
+                    mixer_bias[1],
+                    merge_bias,
+                    second_gain,
+                    second_shift,
+                    reduce_bias,
+                ]
+            ).reshape(-1),
+            expand_bias,
+        ]
+    ).astype(low)
+    vector_rows = vectors.shape[0] // GROUP
+    vector_block = jnp.pad(
+        vectors.reshape(vector_rows, GROUP), ((0, block_rows - vector_rows), (0, 0))
+    )
+    mixer_width = 3 * mixer_weight.shape[2]
+    first_block = jnp.concatenate([group_order(mixer_weight).astype(low), vector_block], 1)
+    mixed = gather_blocks(first_block)
+    mixer = mixed[:, :, :mixer_width]
+    merger = gather_blocks(merge_weight.astype(low).T)
+    expander = gather_blocks(expand_weight.astype(low))
+    reducer = gather_blocks(reduce_weight.astype(low).T)
+    spread = mixed[:, :, mixer_width:].reshape(cols, rows, block_rows, GROUP)[:, :, :vector_rows]
+    spread = spread.reshape(cols, rows, -1).astype(jnp.float32).transpose(1, 0, 2)
+    rows_of = spread[:, :, : 8 * piece].reshape(rows, cols, 8, piece).transpose(2, 0, 1, 3)
+    rows_of = rows_of.reshape(8, -1)
+    expand_shift = spread[:, :, 8 * piece :].reshape(cols, -1)
+    first_gain_row, first_shift_row = rows_of[0], rows_of[1]
+    query_bias, value_bias, merge_shift = rows_of[2], rows_of[3], rows_of[4]
+    second_gain_row, second_shift_row, reduce_shift = rows_of[5], rows_of[6], rows_of[7]
+    mixer_shift = jnp.stack(
+        [
+            query_bias.reshape(cols, -1, GROUP),
+            jnp.zeros_like(query_bias).reshape(cols, -1, GROUP),
+            value_bias.reshape(cols, -1, GROUP),
+        ],
+        2,
+    ).reshape(cols, -1)
+
+    image = to_image(tokens)
+    upstream_low = to_image(cotangent)
+    inputs = image.astype(jnp.float32)
+    first_scaled, first_inverse, first_normed = normalize(inputs, first_gain_row, first_shift_row)
+    first_low = first_normed.astype(low)
+    projected = jnp.stack(
+        [(product(first_low, mixer[h], 1, 0) + mixer_shift[h]).astype(low) for h in range(cols)]
+    )
+    attended = attention_forward(projected)
+    merged = sum(product(attended[h], merger[h], 1, 1) for h in range(cols))
+    hidden = inputs + merged + merge_shift
+    second_scaled, second_inverse, second_normed = normalize(
+        hidden, second_gain_row, second_shift_row
+    )
+    second_low = second_normed.astype(low)
+    expanded = [product(second_low, expander[h], 1, 0) + expand_shift[h] for h in range(cols)]
+    activated = [quick_gelu(part).astype(low) for part in expanded]
+    reduced = sum(product(activated[h], reducer[h], 1, 1) for h in range(cols))
+    layer_output = from_image((hidden + reduced + reduce_shift).astype(low))
+
+    upstream = upstream_low.astype(jnp.float32)
+    reducer_grad = [product(upstream_low, activated[h], 0, 0).astype(low) for h in range(cols)]
+    reduce_total = scatter_blocks(reducer_grad)
+    expanded_grad = [
+        (product(upstream_low, reducer[h], 1, 0) * gelu_slope(expanded[h])).astype(low)
+        for h in range(cols)
+    ]
+    expander_grad = [product(second_low, expanded_grad[h], 0, 0).astype(low) for h in range(cols)]
+    expand_total = scatter_blocks(expander_grad)
+    expand_shift_grad = [jnp.sum(part.astype(jnp.float32), 0) for part in expanded_grad]
+    second_grad = sum(product(expanded_grad[h], expander[h], 1, 1) for h in range(cols))
+    hidden_grad = upstream + norm_back(
+        second_grad, second_scaled, second_inverse, second_gain_row
+    )
+    hidden_low = hidden_grad.astype(low)
+    merger_grad = [product(hidden_low, attended[h], 0, 0).astype(low) for h in range(cols)]
+    merge_total = scatter_blocks(merger_grad)
+    attended_grad = jnp.stack(
+        [product(hidden_low, merger[h], 1, 0).astype(low) for h in range(cols)]
+    )
+    projected_grad = attention_back(projected, attended_grad)
+    mixer_grad = [product(first_low, projected_grad[h], 0, 0).astype(low) for h in range(cols)]
+    bias_sums = jnp.sum(projected_grad.astype(jnp.float32), 1)
+    bias_sums = bias_sums.reshape(cols, -1, 3, GROUP).transpose(2, 0, 1, 3).reshape(3, -1)
+    first_grad = sum(product(projected_grad[h], mixer[h], 1, 1) for h in range(cols))
+    input_grad = hidden_grad + norm_back(first_grad, first_scaled, first_inverse, first_gain_row)
+    tokens_gradient = from_image(input_grad.astype(low)).astype(jnp.float32)
+    vector_grads = jnp.stack(
+        [
+            jnp.sum(first_grad * first_scaled, 0),
+            jnp.sum(first_grad, 0),
+            bias_sums[0],
+            bias_sums[2],
+            jnp.sum(hidden_grad, 0),
+            jnp.sum(second_grad * second_scaled, 0),
+            jnp.sum(second_grad, 0),
+            jnp.sum(upstream, 0),
+        ]
+    )
+    vector_grads = vector_grads.reshape(8, rows, cols, piece).transpose(2, 1, 0, 3)
+    hidden_grads = jnp.concatenate(expand_shift_grad).reshape(rows, cols, hidden_piece)
+    vector_grads = jnp.concatenate(
+        [vector_grads.reshape(cols, rows, -1), hidden_grads.transpose(1, 0, 2)], 2
+    )
+    vector_grads = vector_grads.reshape(cols, rows, vector_rows, GROUP).astype(low)
+    vector_grads = jnp.pad(
+        vector_grads, ((0, 0), (0, 0), (0, block_rows - vector_rows), (0, 0))
+    ).reshape(cols, rows * block_rows, GROUP)
+    mixed_total = scatter_blocks(
+        [jnp.concatenate([mixer_grad[h], vector_grads[h]], 1) for h in range(cols)]
+    )
+    mixer_total = part_order(mixed_total[:, :mixer_width])
+    vector_total = mixed_total[:vector_rows, mixer_width:].reshape(-1)
+    small = vector_total[: 8 * piece].reshape(8, piece)
+    return (
+        layer_output,
+        tokens_gradient,
+        small[0],
+        small[1],
+        mixer_total,
+        small[2:4],
+        merge_total.T,
+        small[4],
+        small[5],
+        small[6],
+        expand_total,
+        vector_total[8 * piece :],
+        reduce_total.T,
+        small[7],
+    )
+
+
 def solution(mesh):
+    def body(*arguments):
+        images = arguments[0].shape[0] // SEQ
+        whole = images == 2 and lax.axis_size("col") == 2
+        return (image_shards if whole else split_shards)(*arguments)
+
     return jax.shard_map(
-        shards,
+        body,
         mesh=mesh,
         in_specs=(
             P("row", "col"),

time: 1170 us -> 974 us (0.83)
  blocking collectives: 180 us -> 0 us
  local copies, waits for them, and re-layouts: 78.5 us -> 15 us
  Pallas kernels: 0 us -> 44.5 us
  waiting for transfers between devices: 672 us -> 700 us
  matrix products: 138 us -> 119 us
    reduce_scatter x8 -> x4, waiting for transfers between devices: 308 us -> 441 us  [scatter_blocks(): lax.psum_scatter(flat, BOTH, scatter_dimension=0, tiled=True)]
    unnamed x22 -> x8, waiting for transfers between devices: 130 us -> 0.16 us
    all_gather x2 -> x0, blocking collectives: 116 us -> none  [the longest x1 59.2 us: shards(): lax.all_gather(vector_pieces, ('row', 'col'), axis=1, tiled=True)]
    ppermute x0 -> x4, waiting for transfers between devices: none -> 53.1 us  [the longest x2 29.9 us: to_image(): other = lax.ppermute(sent, 'col', [(0, 1), (1, 0)])]
    pallas_call x0 -> x2, Pallas kernels: none -> 44.5 us  [the longest x1 28.2 us: attention_back(): pl.pallas_call(attention_back_kernel, grid=(halves, groups), in_specs=[pl...]
    unnamed x1 -> x0, blocking collectives: 42 us -> none
    concatenate x0 -> x6, other arithmetic: none -> 33.4 us  [the longest x4 32.7 us: scatter_blocks(): flat = jnp.concatenate(halves, 0)]
    another operation x14, local copies, waits for them, and re-layouts: 30.8 us -> 0.95 us  [the longest x9 0.65 us: image_shards(): jnp.stack([jnp.sum(first_grad * first_scaled, 0), jnp.sum(first_grad, 0),...]
  transfers between devices with their start and end apart: 21 -> 12, of which waited for: 17 -> 12; matrix products, arithmetic and copies ran while one was open for 21% -> 15% of each run, Pallas kernels for 0% -> 2%
where the time goes in v1:
time: 974 us; the launch traced here: 960 us
  waiting for transfers between devices  700 us (72%)
  matrix products  119 us (12%)
  other arithmetic  61.9 us (6%)
  Pallas kernels  44.5 us (5%)
  between operations  15.3 us (2%)
  local copies, waits for them, and re-layouts  15 us (2%)
    reduce_scatter x4, waiting for transfers between devices, scatter_blocks(): lax.psum_scatter(flat, BOTH, scatter_dimension=0, tiled=True)  441 us
    all_gather x4, waiting for transfers between devices, gather_blocks(): whole = lax.all_gather(block, BOTH, axis=0, tiled=True)  206 us
    dot_general x24, matrix products, product(): lax.dot_general(left, right, (((left_at,), (right_at,)), ((), ())), prefe...  119 us
    concatenate x4, other arithmetic, scatter_blocks(): flat = jnp.concatenate(halves, 0)  32.7 us
    ppermute x2, waiting for transfers between devices, to_image(): other = lax.ppermute(sent, 'col', [(0, 1), (1, 0)])  29.9 us
    pallas_call x1, Pallas kernels, attention_back(): pl.pallas_call(attention_back_kernel, grid=(halves, groups), in_specs=[pl...  28.2 us
    ppermute x2, waiting for transfers between devices, from_image(): other = lax.ppermute(sent, 'col', [(0, 1), (1, 0)])  23.3 us
  transfers between devices with their start and end apart: 12, of which 12 were waited for; matrix products, arithmetic and copies ran while one was open for 15% of the time, Pallas kernels for 2%

profile of v1, /device:TPU:28, one launch (start us, length us, event | category | flops | bytes accessed | tf_op | source)
XLA Modules:
  0.0 960.1 jit_solution(12584042551632144772)
XLA Ops:
  10.8 1.1 convert_element_type.128
  15.6 1.1 constant_dynamic-slice_fusion.3
  16.7 1.5 collective-permute-start.2
  18.2 1.5 constant_dynamic-slice_fusion.6
  20.4 14.4 %collective-permute-done.2 = bf16[577,512]{1,0:T(8,128)(2,1)S(1)} collective-permute-done((bf16[577,512]{1,0:T(8,128)(2,1)}, bf16[577,512]{1,0:T(8,128)(2,1)S(1)}, u32[]{:S(2)}, u32[]{:S(2)}) %collective-permute-start.2) | collective-permute-done | bytes 590880 | tf_op jit(solution)/shard_map/ppermute | solution.py:403
  35.2 15.4 %collective-permute-done = bf16[577,512]{1,0:T(8,128)(2,1)S(1)} collective-permute-done((bf16[577,512]{1,0:T(8,128)(2,1)S(1)}, bf16[577,512]{1,0:T(8,128)(2,1)S(1)}, u32[]{:S(2)}, u32[]{:S(2)}) %collective-permute-start) | collective-permute-done | bytes 590880 | tf_op jit(solution)/shard_map/ppermute | solution.py:403
  51.2 37.4 %all-gather.5.cloned.1.call-done = bf16[2048,1664]{1,0:T(8,128)(2,1)} async-done(((bf16[64,1664]{1,0:T(8,128)(2,1)}), bf16[2048,1664]{1,0:T(8,128)(2,1)}) %all-gather.5.cloned.1.call-update) | async-done | bytes 6815760 | tf_op jit(solution)/shard_map/all_gather | solution.py:421
  88.6 1.1 slice.217
  91.1 4.3 fusion.17
  95.4 4.3 fusion.16
  99.7 2.2 pad_maximum_fusion.2.projected_ref
  101.8 16.3 %attention_forward.1 = bf16[2,577,512]{2,1,0:T(8,128)(2,1)} custom-call(bf16[2,577,1536]{2,1,0:T(8,128)(2,1)} %pad_maximum_fusion.2.projected_ref), custom_call_target="tpu_custom_call" | custom-call | tf_op jit(solution)/shard_map/attention_forward/pallas_call | solution.py:372
  118.4 28.8 %all-gather.7.cloned.1.call-done = bf16[2048,512]{1,0:T(8,128)(2,1)} async-done(((bf16[64,512]{1,0:T(8,128)(2,1)}), bf16[2048,512]{1,0:T(8,128)(2,1)}) %all-gather.7.cloned.1.call-update) | async-done | bytes 2097168 | tf_op jit(solution)/shard_map/all_gather | solution.py:421
  147.2 2.4 fusion.51
  149.6 2.5 fusion.60
  152.2 1.7 add_convert_fusion.3
  153.9 72.4 %all-gather.9.cloned.1.call-done = bf16[2048,2048]{1,0:T(8,128)(2,1)} async-done(((bf16[64,2048]{1,0:T(8,128)(2,1)}), bf16[2048,2048]{1,0:T(8,128)(2,1)}) %all-gather.9.cloned.1.call-update) | async-done | bytes 8388624 | tf_op jit(solution)/shard_map/all_gather | solution.py:421
  226.3 7.5 fusion.6
  233.8 4.6 fusion.14
  238.4 67.0 %all-gather.11.cloned.1.call-done = bf16[2048,2048]{1,0:T(8,128)(2,1)} async-done(((bf16[64,2048]{1,0:T(8,128)(2,1)}), bf16[2048,2048]{1,0:T(8,128)(2,1)}) %all-gather.11.cloned.1.call-update) | async-done | bytes 8388624 | tf_op jit(solution)/shard_map/all_gather | solution.py:421
  305.4 8.2 fusion.65
  313.7 7.2 fusion.4
  320.9 0.8 copy-done.29
  321.7 4.0 fusion.66
  325.7 5.9 multiply_reduce_fusion
  331.6 3.2 fusion.61
  335.0 1.1 copy-done.8
  336.1 2.0 convolution_convert_fusion.6
  338.1 2.0 convolution_convert_fusion.7
  340.1 0.8 fusion.42
  340.9 0.8 fusion.41
  341.7 1.1 pad_maximum_fusion.4.upstream_ref
  342.8 28.2 %attention_back.1 = bf16[2,577,1536]{2,1,0:T(8,128)(2,1)} custom-call(bf16[2,577,1536]{2,1,0:T(8,128)(2,1)} %pad_maximum_fusion.2.projected_ref, bf16[2,577,512]{2,1,0:T(8,128)(2,1)} %pad_maximum_fusion.4.upstream_ref), custom_call_target="tpu_custom_call" | custom-call | tf_op jit(solution)/shard_map/attention_back/pallas_call | solution.py:385
  371.0 3.0 pad_maximum_fusion.3
  374.2 4.6 fusion.18
  378.9 6.0 fusion.32
  385.1 2.6 reduce.3
  388.6 5.0 convolution_convert_fusion
  393.6 3.0 convolution_convert_fusion.1
  396.6 12.9 %maximum_maximum_fusion = bf16[2048,1664]{1,0:T(8,128)(2,1)} fusion(bf16[1024,128]{1,0:T(8,128)(2,1)S(1)} %bitcast.122, bf16[1024,1536]{1,0:T(8,128)(2,1)S(1)} %convolution_convert_fusion, bf16[1024,128]{1,0:T(8,128)(2,1)S(1)} %bitcast.121, bf16[1024,1536]{1,0:T(8,128)(2,1)S(1)} %convolution_convert_fusion.1), kind=kLoop, calls=%fused_computation.2 | loop fusion | flops 27262976 | bytes 13631488 | tf_op jit(solution)/shard_map/concatenate | solution.py:426
  409.7 7.6 convolution_convert_fusion.4
  417.3 5.1 convolution_convert_fusion.5
  422.4 8.4 pad_maximum_fusion
  430.9 8.8 convolution_convert_fusion.2
  439.7 9.0 convolution_convert_fusion.3
  448.8 8.4 pad_maximum_fusion.1
  458.0 6.6 fusion.2
  464.6 6.6 add_convert_fusion.2
  472.2 1.4 fusion.31
  473.8 1.3 collective-permute-start.3
  475.0 12.7 %collective-permute-done.1 = bf16[577,512]{1,0:T(8,128)(2,1)S(1)} collective-permute-done((bf16[577,512]{1,0:T(8,128)(2,1)S(1)}, bf16[577,512]{1,0:T(8,128)(2,1)S(1)}, u32[]{:S(2)}, u32[]{:S(2)}) %collective-permute-start.1) | collective-permute-done | bytes 590880 | tf_op jit(solution)/shard_map/ppermute | solution.py:414
  487.8 1.5 maximum_select_fusion.2
  489.2 10.6 %collective-permute-done.3 = bf16[577,512]{1,0:T(8,128)(2,1)S(1)} collective-permute-done((bf16[577,512]{1,0:T(8,128)(2,1)S(1)}, bf16[577,512]{1,0:T(8,128)(2,1)S(1)}, u32[]{:S(2)}, u32[]{:S(2)}) %collective-permute-start.3) | collective-permute-done | bytes 590880 | tf_op jit(solution)/shard_map/ppermute | solution.py:414
  499.8 1.8 fusion.47
  501.6 5.9 reduce-scatter.7.cloned.1.call-done
  507.5 1.5 convert_bitcast_fusion.2
  509.0 143.6 %reduce-scatter.5.cloned.1.call-done = bf16[64,1664]{1,0:T(8,128)(2,1)} async-done(((bf16[2048,1664]{1,0:T(8,128)(2,1)}), bf16[64,1664]{1,0:T(8,128)(2,1)}) %reduce-scatter.5.cloned.1.call-update) | async-done | bytes 213008 | tf_op jit(solution)/shard_map/reduce_scatter | solution.py:427
  652.6 0.7 slice.246
  653.4 1.0 slice.247
  654.8 0.9 reshape.213
  657.3 144.8 %reduce-scatter.9.cloned.1.call-done = bf16[64,2048]{1,0:T(8,128)(2,1)} async-done(((bf16[2048,2048]{1,0:T(8,128)(2,1)}), bf16[64,2048]{1,0:T(8,128)(2,1)}) %reduce-scatter.9.cloned.1.call-update) | async-done | bytes 262160 | tf_op jit(solution)/shard_map/reduce_scatter | solution.py:427
  802.1 1.8 convert_element_type.163
  803.9 147.2 %reduce-scatter.11.cloned.1.call-done = bf16[64,2048]{1,0:T(8,128)(2,1)} async-done(((bf16[2048,2048]{1,0:T(8,128)(2,1)}), bf16[64,2048]{1,0:T(8,128)(2,1)}) %reduce-scatter.11.cloned.1.call-update) | async-done | bytes 262160 | tf_op jit(solution)/shard_map/reduce_scatter | solution.py:427
  951.1 1.8 convert_bitcast_fusion
  (170 shorter events, 16.1 us)
Async XLA Ops:
  7.2 6.0 copy-start.25
  7.2 6.7 copy-start.21
  7.2 7.5 copy-start.22
  7.2 81.3 %all-gather.5.cloned.1.call-start = ((), (), s32[]{:S(2)}) async-start(), calls=%async_computation.4 | async-start | bytes 7028736 | tf_op jit(solution)/shard_map/all_gather | solution.py:421
  10.8 4.7 copy-start.18
  13.1 134.1 %all-gather.7.cloned.1.call-start = ((), (), s32[]{:S(2)}) async-start(), calls=%async_computation.5 | async-start | bytes 2162688 | tf_op jit(solution)/shard_map/all_gather | solution.py:421
  13.9 212.5 %all-gather.9.cloned.1.call-start = ((), (), s32[]{:S(2)}) async-start(), calls=%async_computation.6 | async-start | bytes 8650752 | tf_op jit(solution)/shard_map/all_gather | solution.py:421
  14.7 290.7 %all-gather.11.cloned.1.call-start = ((), (), s32[]{:S(2)}) async-start(), calls=%async_computation.7 | async-start | bytes 8650752 | tf_op jit(solution)/shard_map/all_gather | solution.py:421
  15.5 492.0 %reduce-scatter.7.cloned.1.call-start = ((), (), s32[]{:S(2)}) async-start(), calls=%async_computation.9 | async-start | bytes 2162688 | tf_op jit(solution)/shard_map/reduce_scatter | solution.py:427
  16.7 34.5 %copy-start.4 = (bf16[577,512]{1,0:T(8,128)(2,1)}, bf16[577,512]{1,0:T(8,128)(2,1)S(1)}, u32[]{:S(2)}) copy-start(bf16[577,512]{1,0:T(8,128)(2,1)S(1)} %get-tuple-element.34) | copy-start | bytes 1772548
  16.7 18.1 %collective-permute-start.2 = (bf16[577,512]{1,0:T(8,128)(2,1)}, bf16[577,512]{1,0:T(8,128)(2,1)S(1)}, u32[]{:S(2)}, u32[]{:S(2)}) collective-permute-start(bf16[577,512]{1,0:T(8,128)(2,1)} %get-tuple-element.35), channel_id=1, source_target_pairs={{0,1},{1,0},{2,3},{3,2},{4,5},{5,4},{6,7},{7,6},{8,9},{9,8},{10,11... | collective-permute-start | bytes 1772552 | tf_op jit(solution)/shard_map/ppermute | solution.py:403
  19.7 31.0 %collective-permute-start = (bf16[577,512]{1,0:T(8,128)(2,1)S(1)}, bf16[577,512]{1,0:T(8,128)(2,1)S(1)}, u32[]{:S(2)}, u32[]{:S(2)}) collective-permute-start(bf16[577,512]{1,0:T(8,128)(2,1)S(1)} %get-tuple-element.36), channel_id=1, source_target_pairs={{0,1},{1,0},{2,3},{3,2},{4,5},{5,4},{6,7},{7,6},{8,9},{9,8},{10,11... | collective-permute-start | bytes 1772552 | tf_op jit(solution)/shard_map/ppermute | solution.py:403
  34.8 60.6 %copy-start.14 = (bf16[577,512]{1,0:T(8,128)(2,1)}, bf16[577,512]{1,0:T(8,128)(2,1)S(1)}, u32[]{:S(2)}) copy-start(bf16[577,512]{1,0:T(8,128)(2,1)S(1)} %collective-permute-done.2) | copy-start | bytes 1772548
  50.7 44.7 %copy-start.9 = (bf16[577,512]{1,0:T(8,128)(2,1)}, bf16[577,512]{1,0:T(8,128)(2,1)S(1)}, u32[]{:S(2)}) copy-start(bf16[577,512]{1,0:T(8,128)(2,1)S(1)} %collective-permute-done) | copy-start | bytes 1772548
  147.2 2.4 copy-start.7
  147.2 2.5 copy-start.23
  152.1 173.5 %copy-start.2 = (f32[577,1024]{1,0:T(8,128)}, f32[577,1024]{1,0:T(8,128)S(1)}, u32[]{:S(2)}) copy-start(f32[577,1024]{1,0:T(8,128)S(1)} %get-tuple-element.62) | copy-start | bytes 7090180
  226.3 7.5 copy-start.19
  226.3 7.5 copy-start.28
  313.6 7.3 copy-start.30
  313.6 7.3 copy-start.5
  313.6 7.3 copy-start.15
  313.6 7.3 copy-start.27
  313.7 8.1 copy-start.29
  313.7 12.0 %slice-start = ((s8[8388608]{0:T(1024)(128)(4,1)}), s8[4194304]{0:T(1024)(128)(4,1)S(1)}, s32[]{:S(2)}) async-start(s8[8388608]{0:T(1024)(128)(4,1)} %bitcast.142), calls=%async_computation.12 | async-start | bytes 8388608
  321.7 4.0 slice-start.1
  325.7 5.9 copy-start.31
  334.8 1.3 copy-start.8
  338.1 2.0 copy-start.24
  374.0 278.6 %reduce-scatter.5.cloned.1.call-start = ((), (), s32[]{:S(2)}) async-start(), calls=%async_computation.8 | async-start | bytes 7028736 | tf_op jit(solution)/shard_map/reduce_scatter | solution.py:427
  374.2 4.7 copy-start
  374.2 4.7 copy-start.10
  388.6 5.0 copy-start.1
  388.6 5.0 copy-start.11
  409.6 392.5 %reduce-scatter.9.cloned.1.call-start = ((), (), s32[]{:S(2)}) async-start(), calls=%async_computation.10 | async-start | bytes 8650752 | tf_op jit(solution)/shard_map/reduce_scatter | solution.py:427
  409.7 7.7 copy-start.20
  409.7 7.6 copy-start.32
  430.9 520.2 %reduce-scatter.11.cloned.1.call-start = ((), (), s32[]{:S(2)}) async-start(), calls=%async_computation.11 | async-start | bytes 8650752 | tf_op jit(solution)/shard_map/reduce_scatter | solution.py:427
  430.9 8.8 copy-start.6
  430.9 8.8 copy-start.16
  457.2 0.7 copy-start.26
  458.0 6.6 copy-start.3
  464.5 7.4 copy-start.13
  471.2 1.1 copy-start.12
  471.3 16.4 %collective-permute-start.1 = (bf16[577,512]{1,0:T(8,128)(2,1)S(1)}, bf16[577,512]{1,0:T(8,128)(2,1)S(1)}, u32[]{:S(2)}, u32[]{:S(2)}) collective-permute-start(bf16[577,512]{1,0:T(8,128)(2,1)S(1)} %get-tuple-element.33), channel_id=1, source_target_pairs={{0,1},{1,0},{2,3},{3,2},{4,5},{5,4},{6,7},{7,6},{8,9},{9,8},{10,11... | collective-permute-start | bytes 1772552 | tf_op jit(solution)/shard_map/ppermute | solution.py:414
  473.8 26.0 %collective-permute-start.3 = (bf16[577,512]{1,0:T(8,128)(2,1)S(1)}, bf16[577,512]{1,0:T(8,128)(2,1)S(1)}, u32[]{:S(2)}, u32[]{:S(2)}) collective-permute-start(bf16[577,512]{1,0:T(8,128)(2,1)S(1)} %get-tuple-element.31), channel_id=1, source_target_pairs={{0,1},{1,0},{2,3},{3,2},{4,5},{5,4},{6,7},{7,6},{8,9},{9,8},{10,11... | collective-permute-start | bytes 1772552 | tf_op jit(solution)/shard_map/ppermute | solution.py:414
  652.6 3.7 copy-start.17
Sparse Core Ops, SparseCore 0:
  13.2 75.2 all-gather.4
  92.0 55.1 all-gather.6
  150.6 75.6 all-gather.8
  229.6 75.6 all-gather.10
  374.1 133.3 reduce-scatter.6
  509.7 142.8 reduce-scatter.4
  654.9 147.1 reduce-scatter.8
  804.4 146.6 reduce-scatter.10

commit v2 on v1

--- a/solution.py
+++ b/solution.py
@@ -1,3 +1,5 @@
+import functools
+
 import jax
 import jax.numpy as jnp
 from jax import lax
@@ -311,7 +313,6 @@
 
 
 GROUP = 128
-BOTH = ("col", "row")
 
 
 def attention_forward_kernel(projected_ref, attended_ref):
@@ -395,36 +396,389 @@
     )(projected, upstream)
 
 
-def to_image(piece):
+MESH = pl.DeviceIdType.MESH
+ANY = pl.BlockSpec(memory_space=pl.ANY)
+IN_VMEM = pl.BlockSpec(memory_space=pltpu.VMEM)
+SIDES = 2
+
+
+def place():
     col = lax.axis_index("col")
-    rows = piece.shape[0] // 2
-    kept = lax.dynamic_slice_in_dim(piece, col * rows, rows, 0)
-    sent = lax.dynamic_slice_in_dim(piece, (1 - col) * rows, rows, 0)
-    other = lax.ppermute(sent, "col", [(0, 1), (1, 0)])
-    return jnp.where(
-        col == 0, jnp.concatenate([kept, other], 1), jnp.concatenate([other, kept], 1)
-    )
-
-
-def from_image(whole):
-    col = lax.axis_index("col")
-    width = whole.shape[1] // 2
-    kept = lax.dynamic_slice_in_dim(whole, col * width, width, 1)
-    sent = lax.dynamic_slice_in_dim(whole, (1 - col) * width, width, 1)
-    other = lax.ppermute(sent, "col", [(0, 1), (1, 0)])
-    return jnp.where(
-        col == 0, jnp.concatenate([kept, other], 0), jnp.concatenate([other, kept], 0)
-    )
-
-
-def gather_blocks(block):
-    whole = lax.all_gather(block, BOTH, axis=0, tiled=True)
-    return whole.reshape(2, whole.shape[0] // 2, block.shape[1])
-
-
-def scatter_blocks(halves):
-    flat = jnp.concatenate(halves, 0)
-    return lax.psum_scatter(flat, BOTH, scatter_dimension=0, tiled=True).astype(jnp.float32)
+    row = lax.axis_index("row")
+    return col, lax.div(row, 4), lax.rem(lax.div(row, 2), 2), lax.rem(row, 2)
+
+
+def device_of(x, z, y, core):
+    return (z * 4 + y * 2 + core, x)
+
+
+def greet(x, z, y, core, depth):
+    barrier = pltpu.get_barrier_semaphore()
+    others = [device_of(x, lax.rem(z + k, depth), y, core) for k in range(1, depth)]
+    others += [
+        device_of(x, z, 1 - y, core),
+        device_of(1 - x, z, y, core),
+        device_of(x, z, y, 1 - core),
+    ]
+    for other in others:
+        pl.semaphore_signal(barrier, inc=1, device_id=other, device_id_type=MESH)
+    pl.semaphore_wait(barrier, len(others))
+
+
+def split_width(width):
+    tiles = width // GROUP
+    first = -(-tiles * 5 // 8)
+    return first * GROUP
+
+
+class Copies:
+    def __init__(self, send_sems, recv_sems):
+        self.send_sems, self.recv_sems, self.count, self.sent = send_sems, recv_sems, 0, []
+
+    def slot(self):
+        self.count += 1
+        return self.count - 1
+
+    def send(self, slot, source, target, device):
+        copy = pltpu.make_async_remote_copy(
+            src_ref=source,
+            dst_ref=target,
+            send_sem=self.send_sems.at[slot],
+            recv_sem=self.recv_sems.at[slot],
+            device_id=device,
+            device_id_type=MESH,
+        )
+        copy.start()
+        self.sent.append(copy)
+
+    def arrived(self, slot, target, device):
+        pltpu.make_async_remote_copy(
+            src_ref=target,
+            dst_ref=target,
+            send_sem=self.send_sems.at[slot],
+            recv_sem=self.recv_sems.at[slot],
+            device_id=device,
+            device_id_type=MESH,
+        ).wait_recv()
+
+    def finish(self):
+        for copy in self.sent:
+            copy.wait_send()
+
+
+def run_waves(chains):
+    stages = max(len(chain) for chain in chains)
+    for wave in range(len(chains) + stages - 1):
+        for stage in range(stages - 1, -1, -1):
+            at = wave - stage
+            if 0 <= at < len(chains) and stage < len(chains[at]):
+                chains[at][stage]()
+
+
+def gather_chain(copies, where, depth, block, whole, local):
+    x, z, y, core = where
+    width = block.shape[1]
+    first = split_width(width)
+    parts = (pl.ds(0, first), pl.ds(first, width - first))
+    x_peer = device_of(1 - x, z, y, core)
+    y_peer = device_of(x, z, 1 - y, core)
+    partner = device_of(x, z, y, 1 - core)
+    steps = range(1, depth)
+    z_peers = [device_of(x, lax.rem(z + k, depth), y, core) for k in steps]
+    z_from = [lax.rem(z + depth - k, depth) for k in steps]
+    a, c = parts
+    az, cz = [copies.slot() for _ in steps], [copies.slot() for _ in steps]
+    ay, ax, cx, cy = [copies.slot() for _ in range(4)]
+    shared = [copies.slot() for _ in range(5)]
+
+    def share(slot, target):
+        copies.send(slot, target, target, partner)
+
+    def begin():
+        mine = whole.at[x, z, y, core]
+        for k in range(depth - 1):
+            copies.send(az[k], block.at[:, a], mine.at[:, a], z_peers[k])
+        copies.send(cx, block.at[:, c], mine.at[:, c], x_peer)
+
+    def second():
+        local.wait()
+        for k in range(depth - 1):
+            copies.arrived(az[k], whole.at[x, z_from[k], y, core, :, a], z_peers[k])
+        column = whole.at[x, :, y, core, :, a]
+        copies.send(ay, column, column, y_peer)
+        copies.arrived(cx, whole.at[1 - x, z, y, core, :, c], x_peer)
+        pair = whole.at[:, z, y, core, :, c]
+        for k in range(depth - 1):
+            copies.send(cz[k], pair, pair, z_peers[k])
+        share(shared[0], column)
+
+    def third():
+        copies.arrived(ay, whole.at[x, :, 1 - y, core, :, a], y_peer)
+        plane = whole.at[x, :, :, core, :, a]
+        copies.send(ax, plane, plane, x_peer)
+        for k in range(depth - 1):
+            copies.arrived(cz[k], whole.at[:, z_from[k], y, core, :, c], z_peers[k])
+        sheet = whole.at[:, :, y, core, :, c]
+        copies.send(cy, sheet, sheet, y_peer)
+        share(shared[1], whole.at[x, :, 1 - y, core, :, a])
+        share(shared[2], sheet)
+
+    def fourth():
+        copies.arrived(ax, whole.at[1 - x, :, :, core, :, a], x_peer)
+        share(shared[3], whole.at[1 - x, :, :, core, :, a])
+        copies.arrived(cy, whole.at[:, :, 1 - y, core, :, c], y_peer)
+        share(shared[4], whole.at[:, :, 1 - y, core, :, c])
+
+    def last():
+        other = 1 - core
+        copies.arrived(shared[0], whole.at[x, :, y, other, :, a], partner)
+        copies.arrived(shared[1], whole.at[x, :, 1 - y, other, :, a], partner)
+        copies.arrived(shared[2], whole.at[:, :, y, other, :, c], partner)
+        copies.arrived(shared[3], whole.at[1 - x, :, :, other, :, a], partner)
+        copies.arrived(shared[4], whole.at[:, :, 1 - y, other, :, c], partner)
+
+    return begin, (second, third, fourth, last)
+
+
+def gather_kernel(depth, pieces_count, *refs):
+    count = (len(refs) - 3 - 2 * pieces_count) // 2
+    pieces, blocks = refs[:pieces_count], refs[pieces_count : pieces_count + count]
+    outs = refs[pieces_count + count : -3]
+    images, wholes = outs[:pieces_count], outs[pieces_count:]
+    send_sems, recv_sems, own_sems = refs[-3:]
+    where = place()
+    x, z, y, core = where
+    copies = Copies(send_sems, recv_sems)
+    local = [
+        pltpu.make_async_copy(block, whole.at[x, z, y, core], own_sems.at[at])
+        for at, (block, whole) in enumerate(zip(blocks, wholes))
+    ]
+    kept = [
+        pltpu.make_async_copy(piece.at[x], image.at[x], own_sems.at[count + at])
+        for at, (piece, image) in enumerate(zip(pieces, images))
+    ]
+    for copy in local + kept:
+        copy.start()
+    greet(*where, depth)
+    chains = [
+        gather_chain(copies, where, depth, *item) for item in zip(blocks, wholes, local)
+    ]
+    x_peer = device_of(1 - x, z, y, core)
+    slots = [copies.slot() for _ in pieces]
+    for at in range(pieces_count):
+        if at == 0:
+            copies.send(slots[at], pieces[at].at[1 - x], images[at].at[x], x_peer)
+    for begin, _ in chains:
+        begin()
+    for at in range(1, pieces_count):
+        copies.send(slots[at], pieces[at].at[1 - x], images[at].at[x], x_peer)
+    run_waves([rest for _, rest in chains])
+    for at in range(pieces_count):
+        copies.arrived(slots[at], images[at].at[1 - x], x_peer)
+        kept[at].wait()
+    copies.finish()
+
+
+def gather_weights(pieces, blocks, depth):
+    copies = (2 * (depth - 1) + 9) * len(blocks) + len(pieces)
+    return pl.pallas_call(
+        functools.partial(gather_kernel, depth, len(pieces)),
+        in_specs=[IN_VMEM] * (len(pieces) + len(blocks)),
+        out_specs=[ANY] * (len(pieces) + len(blocks)),
+        out_shape=[jax.ShapeDtypeStruct(piece.shape, piece.dtype) for piece in pieces]
+        + [
+            jax.ShapeDtypeStruct((SIDES, depth, 2, 2) + block.shape, block.dtype)
+            for block in blocks
+        ],
+        scratch_shapes=[
+            pltpu.SemaphoreType.DMA((copies,)),
+            pltpu.SemaphoreType.DMA((copies,)),
+            pltpu.SemaphoreType.DMA((len(pieces) + len(blocks),)),
+        ],
+        compiler_params=pltpu.CompilerParams(collective_id=1, has_side_effects=True),
+        name="gather_weights",
+    )(*pieces, *blocks)
+
+
+def add_blocks(count, target, term):
+    @pl.loop(0, count)
+    def _(at):
+        total = target(at)[...].astype(jnp.float32) + term(at)[...].astype(jnp.float32)
+        target(at)[...] = total.astype(jnp.bfloat16)
+
+
+def scatter_chain(copies, where, depth, grad, total, buffers, load):
+    x, z, y, core = where
+    own, halves, ax_in, ay_in, az_in, cy_in, cz_in, c_sum, cx_in = buffers
+    width = total.shape[1]
+    first = split_width(width)
+    a, c = pl.ds(0, first), pl.ds(first, width - first)
+    x_peer = device_of(1 - x, z, y, core)
+    y_peer = device_of(x, z, 1 - y, core)
+    partner = device_of(x, z, y, 1 - core)
+    steps = range(1, depth)
+    z_to = [lax.rem(z + k, depth) for k in steps]
+    z_peers = [device_of(x, at, y, core) for at in z_to]
+    az, cz = [copies.slot() for _ in steps], [copies.slot() for _ in steps]
+    pair = [copies.slot() for _ in range(SIDES)]
+    ax, ay, cy, cx = [copies.slot() for _ in range(4)]
+
+    def begin():
+        for copy in load:
+            copy.start()
+        for side in range(SIDES):
+            copies.send(
+                pair[side], grad[side].at[:, :, 1 - core], halves.at[side], partner
+            )
+
+    def second():
+        for side in range(SIDES):
+            load[side].wait()
+            copies.arrived(pair[side], halves.at[side], partner)
+
+        def at_block(ref, at):
+            return ref.at[lax.div(at, depth * 2), lax.rem(lax.div(at, 2), depth), lax.rem(at, 2)]
+
+        add_blocks(
+            SIDES * depth * 2, lambda at: at_block(halves, at), lambda at: at_block(own, at)
+        )
+        copies.send(ax, halves.at[1 - x, :, :, :, a], ax_in, x_peer)
+        copies.send(cy, halves.at[:, :, 1 - y, :, c], cy_in, y_peer)
+
+    def third():
+        copies.arrived(ax, ax_in, x_peer)
+        add_blocks(
+            depth * 2,
+            lambda at: ax_in.at[lax.div(at, 2), lax.rem(at, 2)],
+            lambda at: halves.at[x, lax.div(at, 2), lax.rem(at, 2), :, a],
+        )
+        copies.send(ay, ax_in.at[:, 1 - y], ay_in, y_peer)
+        copies.arrived(cy, cy_in, y_peer)
+        add_blocks(
+            SIDES * depth,
+            lambda at: cy_in.at[lax.div(at, depth), lax.rem(at, depth)],
+            lambda at: halves.at[lax.div(at, depth), lax.rem(at, depth), y, :, c],
+        )
+        for k in range(depth - 1):
+            copies.send(cz[k], cy_in.at[:, z_to[k]], cz_in.at[k], z_peers[k])
+
+    def fourth():
+        copies.arrived(ay, ay_in, y_peer)
+        add_blocks(depth, lambda at: ay_in.at[at], lambda at: ax_in.at[at, y])
+        for k in range(depth - 1):
+            copies.send(az[k], ay_in.at[z_to[k]], az_in.at[k], z_peers[k])
+        for k in range(depth - 1):
+            copies.arrived(cz[k], cz_in.at[k], z_peers[k])
+
+        @pl.loop(0, SIDES)
+        def _(at):
+            sums = cy_in[at, z].astype(jnp.float32)
+            for k in range(depth - 1):
+                sums += cz_in[k, at].astype(jnp.float32)
+            c_sum[at] = sums.astype(jnp.bfloat16)
+
+        copies.send(cx, c_sum.at[1 - x], cx_in, x_peer)
+
+    def last():
+        for k in range(depth - 1):
+            copies.arrived(az[k], az_in.at[k], z_peers[k])
+        sums = ay_in[z].astype(jnp.float32)
+        for k in range(depth - 1):
+            sums += az_in[k].astype(jnp.float32)
+        total[:, :first] = sums
+        copies.arrived(cx, cx_in, x_peer)
+        total[:, first:] = c_sum[x].astype(jnp.float32) + cx_in[...].astype(jnp.float32)
+
+    return begin, (second, third, fourth, last)
+
+
+def scatter_kernel(depth, count, wholes_count, *refs):
+    grads = [refs[SIDES * at : SIDES * at + SIDES] for at in range(count)]
+    refs = refs[SIDES * count :]
+    wholes, refs = refs[:wholes_count], refs[wholes_count:]
+    totals, pieces = refs[:count], refs[count : count + wholes_count]
+    refs = refs[count + wholes_count :]
+    send_sems, recv_sems, own_sems = refs[-3:]
+    where = place()
+    x, z, y, core = where
+    copies = Copies(send_sems, recv_sems)
+    greet(*where, depth)
+    x_peer = device_of(1 - x, z, y, core)
+    kept = []
+    slots = [copies.slot() for _ in wholes]
+    for at in range(wholes_count):
+        width = pieces[at].shape[2]
+        mine = pl.ds(pl.multiple_of(x * width, width), width)
+        theirs = pl.ds(pl.multiple_of((1 - x) * width, width), width)
+        copy = pltpu.make_async_copy(
+            wholes[at].at[:, mine], pieces[at].at[x], own_sems.at[SIDES * count + at]
+        )
+        copy.start()
+        kept.append(copy)
+        copies.send(slots[at], wholes[at].at[:, theirs], pieces[at].at[x], x_peer)
+    chains = []
+    for at in range(count):
+        buffers = refs[9 * at : 9 * at + 9]
+        load = [
+            pltpu.make_async_copy(
+                grads[at][side].at[:, :, core], buffers[0].at[side], own_sems.at[SIDES * at + side]
+            )
+            for side in range(SIDES)
+        ]
+        chains.append(
+            scatter_chain(copies, where, depth, grads[at], totals[at], buffers, load)
+        )
+    for begin, _ in chains:
+        begin()
+    run_waves([rest for _, rest in chains])
+    for at in range(wholes_count):
+        copies.arrived(slots[at], pieces[at].at[1 - x], x_peer)
+        kept[at].wait()
+    copies.finish()
+
+
+def scatter_buffers(depth, rows, width):
+    first = split_width(width)
+    rest = width - first
+    shapes = [
+        (SIDES, depth, 2, rows, width),
+        (SIDES, depth, 2, rows, width),
+        (depth, 2, rows, first),
+        (depth, rows, first),
+        (depth - 1, rows, first),
+        (SIDES, depth, rows, rest),
+        (depth - 1, SIDES, rows, rest),
+        (SIDES, rows, rest),
+        (rows, rest),
+    ]
+    return [pltpu.VMEM(shape, jnp.bfloat16) for shape in shapes]
+
+
+def scatter_grads(grads, wholes, depth):
+    copies = (2 * (depth - 1) + 6) * len(grads) + len(wholes)
+    scratch = []
+    for grad in grads:
+        scratch += scatter_buffers(depth, grad[0].shape[3], grad[0].shape[4])
+    return pl.pallas_call(
+        functools.partial(scatter_kernel, depth, len(grads), len(wholes)),
+        in_specs=[ANY] * SIDES * len(grads) + [IN_VMEM] * len(wholes),
+        out_specs=[IN_VMEM] * len(grads) + [ANY] * len(wholes),
+        out_shape=[jax.ShapeDtypeStruct(grad[0].shape[3:], jnp.float32) for grad in grads]
+        + [
+            jax.ShapeDtypeStruct((SIDES, whole.shape[0], whole.shape[1] // SIDES), whole.dtype)
+            for whole in wholes
+        ],
+        scratch_shapes=scratch
+        + [
+            pltpu.SemaphoreType.DMA((copies,)),
+            pltpu.SemaphoreType.DMA((copies,)),
+            pltpu.SemaphoreType.DMA((SIDES * len(grads) + len(wholes),)),
+        ],
+        compiler_params=pltpu.CompilerParams(
+            collective_id=2, has_side_effects=True, vmem_limit_bytes=60 * 2**20
+        ),
+        name="scatter_grads",
+    )(*[half for grad in grads for half in grad], *wholes)
 
 
 def product(left, right, left_at, right_at):
@@ -495,11 +849,25 @@
     )
     mixer_width = 3 * mixer_weight.shape[2]
     first_block = jnp.concatenate([group_order(mixer_weight).astype(low), vector_block], 1)
-    mixed = gather_blocks(first_block)
+    depth = rows // 4
+    sides = (cols, tokens.shape[0] // cols, tokens.shape[1])
+    image, upstream_low, mixed, merger, expander, reducer = gather_weights(
+        [tokens.reshape(sides), cotangent.reshape(sides)],
+        [
+            first_block,
+            merge_weight.astype(low).T,
+            expand_weight.astype(low),
+            reduce_weight.astype(low).T,
+        ],
+        depth,
+    )
+    image = jnp.concatenate([image[h] for h in range(cols)], 1)
+    upstream_low = jnp.concatenate([upstream_low[h] for h in range(cols)], 1)
+    mixed, merger, expander, reducer = [
+        whole.reshape(cols, rows * block_rows, whole.shape[-1])
+        for whole in (mixed, merger, expander, reducer)
+    ]
     mixer = mixed[:, :, :mixer_width]
-    merger = gather_blocks(merge_weight.astype(low).T)
-    expander = gather_blocks(expand_weight.astype(low))
-    reducer = gather_blocks(reduce_weight.astype(low).T)
     spread = mixed[:, :, mixer_width:].reshape(cols, rows, block_rows, GROUP)[:, :, :vector_rows]
     spread = spread.reshape(cols, rows, -1).astype(jnp.float32).transpose(1, 0, 2)
     rows_of = spread[:, :, : 8 * piece].reshape(rows, cols, 8, piece).transpose(2, 0, 1, 3)
@@ -517,8 +885,6 @@
         2,
     ).reshape(cols, -1)
 
-    image = to_image(tokens)
-    upstream_low = to_image(cotangent)
     inputs = image.astype(jnp.float32)
     first_scaled, first_inverse, first_normed = normalize(inputs, first_gain_row, first_shift_row)
     first_low = first_normed.astype(low)
@@ -535,17 +901,15 @@
     expanded = [product(second_low, expander[h], 1, 0) + expand_shift[h] for h in range(cols)]
     activated = [quick_gelu(part).astype(low) for part in expanded]
     reduced = sum(product(activated[h], reducer[h], 1, 1) for h in range(cols))
-    layer_output = from_image((hidden + reduced + reduce_shift).astype(low))
+    image_output = (hidden + reduced + reduce_shift).astype(low)
 
     upstream = upstream_low.astype(jnp.float32)
     reducer_grad = [product(upstream_low, activated[h], 0, 0).astype(low) for h in range(cols)]
-    reduce_total = scatter_blocks(reducer_grad)
     expanded_grad = [
         (product(upstream_low, reducer[h], 1, 0) * gelu_slope(expanded[h])).astype(low)
         for h in range(cols)
     ]
     expander_grad = [product(second_low, expanded_grad[h], 0, 0).astype(low) for h in range(cols)]
-    expand_total = scatter_blocks(expander_grad)
     expand_shift_grad = [jnp.sum(part.astype(jnp.float32), 0) for part in expanded_grad]
     second_grad = sum(product(expanded_grad[h], expander[h], 1, 1) for h in range(cols))
     hidden_grad = upstream + norm_back(
@@ -553,7 +917,6 @@
     )
     hidden_low = hidden_grad.astype(low)
     merger_grad = [product(hidden_low, attended[h], 0, 0).astype(low) for h in range(cols)]
-    merge_total = scatter_blocks(merger_grad)
     attended_grad = jnp.stack(
         [product(hidden_low, merger[h], 1, 0).astype(low) for h in range(cols)]
     )
@@ -563,7 +926,6 @@
     bias_sums = bias_sums.reshape(cols, -1, 3, GROUP).transpose(2, 0, 1, 3).reshape(3, -1)
     first_grad = sum(product(projected_grad[h], mixer[h], 1, 1) for h in range(cols))
     input_grad = hidden_grad + norm_back(first_grad, first_scaled, first_inverse, first_gain_row)
-    tokens_gradient = from_image(input_grad.astype(low)).astype(jnp.float32)
     vector_grads = jnp.stack(
         [
             jnp.sum(first_grad * first_scaled, 0),
@@ -585,9 +947,16 @@
     vector_grads = jnp.pad(
         vector_grads, ((0, 0), (0, 0), (0, block_rows - vector_rows), (0, 0))
     ).reshape(cols, rows * block_rows, GROUP)
-    mixed_total = scatter_blocks(
-        [jnp.concatenate([mixer_grad[h], vector_grads[h]], 1) for h in range(cols)]
-    )
+    mixed_grad = [jnp.concatenate([mixer_grad[h], vector_grads[h]], 1) for h in range(cols)]
+    grads = [
+        [part.reshape(depth, 2, 2, block_rows, -1) for part in halves]
+        for halves in (reducer_grad, expander_grad, merger_grad, mixed_grad)
+    ]
+    reduce_total, expand_total, merge_total, mixed_total, layer_output, tokens_gradient = (
+        scatter_grads(grads, [image_output, input_grad.astype(low)], depth)
+    )
+    layer_output = layer_output.reshape(tokens.shape)
+    tokens_gradient = tokens_gradient.reshape(tokens.shape).astype(jnp.float32)
     mixer_total = part_order(mixed_total[:, :mixer_width])
     vector_total = mixed_total[:vector_rows, mixer_width:].reshape(-1)
     small = vector_total[: 8 * piece].reshape(8, piece)

time: 974 us -> 535 us (0.55)
  waiting for transfers between devices: 700 us -> 0 us
  Pallas kernels: 44.5 us -> 376 us
  other arithmetic: 61.9 us -> 25.5 us
  matrix products: 119 us -> 96.1 us
  local copies, waits for them, and re-layouts: 15 us -> 29.1 us
  between operations: 15.3 us -> 1.86 us
    reduce_scatter x4 -> x0, waiting for transfers between devices: 441 us -> none  [scatter_blocks(): lax.psum_scatter(flat, BOTH, scatter_dimension=0, tiled=True)]
    pallas_call x0 -> x2, Pallas kernels: none -> 331 us  [the longest x1 170 us: scatter_grads(): pl.pallas_call(functools.partial(scatter_kernel, depth, len(grads), len(w...]
    all_gather x4 -> x0, waiting for transfers between devices: 206 us -> none  [gather_blocks(): whole = lax.all_gather(block, BOTH, axis=0, tiled=True)]
    ppermute x4 -> x0, waiting for transfers between devices: 53.1 us -> none  [the longest x2 29.9 us: to_image(): other = lax.ppermute(sent, 'col', [(0, 1), (1, 0)])]
    concatenate x4 -> x2, other arithmetic: 32.7 us -> 6.24 us  [image_shards(): jnp.concatenate([mixer_grad[h], vector_grads[h]], 1)]
    dot_general x24, matrix products: 119 us -> 96.1 us  [product(): lax.dot_general(left, right, (((left_at,), (right_at,)), ((), ())), prefe...]
  transfers between devices with their start and end apart: 12 -> 0, of which waited for: 12 -> 0; matrix products, arithmetic and copies ran while one was open for 15% -> 0% of each run, Pallas kernels for 2% -> 0%
where the time goes in v2:
time: 535 us; the launch traced here: 529 us
  Pallas kernels  376 us (70%)
  matrix products  96.1 us (18%)
  local copies, waits for them, and re-layouts  29.1 us (5%)
  other arithmetic  25.5 us (5%)
    pallas_call x1, Pallas kernels, scatter_grads(): pl.pallas_call(functools.partial(scatter_kernel, depth, len(grads), len(w...  170 us
    pallas_call x1, Pallas kernels, gather_weights(): pl.pallas_call(functools.partial(gather_kernel, depth, len(pieces)), in_s...  161 us
    dot_general x24, matrix products, product(): lax.dot_general(left, right, (((left_at,), (right_at,)), ((), ())), prefe...  96.1 us
    pallas_call x1, Pallas kernels, attention_back(): pl.pallas_call(attention_back_kernel, grid=(halves, groups), in_specs=[pl...  28.3 us
    pallas_call x1, Pallas kernels, attention_forward(): pl.pallas_call(attention_forward_kernel, grid=(halves, groups), in_specs=...  16.8 us

profile of v2, /device:TPU:28, one launch (start us, length us, event | category | flops | bytes accessed | tf_op | source)
XLA Modules:
  0.0 529.1 jit_solution(7116277239386017771)
XLA Ops:
  0.7 0.8 convert_bitcast_fusion.4
  1.5 0.7 convert_bitcast_fusion.6
  2.2 0.7 convert_bitcast_fusion.2
  2.8 0.7 convert.82
  3.6 0.7 convert.87
  4.3 1.0 convert_element_type.122
  5.7 0.7 fusion.24.refs_2_
  6.5 1.3 reshape.243.refs_0_
  7.7 1.3 reshape.244.refs_1_
  9.0 0.7 convert_bitcast_fusion.refs_5_
  9.7 0.7 convert_element_type.128.refs_4_
  10.4 0.6 convert_bitcast_fusion.1.refs_3_
  11.1 161.2 %gather_weights.1 = (bf16[2,577,512]{2,1,0:T(8,128)(2,1)}, bf16[2,577,512]{2,1,0:T(8,128)(2,1)}, bf16[2,4,2,2,64,1664]{5,4,3,2,1,0:T(8,128)(2,1)}, bf16[2,4,2,2,...) custom-call(bf16[2,577,512]{2,1,0:T(8,128)(2,1)} %reshape.243.refs_0_,, ...), custom_call_target="tpu_custom_call" | custom-call | tf_op jit(solution)/shard_map/gather_weights/pallas_call | solution.py:584
  172.3 1.3 slice_bitcast_fusion.19
  174.1 1.1 slice.233
  176.0 4.2 fusion
  180.3 4.2 fusion.1
  184.5 2.1 pad_maximum_fusion.projected_ref
  186.7 16.8 %attention_forward.1 = bf16[2,577,512]{2,1,0:T(8,128)(2,1)} custom-call(bf16[2,577,1536]{2,1,0:T(8,128)(2,1)} %pad_maximum_fusion.projected_ref), custom_call_target="tpu_custom_call" | custom-call | tf_op jit(solution)/shard_map/attention_forward/pallas_call | solution.py:373
  203.4 1.2 fusion.34
  204.6 1.0 copy-done.16
  205.6 2.3 fusion.22
  207.9 3.4 fusion.30
  212.0 4.4 fusion.33
  216.4 5.4 %multiply_convert_fusion.3 = (bf16[577,2048]{1,0:T(8,128)(2,1)}, f32[577,2048]{1,0:T(8,128)}) fusion(f32[2048]{0:T(1024)S(1)} %bitcast.195, bf16[577,1024]{1,0:T(8,128)(2,1)S(1)} %add_convert_fusion.3, bf16[1024,2048]{1,0:T(8,128)(2,1)S(1)} %bitcast.163), kind=kOutput, calls=%fused_computation.4 | convolution fusion | flops 2428385280 | bytes 12474368 | tf_op jit(solution)/shard_map/dot_general | solution.py:785
  221.9 0.9 slice-done.1
  222.7 0.6 fusion.32
  223.4 7.7 %fusion.39 = (bf16[2048]{0:T(1024)(128)(2,1)S(1)}, bf16[577,2048]{1,0:T(8,128)(2,1)S(1)}) fusion(f32[577,2048]{1,0:T(8,128)} %get-tuple-element.90, f32[2048]{0:T(1024)S(1)} %bitcast.196, bf16[1024,2048]{1,0:T(8,128)(2,1)S(1)} %bitcast.157, bf16[577,512]{1,0:T(8,128)(2,1)S(1)} %get-tuple-element.61, bf16[577,512]{1,0:T(8,128)(2,1)S(1)} %get-tuple-element.60), kind=kOutput, calls=%fused_computation.126 | convolution fusion | flops 2436655104 | bytes 12478464 | tf_op jit(solution)/shard_map/dot_general | solution.py:785
  231.1 2.7 fusion.41
  233.8 2.7 fusion.40
  236.6 4.4 fusion.38
  241.0 3.4 multiply_reduce_fusion
  244.4 2.5 fusion.31
  247.1 1.0 copy-done.17
  248.1 0.8 fusion.20
  249.1 0.6 copy-done.29
  249.7 0.8 fusion.21
  250.5 1.2 pad_maximum_fusion.5.upstream_ref
  251.7 28.3 %attention_back.1 = bf16[2,577,1536]{2,1,0:T(8,128)(2,1)} custom-call(bf16[2,577,1536]{2,1,0:T(8,128)(2,1)} %pad_maximum_fusion.projected_ref, bf16[2,577,512]{2,1,0:T(8,128)(2,1)} %pad_maximum_fusion.5.upstream_ref), custom_call_target="tpu_custom_call" | custom-call | tf_op jit(solution)/shard_map/attention_back/pallas_call | solution.py:386
  280.1 4.6 fusion.2
  284.8 4.6 fusion.12
  289.4 2.0 fusion.16.refs_9_
  291.4 0.6 copy-done.15
  292.0 0.8 copy-done.38
  292.8 4.2 fusion.42
  297.0 8.3 %add_convert_fusion.2.refs_8_ = bf16[577,1024]{1,0:T(8,128)(2,1)} fusion(f32[577,1024]{1,0:T(8,128)S(1)} %copy-done.4, f32[577,1024]{1,0:T(8,128)} %fusion.42, bf16[1024,2048]{1,0:T(8,128)(2,1)} %bitcast.156, f32[1024]{0:T(1024)S(1)} %add.172, f32[577,2048]{1,0:T(8,128)} %copy-done.37, f32[2048]{0:T(1024)S(1)} %bitcast.193), kind=kOutput, calls=%fused_computation.42 | convolution fusion | flops 2430748672 | bytes 14841856 | tf_op jit(solution)/shard_map/dot_general | solution.py:785
  305.4 4.4 convolution_convert_fusion
  310.0 2.7 reduce.3
  313.9 4.2 pad_maximum_fusion.2.refs_7_
  318.1 3.6 convolution_convert_fusion.1
  321.7 2.1 pad_maximum_fusion.1.refs_6_
  324.2 2.0 convolution_convert_fusion.6
  326.2 2.0 convolution_convert_fusion.7
  328.3 5.1 convolution_convert_fusion.2
  333.4 5.1 convolution_convert_fusion.3
  338.5 5.3 %convolution_convert_fusion.4 = bf16[1024,2048]{1,0:T(8,128)(2,1)} fusion(bf16[577,512]{1,0:T(8,128)(2,1)S(1)} %copy-done.12, bf16[577,512]{1,0:T(8,128)(2,1)S(1)} %copy-done.10, f32[577,2048]{1,0:T(8,128)S(1)} %bitcast.200, f32[2048]{0:T(1024)S(1)} %bitcast.194), kind=kOutput, calls=%fused_computation.14 | convolution fusion | flops 2432845824 | bytes 10110976 | tf_op jit(solution)/shard_map/dot_general | solution.py:785
  343.8 5.1 convolution_convert_fusion.5
  348.9 170.1 %scatter_grads.1 = (f32[64,2048]{1,0:T(8,128)}, f32[64,2048]{1,0:T(8,128)}, f32[64,512]{1,0:T(8,128)}, f32[64,1664]{1,0:T(8,128)}, bf16[2,577,512]{2,1,0:T(8,128)(2,1)}, /*index=5*/bf16[2,577,512]{2,1,0:T(8,128)(2,1)}) custom-call(bf16[4,2,2,64,2048]{4,3,2,1,0:T(8,128)(2,1)} %bitcast.166, bf16[4,2,2,64,2048]{4,3,2,1,0:T(8,128)(2,1)} %bitcast.165, ...), custom_call_target="tpu_custom_call" | custom-call | tf_op jit(solution)/shard_map/scatter_grads/pallas_call | solution.py:762
  519.1 3.0 reshape.261
  522.5 0.9 reshape.260
  523.4 1.2 reshape.257
  526.4 0.7 copy.61
  527.0 0.8 copy.62
  527.8 0.8 copy.63
  (167 shorter events, 7.3 us)
Async XLA Ops:
  0.6 5.8 %copy-start.27 = (bf16[1154,512]{1,0:T(8,128)(2,1)S(1)}, bf16[1154,512]{1,0:T(8,128)(2,1)}, u32[]{:S(2)}) copy-start(bf16[1154,512]{1,0:T(8,128)(2,1)} %param.14) | copy-start | bytes 3545092
  0.7 7.1 %copy-start.28 = (bf16[1154,512]{1,0:T(8,128)(2,1)S(1)}, bf16[1154,512]{1,0:T(8,128)(2,1)}, u32[]{:S(2)}) copy-start(bf16[1154,512]{1,0:T(8,128)(2,1)} %param.27) | copy-start | bytes 3545092
  6.4 2.5 copy-start.30
  6.5 3.3 copy-start.31
  7.7 2.7 copy-start.35
  173.6 6.6 %copy-start.5 = (bf16[577,512]{1,0:T(8,128)(2,1)}, bf16[577,512]{1,0:T(8,128)(2,1)S(1)}, u32[]{:S(2)}) copy-start(bf16[577,512]{1,0:T(8,128)(2,1)S(1)} %get-tuple-element.63) | copy-start | bytes 1772548
  186.7 16.8 %copy-start.20 = (bf16[2,4,2,2,64,512]{5,4,3,2,1,0:T(8,128)(2,1)S(1)}, bf16[2,4,2,2,64,512]{5,4,3,2,1,0:T(8,128)(2,1)}, u32[]{:S(2)}) copy-start(bf16[2,4,2,2,64,512]{5,4,3,2,1,0:T(8,128)(2,1)} %get-tuple-element.29) | copy-start | bytes 6291460
  203.4 2.2 copy-start.18
  204.6 1.0 copy-start.16
  211.3 29.6 %copy-start.3 = (f32[577,1024]{1,0:T(8,128)}, f32[577,1024]{1,0:T(8,128)S(1)}, u32[]{:S(2)}) copy-start(f32[577,1024]{1,0:T(8,128)S(1)} %get-tuple-element.88) | copy-start | bytes 7090180
  212.0 21.9 %copy-start.21 = (bf16[577,1024]{1,0:T(8,128)(2,1)}, bf16[577,1024]{1,0:T(8,128)(2,1)S(1)}, u32[]{:S(2)}) copy-start(bf16[577,1024]{1,0:T(8,128)(2,1)S(1)} %add_convert_fusion.3) | copy-start | bytes 3545092
  216.4 5.5 %slice-start = ((s8[8388608]{0:T(1024)(128)(4,1)}), s8[4194304]{0:T(1024)(128)(4,1)S(1)}, s32[]{:S(2)}) async-start(s8[8388608]{0:T(1024)(128)(4,1)} %bitcast.153), calls=%async_computation | async-start | bytes 8388608
  216.4 5.4 %copy-start.25 = (bf16[2,577,512]{2,1,0:T(8,128)(2,1)S(1)}, bf16[2,577,512]{2,1,0:T(8,128)(2,1)}, u32[]{:S(2)}) copy-start(bf16[2,577,512]{2,1,0:T(8,128)(2,1)} %get-tuple-element.26) | copy-start | bytes 3545092
  216.4 6.3 %slice-start.1 = ((s8[8388608]{0:T(1024)(128)(4,1)}), s8[4194304]{0:T(1024)(128)(4,1)S(1)}, s32[]{:S(2)}) async-start(s8[8388608]{0:T(1024)(128)(4,1)} %bitcast.153), calls=%async_computation.1 | async-start | bytes 8388608
  221.9 22.5 %copy-start.9 = (bf16[577,512]{1,0:T(8,128)(2,1)}, bf16[577,512]{1,0:T(8,128)(2,1)S(1)}, u32[]{:S(2)}) copy-start(bf16[577,512]{1,0:T(8,128)(2,1)S(1)} %get-tuple-element.60) | copy-start | bytes 1772548
  221.9 22.5 %copy-start.11 = (bf16[577,512]{1,0:T(8,128)(2,1)}, bf16[577,512]{1,0:T(8,128)(2,1)S(1)}, u32[]{:S(2)}) copy-start(bf16[577,512]{1,0:T(8,128)(2,1)S(1)} %get-tuple-element.61) | copy-start | bytes 1772548
  223.4 7.7 %copy-start.14 = (bf16[1,4,2,2,64,2048]{5,4,3,2,1,0:T(8,128)(2,1)}, bf16[1,4,2,2,64,2048]{5,4,3,2,1,0:T(8,128)(2,1)S(1)}, u32[]{:S(2)}) copy-start(bf16[1,4,2,2,64,2048]{5,4,3,2,1,0:T(8,128)(2,1)S(1)} %get-tuple-element.55) | copy-start | bytes 12582916
  223.4 13.1 %copy-start.13 = (bf16[1,4,2,2,64,2048]{5,4,3,2,1,0:T(8,128)(2,1)}, bf16[1,4,2,2,64,2048]{5,4,3,2,1,0:T(8,128)(2,1)S(1)}, u32[]{:S(2)}) copy-start(bf16[1,4,2,2,64,2048]{5,4,3,2,1,0:T(8,128)(2,1)S(1)} %get-tuple-element.54) | copy-start | bytes 12582916
  231.1 2.7 copy-start.40
  236.5 4.4 copy-start.37
  240.9 3.4 copy-start.42
  246.9 1.2 copy-start.17
  248.1 1.0 copy-start.23
  248.1 1.7 copy-start.29
  280.1 4.7 copy-start
  280.1 4.7 copy-start.6
  289.4 2.6 copy-start.15
  289.4 3.4 copy-start.38
  292.8 4.3 copy-start.4
  297.0 8.3 %copy-start.1 = (bf16[2,577,1536]{2,1,0:T(8,128)(2,1)S(1)}, bf16[2,577,1536]{2,1,0:T(8,128)(2,1)}, u32[]{:S(2)}) copy-start(bf16[2,577,1536]{2,1,0:T(8,128)(2,1)} %attention_back.1) | copy-start | bytes 10635268
  297.0 8.4 %copy-start.7 = (bf16[577,512]{1,0:T(8,128)(2,1)S(1)}, bf16[577,512]{1,0:T(8,128)(2,1)}, u32[]{:S(2)}) copy-start(bf16[577,512]{1,0:T(8,128)(2,1)} %copy-done.5) | copy-start | bytes 1772548
  309.8 3.4 copy-start.10
  309.8 3.4 copy-start.12
  313.9 4.2 copy-start.2
  313.9 4.2 copy-start.8
  321.7 2.1 copy-start.19
  321.7 2.5 copy-start.24
  326.2 2.0 copy-start.22
  326.2 2.1 copy-start.43
  328.3 5.1 copy-start.41
  328.3 10.2 %slice-start.2 = ((s8[4784128]{0:T(1024)(128)(4,1)}), s8[4194304]{0:T(1024)(128)(4,1)S(1)}, s32[]{:S(2)}) async-start(s8[4784128]{0:T(1024)(128)(4,1)} %bitcast.199), calls=%async_computation.2 | async-start | bytes 8388608
  333.4 5.1 slice-start.3
  338.5 5.3 %copy-start.39 = (bf16[577,2048]{1,0:T(8,128)(2,1)S(1)}, bf16[577,2048]{1,0:T(8,128)(2,1)}, u32[]{:S(2)}) copy-start(bf16[577,2048]{1,0:T(8,128)(2,1)} %get-tuple-element.89) | copy-start | bytes 7090180
  519.1 3.0 copy-start.34
  522.0 1.4 copy-start.26
  522.1 4.3 copy-start.36
  522.4 4.6 copy-start.33
  522.5 5.3 %copy-start.32 = (f32[64,2048]{1,0:T(8,128)S(1)}, f32[64,2048]{1,0:T(8,128)}, u32[]{:S(2)}) copy-start(f32[64,2048]{1,0:T(8,128)} %get-tuple-element.37) | copy-start | bytes 1572868

commit v3 on v2

--- a/solution.py
+++ b/solution.py
@@ -400,6 +400,10 @@
 ANY = pl.BlockSpec(memory_space=pl.ANY)
 IN_VMEM = pl.BlockSpec(memory_space=pltpu.VMEM)
 SIDES = 2
+BUFFERS = 6
+CHUNK = 4
+AHEAD = 12
+SPACING = 2
 
 
 def place():
@@ -426,9 +430,14 @@
 
 
 def split_width(width):
+    return width // GROUP // 2 * GROUP
+
+
+def chunks_of(width):
     tiles = width // GROUP
-    first = -(-tiles * 5 // 8)
-    return first * GROUP
+    count = max(tiles // CHUNK, 1)
+    edges = [CHUNK * GROUP * at for at in range(count)] + [width]
+    return [(edges[at], edges[at + 1] - edges[at]) for at in range(count)]
 
 
 class Copies:
@@ -467,28 +476,32 @@
 
 
 def run_waves(chains):
-    stages = max(len(chain) for chain in chains)
-    for wave in range(len(chains) + stages - 1):
-        for stage in range(stages - 1, -1, -1):
-            at = wave - stage
-            if 0 <= at < len(chains) and stage < len(chains[at]):
+    stages = len(chains[0])
+    count = len(chains)
+    for at in range(min(AHEAD, count)):
+        chains[at][0]()
+    for wave in range(1, count + SPACING * (stages - 1)):
+        if wave + AHEAD - 1 < count:
+            chains[wave + AHEAD - 1][0]()
+        for stage in range(stages - 1, 0, -1):
+            at = wave - 1 - SPACING * (stage - 1)
+            if 0 <= at < count:
                 chains[at][stage]()
 
 
-def gather_chain(copies, where, depth, block, whole, local):
+def gather_chain(copies, where, depth, block, whole, local, start, width):
     x, z, y, core = where
-    width = block.shape[1]
     first = split_width(width)
-    parts = (pl.ds(0, first), pl.ds(first, width - first))
+    every = pl.ds(start, width)
+    a, b = pl.ds(start, first), pl.ds(start + first, width - first)
     x_peer = device_of(1 - x, z, y, core)
     y_peer = device_of(x, z, 1 - y, core)
     partner = device_of(x, z, y, 1 - core)
     steps = range(1, depth)
     z_peers = [device_of(x, lax.rem(z + k, depth), y, core) for k in steps]
     z_from = [lax.rem(z + depth - k, depth) for k in steps]
-    a, c = parts
-    az, cz = [copies.slot() for _ in steps], [copies.slot() for _ in steps]
-    ay, ax, cx, cy = [copies.slot() for _ in range(4)]
+    along = [copies.slot() for _ in steps]
+    ay, ax, bx, by = [copies.slot() for _ in range(4)]
     shared = [copies.slot() for _ in range(5)]
 
     def share(slot, target):
@@ -497,47 +510,43 @@
     def begin():
         mine = whole.at[x, z, y, core]
         for k in range(depth - 1):
-            copies.send(az[k], block.at[:, a], mine.at[:, a], z_peers[k])
-        copies.send(cx, block.at[:, c], mine.at[:, c], x_peer)
+            copies.send(along[k], block.at[:, every], mine.at[:, every], z_peers[k])
 
     def second():
-        local.wait()
+        if local is not None:
+            local.wait()
         for k in range(depth - 1):
-            copies.arrived(az[k], whole.at[x, z_from[k], y, core, :, a], z_peers[k])
-        column = whole.at[x, :, y, core, :, a]
-        copies.send(ay, column, column, y_peer)
-        copies.arrived(cx, whole.at[1 - x, z, y, core, :, c], x_peer)
-        pair = whole.at[:, z, y, core, :, c]
-        for k in range(depth - 1):
-            copies.send(cz[k], pair, pair, z_peers[k])
-        share(shared[0], column)
+            copies.arrived(along[k], whole.at[x, z_from[k], y, core, :, every], z_peers[k])
+        for slot, part, peer in ((ay, a, y_peer), (bx, b, x_peer)):
+            column = whole.at[x, :, y, core, :, part]
+            copies.send(slot, column, column, peer)
+        share(shared[0], whole.at[x, :, y, core, :, every])
 
     def third():
         copies.arrived(ay, whole.at[x, :, 1 - y, core, :, a], y_peer)
         plane = whole.at[x, :, :, core, :, a]
         copies.send(ax, plane, plane, x_peer)
-        for k in range(depth - 1):
-            copies.arrived(cz[k], whole.at[:, z_from[k], y, core, :, c], z_peers[k])
-        sheet = whole.at[:, :, y, core, :, c]
-        copies.send(cy, sheet, sheet, y_peer)
+        copies.arrived(bx, whole.at[1 - x, :, y, core, :, b], x_peer)
+        sheet = whole.at[:, :, y, core, :, b]
+        copies.send(by, sheet, sheet, y_peer)
         share(shared[1], whole.at[x, :, 1 - y, core, :, a])
-        share(shared[2], sheet)
+        share(shared[2], whole.at[1 - x, :, y, core, :, b])
 
     def fourth():
         copies.arrived(ax, whole.at[1 - x, :, :, core, :, a], x_peer)
         share(shared[3], whole.at[1 - x, :, :, core, :, a])
-        copies.arrived(cy, whole.at[:, :, 1 - y, core, :, c], y_peer)
-        share(shared[4], whole.at[:, :, 1 - y, core, :, c])
+        copies.arrived(by, whole.at[:, :, 1 - y, core, :, b], y_peer)
+        share(shared[4], whole.at[:, :, 1 - y, core, :, b])
 
     def last():
         other = 1 - core
-        copies.arrived(shared[0], whole.at[x, :, y, other, :, a], partner)
+        copies.arrived(shared[0], whole.at[x, :, y, other, :, every], partner)
         copies.arrived(shared[1], whole.at[x, :, 1 - y, other, :, a], partner)
-        copies.arrived(shared[2], whole.at[:, :, y, other, :, c], partner)
+        copies.arrived(shared[2], whole.at[1 - x, :, y, other, :, b], partner)
         copies.arrived(shared[3], whole.at[1 - x, :, :, other, :, a], partner)
-        copies.arrived(shared[4], whole.at[:, :, 1 - y, other, :, c], partner)
-
-    return begin, (second, third, fourth, last)
+        copies.arrived(shared[4], whole.at[:, :, 1 - y, other, :, b], partner)
+
+    return begin, second, third, fourth, last
 
 
 def gather_kernel(depth, pieces_count, *refs):
@@ -560,19 +569,17 @@
     for copy in local + kept:
         copy.start()
     greet(*where, depth)
-    chains = [
-        gather_chain(copies, where, depth, *item) for item in zip(blocks, wholes, local)
-    ]
+    chains = []
+    for block, whole, copy in zip(blocks, wholes, local):
+        for start, width in chunks_of(block.shape[1]):
+            once = copy if start == 0 else None
+            chains.append(gather_chain(copies, where, depth, block, whole, once, start, width))
+    slots = []
     x_peer = device_of(1 - x, z, y, core)
-    slots = [copies.slot() for _ in pieces]
     for at in range(pieces_count):
-        if at == 0:
-            copies.send(slots[at], pieces[at].at[1 - x], images[at].at[x], x_peer)
-    for begin, _ in chains:
-        begin()
-    for at in range(1, pieces_count):
+        slots.append(copies.slot())
         copies.send(slots[at], pieces[at].at[1 - x], images[at].at[x], x_peer)
-    run_waves([rest for _, rest in chains])
+    run_waves(chains)
     for at in range(pieces_count):
         copies.arrived(slots[at], images[at].at[1 - x], x_peer)
         kept[at].wait()
@@ -580,7 +587,8 @@
 
 
 def gather_weights(pieces, blocks, depth):
-    copies = (2 * (depth - 1) + 9) * len(blocks) + len(pieces)
+    chunks = sum(len(chunks_of(block.shape[1])) for block in blocks)
+    copies = (depth + 8) * chunks + len(pieces)
     return pl.pallas_call(
         functools.partial(gather_kernel, depth, len(pieces)),
         in_specs=[IN_VMEM] * (len(pieces) + len(blocks)),
@@ -607,89 +615,91 @@
         target(at)[...] = total.astype(jnp.bfloat16)
 
 
-def scatter_chain(copies, where, depth, grad, total, buffers, load):
+def scatter_chain(copies, where, depth, grad, total, buffers, load_sems, start, width):
     x, z, y, core = where
-    own, halves, ax_in, ay_in, az_in, cy_in, cz_in, c_sum, cx_in = buffers
-    width = total.shape[1]
+    own, halves, ax_in, by_in, along, along_in = buffers
     first = split_width(width)
-    a, c = pl.ds(0, first), pl.ds(first, width - first)
+    every = pl.ds(start, width)
+    a, b = pl.ds(start, first), pl.ds(start + first, width - first)
     x_peer = device_of(1 - x, z, y, core)
     y_peer = device_of(x, z, 1 - y, core)
     partner = device_of(x, z, y, 1 - core)
     steps = range(1, depth)
     z_to = [lax.rem(z + k, depth) for k in steps]
     z_peers = [device_of(x, at, y, core) for at in z_to]
-    az, cz = [copies.slot() for _ in steps], [copies.slot() for _ in steps]
     pair = [copies.slot() for _ in range(SIDES)]
-    ax, ay, cy, cx = [copies.slot() for _ in range(4)]
+    ax, ay, bx, by = [copies.slot() for _ in range(4)]
+    hops = [copies.slot() for _ in steps]
+    load = [
+        pltpu.make_async_copy(
+            grad[side].at[:, :, core, :, every],
+            own.at[side, :, :, :, every],
+            load_sems[side],
+        )
+        for side in range(SIDES)
+    ]
 
     def begin():
-        for copy in load:
-            copy.start()
         for side in range(SIDES):
+            load[side].start()
             copies.send(
-                pair[side], grad[side].at[:, :, 1 - core], halves.at[side], partner
+                pair[side],
+                grad[side].at[:, :, 1 - core, :, every],
+                halves.at[side, :, :, :, every],
+                partner,
             )
 
     def second():
         for side in range(SIDES):
             load[side].wait()
-            copies.arrived(pair[side], halves.at[side], partner)
+            copies.arrived(pair[side], halves.at[side, :, :, :, every], partner)
 
         def at_block(ref, at):
-            return ref.at[lax.div(at, depth * 2), lax.rem(lax.div(at, 2), depth), lax.rem(at, 2)]
+            return ref.at[
+                lax.div(at, depth * 2), lax.rem(lax.div(at, 2), depth), lax.rem(at, 2), :, every
+            ]
 
         add_blocks(
             SIDES * depth * 2, lambda at: at_block(halves, at), lambda at: at_block(own, at)
         )
-        copies.send(ax, halves.at[1 - x, :, :, :, a], ax_in, x_peer)
-        copies.send(cy, halves.at[:, :, 1 - y, :, c], cy_in, y_peer)
+        copies.send(ax, halves.at[1 - x, :, :, :, a], ax_in.at[:, :, :, a], x_peer)
+        copies.send(by, halves.at[:, :, 1 - y, :, b], by_in.at[:, :, :, b], y_peer)
 
     def third():
-        copies.arrived(ax, ax_in, x_peer)
+        copies.arrived(ax, ax_in.at[:, :, :, a], x_peer)
         add_blocks(
             depth * 2,
-            lambda at: ax_in.at[lax.div(at, 2), lax.rem(at, 2)],
+            lambda at: ax_in.at[lax.div(at, 2), lax.rem(at, 2), :, a],
             lambda at: halves.at[x, lax.div(at, 2), lax.rem(at, 2), :, a],
         )
-        copies.send(ay, ax_in.at[:, 1 - y], ay_in, y_peer)
-        copies.arrived(cy, cy_in, y_peer)
+        copies.send(ay, ax_in.at[:, 1 - y, :, a], along.at[:, :, a], y_peer)
+        copies.arrived(by, by_in.at[:, :, :, b], y_peer)
         add_blocks(
             SIDES * depth,
-            lambda at: cy_in.at[lax.div(at, depth), lax.rem(at, depth)],
-            lambda at: halves.at[lax.div(at, depth), lax.rem(at, depth), y, :, c],
-        )
+            lambda at: by_in.at[lax.div(at, depth), lax.rem(at, depth), :, b],
+            lambda at: halves.at[lax.div(at, depth), lax.rem(at, depth), y, :, b],
+        )
+        copies.send(bx, by_in.at[1 - x, :, :, b], along.at[:, :, b], x_peer)
+
+    def fourth():
+        copies.arrived(ay, along.at[:, :, a], y_peer)
+        add_blocks(depth, lambda at: along.at[at, :, a], lambda at: ax_in.at[at, y, :, a])
+        copies.arrived(bx, along.at[:, :, b], x_peer)
+        add_blocks(depth, lambda at: along.at[at, :, b], lambda at: by_in.at[x, at, :, b])
         for k in range(depth - 1):
-            copies.send(cz[k], cy_in.at[:, z_to[k]], cz_in.at[k], z_peers[k])
-
-    def fourth():
-        copies.arrived(ay, ay_in, y_peer)
-        add_blocks(depth, lambda at: ay_in.at[at], lambda at: ax_in.at[at, y])
-        for k in range(depth - 1):
-            copies.send(az[k], ay_in.at[z_to[k]], az_in.at[k], z_peers[k])
-        for k in range(depth - 1):
-            copies.arrived(cz[k], cz_in.at[k], z_peers[k])
-
-        @pl.loop(0, SIDES)
-        def _(at):
-            sums = cy_in[at, z].astype(jnp.float32)
-            for k in range(depth - 1):
-                sums += cz_in[k, at].astype(jnp.float32)
-            c_sum[at] = sums.astype(jnp.bfloat16)
-
-        copies.send(cx, c_sum.at[1 - x], cx_in, x_peer)
+            copies.send(
+                hops[k], along.at[z_to[k], :, every], along_in.at[k, :, every], z_peers[k]
+            )
 
     def last():
         for k in range(depth - 1):
-            copies.arrived(az[k], az_in.at[k], z_peers[k])
-        sums = ay_in[z].astype(jnp.float32)
+            copies.arrived(hops[k], along_in.at[k, :, every], z_peers[k])
+        sums = along[z, :, every].astype(jnp.float32)
         for k in range(depth - 1):
-            sums += az_in[k].astype(jnp.float32)
-        total[:, :first] = sums
-        copies.arrived(cx, cx_in, x_peer)
-        total[:, first:] = c_sum[x].astype(jnp.float32) + cx_in[...].astype(jnp.float32)
-
-    return begin, (second, third, fourth, last)
+            sums += along_in[k, :, every].astype(jnp.float32)
+        total[:, every] = sums
+
+    return begin, second, third, fourth, last
 
 
 def scatter_kernel(depth, count, wholes_count, *refs):
@@ -711,26 +721,23 @@
         mine = pl.ds(pl.multiple_of(x * width, width), width)
         theirs = pl.ds(pl.multiple_of((1 - x) * width, width), width)
         copy = pltpu.make_async_copy(
-            wholes[at].at[:, mine], pieces[at].at[x], own_sems.at[SIDES * count + at]
+            wholes[at].at[:, mine], pieces[at].at[x], own_sems.at[at]
         )
         copy.start()
         kept.append(copy)
         copies.send(slots[at], wholes[at].at[:, theirs], pieces[at].at[x], x_peer)
     chains = []
+    loads = iter(range(own_sems.shape[0] - wholes_count))
     for at in range(count):
-        buffers = refs[9 * at : 9 * at + 9]
-        load = [
-            pltpu.make_async_copy(
-                grads[at][side].at[:, :, core], buffers[0].at[side], own_sems.at[SIDES * at + side]
+        buffers = refs[BUFFERS * at : BUFFERS * at + BUFFERS]
+        for start, width in chunks_of(totals[at].shape[1]):
+            load_sems = [own_sems.at[wholes_count + next(loads)] for _ in range(SIDES)]
+            chains.append(
+                scatter_chain(
+                    copies, where, depth, grads[at], totals[at], buffers, load_sems, start, width
+                )
             )
-            for side in range(SIDES)
-        ]
-        chains.append(
-            scatter_chain(copies, where, depth, grads[at], totals[at], buffers, load)
-        )
-    for begin, _ in chains:
-        begin()
-    run_waves([rest for _, rest in chains])
+    run_waves(chains)
     for at in range(wholes_count):
         copies.arrived(slots[at], pieces[at].at[1 - x], x_peer)
         kept[at].wait()
@@ -738,24 +745,20 @@
 
 
 def scatter_buffers(depth, rows, width):
-    first = split_width(width)
-    rest = width - first
     shapes = [
         (SIDES, depth, 2, rows, width),
         (SIDES, depth, 2, rows, width),
-        (depth, 2, rows, first),
-        (depth, rows, first),
-        (depth - 1, rows, first),
-        (SIDES, depth, rows, rest),
-        (depth - 1, SIDES, rows, rest),
-        (SIDES, rows, rest),
-        (rows, rest),
+        (depth, 2, rows, width),
+        (SIDES, depth, rows, width),
+        (depth, rows, width),
+        (depth - 1, rows, width),
     ]
     return [pltpu.VMEM(shape, jnp.bfloat16) for shape in shapes]
 
 
 def scatter_grads(grads, wholes, depth):
-    copies = (2 * (depth - 1) + 6) * len(grads) + len(wholes)
+    chunks = sum(len(chunks_of(grad[0].shape[4])) for grad in grads)
+    copies = (depth + 5) * chunks + len(wholes)
     scratch = []
     for grad in grads:
         scratch += scatter_buffers(depth, grad[0].shape[3], grad[0].shape[4])
@@ -772,13 +775,35 @@
         + [
             pltpu.SemaphoreType.DMA((copies,)),
             pltpu.SemaphoreType.DMA((copies,)),
-            pltpu.SemaphoreType.DMA((SIDES * len(grads) + len(wholes),)),
+            pltpu.SemaphoreType.DMA((SIDES * chunks + len(wholes),)),
         ],
         compiler_params=pltpu.CompilerParams(
             collective_id=2, has_side_effects=True, vmem_limit_bytes=60 * 2**20
         ),
         name="scatter_grads",
     )(*[half for grad in grads for half in grad], *wholes)
+
+
+def to_image(piece):
+    col = lax.axis_index("col")
+    rows = piece.shape[0] // 2
+    kept = lax.dynamic_slice_in_dim(piece, col * rows, rows, 0)
+    sent = lax.dynamic_slice_in_dim(piece, (1 - col) * rows, rows, 0)
+    other = lax.ppermute(sent, "col", [(0, 1), (1, 0)])
+    return jnp.where(
+        col == 0, jnp.concatenate([kept, other], 1), jnp.concatenate([other, kept], 1)
+    )
+
+
+def from_image(whole):
+    col = lax.axis_index("col")
+    width = whole.shape[1] // 2
+    kept = lax.dynamic_slice_in_dim(whole, col * width, width, 1)
+    sent = lax.dynamic_slice_in_dim(whole, (1 - col) * width, width, 1)
+    other = lax.ppermute(sent, "col", [(0, 1), (1, 0)])
+    return jnp.where(
+        col == 0, jnp.concatenate([kept, other], 0), jnp.concatenate([other, kept], 0)
+    )
 
 
 def product(left, right, left_at, right_at):
@@ -851,8 +876,8 @@
     first_block = jnp.concatenate([group_order(mixer_weight).astype(low), vector_block], 1)
     depth = rows // 4
     sides = (cols, tokens.shape[0] // cols, tokens.shape[1])
-    image, upstream_low, mixed, merger, expander, reducer = gather_weights(
-        [tokens.reshape(sides), cotangent.reshape(sides)],
+    image, mixed, merger, expander, reducer = gather_weights(
+        [tokens.reshape(sides)],
         [
             first_block,
             merge_weight.astype(low).T,
@@ -862,7 +887,7 @@
         depth,
     )
     image = jnp.concatenate([image[h] for h in range(cols)], 1)
-    upstream_low = jnp.concatenate([upstream_low[h] for h in range(cols)], 1)
+    upstream_low = to_image(cotangent)
     mixed, merger, expander, reducer = [
         whole.reshape(cols, rows * block_rows, whole.shape[-1])
         for whole in (mixed, merger, expander, reducer)
@@ -901,10 +926,17 @@
     expanded = [product(second_low, expander[h], 1, 0) + expand_shift[h] for h in range(cols)]
     activated = [quick_gelu(part).astype(low) for part in expanded]
     reduced = sum(product(activated[h], reducer[h], 1, 1) for h in range(cols))
-    image_output = (hidden + reduced + reduce_shift).astype(low)
+    layer_output = from_image((hidden + reduced + reduce_shift).astype(low))
 
     upstream = upstream_low.astype(jnp.float32)
     reducer_grad = [product(upstream_low, activated[h], 0, 0).astype(low) for h in range(cols)]
+    reducer_parts = [part.reshape(rows, block_rows, -1) for part in reducer_grad]
+    reduce_total = lax.psum_scatter(
+        jnp.stack(reducer_parts, 1).reshape(rows * cols * block_rows, -1),
+        ("row", "col"),
+        scatter_dimension=0,
+        tiled=True,
+    ).astype(jnp.float32)
     expanded_grad = [
         (product(upstream_low, reducer[h], 1, 0) * gelu_slope(expanded[h])).astype(low)
         for h in range(cols)
@@ -950,12 +982,11 @@
     mixed_grad = [jnp.concatenate([mixer_grad[h], vector_grads[h]], 1) for h in range(cols)]
     grads = [
         [part.reshape(depth, 2, 2, block_rows, -1) for part in halves]
-        for halves in (reducer_grad, expander_grad, merger_grad, mixed_grad)
+        for halves in (expander_grad, merger_grad, mixed_grad)
     ]
-    reduce_total, expand_total, merge_total, mixed_total, layer_output, tokens_gradient = (
-        scatter_grads(grads, [image_output, input_grad.astype(low)], depth)
-    )
-    layer_output = layer_output.reshape(tokens.shape)
+    expand_total, merge_total, mixed_total, tokens_gradient = (
+        scatter_grads(grads, [input_grad.astype(low)], depth)
+    )
     tokens_gradient = tokens_gradient.reshape(tokens.shape).astype(jnp.float32)
     mixer_total = part_order(mixed_total[:, :mixer_width])
     vector_total = mixed_total[:vector_rows, mixer_width:].reshape(-1)

time: 535 us -> 552 us (1.032)
  Pallas kernels: 376 us -> 350 us
  local copies, waits for them, and re-layouts: 29.1 us -> 44.5 us
  between operations: 1.86 us -> 15.3 us
  other arithmetic: 25.5 us -> 33.3 us
    pallas_call x1, Pallas kernels: 161 us -> 129 us  [gather_weights(): pl.pallas_call(functools.partial(gather_kernel, depth, len(pieces)), in_s...]
    another operation x1 -> x2, local copies, waits for them, and re-layouts: 0.01 us -> 8.32 us  [the longest x1 8.3 us: image_shards(): jnp.stack(reducer_parts, 1).reshape(rows * cols * block_rows, -1)]
    another operation x2 -> x3, other arithmetic: 1.34 us -> 7.5 us  [the longest x1 7.49 us: image_shards(): jnp.stack(reducer_parts, 1).reshape(rows * cols * block_rows, -1)]
    pallas_call x1, Pallas kernels: 170 us -> 176 us  [scatter_grads(): pl.pallas_call(functools.partial(scatter_kernel, depth, len(grads), len(w...]
  transfers between devices with their start and end apart: 0 -> 3, of which waited for: 0 -> 0; matrix products, arithmetic and copies ran while one was open for 0% -> 25% of each run, Pallas kernels for 0% -> 65%
where the time goes in v3:
time: 552 us; the launch traced here: 541 us
  Pallas kernels  350 us (63%)
  matrix products  95 us (17%)
  local copies, waits for them, and re-layouts  44.5 us (8%)
  other arithmetic  33.3 us (6%)
  between operations  15.3 us (3%)
    pallas_call x1, Pallas kernels, scatter_grads(): pl.pallas_call(functools.partial(scatter_kernel, depth, len(grads), len(w...  176 us
    pallas_call x1, Pallas kernels, gather_weights(): pl.pallas_call(functools.partial(gather_kernel, depth, len(pieces)), in_s...  129 us
    dot_general x24, matrix products, product(): lax.dot_general(left, right, (((left_at,), (right_at,)), ((), ())), prefe...  95 us
    pallas_call x1, Pallas kernels, attention_back(): pl.pallas_call(attention_back_kernel, grid=(halves, groups), in_specs=[pl...  28.4 us
    pallas_call x1, Pallas kernels, attention_forward(): pl.pallas_call(attention_forward_kernel, grid=(halves, groups), in_specs=...  16.3 us
  transfers between devices with their start and end apart: 3, of which 0 were waited for; matrix products, arithmetic and copies ran while one was open for 25% of the time, Pallas kernels for 65%

profile of v3, /device:TPU:28, one launch (start us, length us, event | category | flops | bytes accessed | tf_op | source)
XLA Modules:
  0.0 541.3 jit_solution(13253279891470859773)
XLA Ops:
  7.3 2.6 constant_dynamic-slice_fusion.1
  10.0 1.6 collective-permute-start.1
  11.5 1.3 reshape.234.refs_0_
  13.5 0.6 convert_bitcast_fusion.2.refs_2_
  14.1 0.7 convert_element_type.129.refs_3_
  14.9 0.7 convert_bitcast_fusion.1.refs_4_
  15.6 0.7 fusion.24.refs_1_
  16.3 129.2 %gather_weights.1 = (bf16[2,577,512]{2,1,0:T(8,128)(2,1)}, bf16[2,4,2,2,64,1664]{5,4,3,2,1,0:T(8,128)(2,1)}, bf16[2,4,2,2,64,512]{5,4,3,2,1,0:T(8,128)(2,1)}, bf...) custom-call(bf16[2,577,512]{2,1,0:T(8,128)(2,1)} %reshape.234.refs_0_, ...), custom_call_target="tpu_custom_call" | custom-call | tf_op jit(solution)/shard_map/gather_weights/pallas_call | solution.py:592
  145.5 1.1 slice.225
  147.0 2.7 fusion.34
  150.2 1.3 slice_bitcast_fusion.19
  152.1 4.2 fusion.1
  156.3 4.2 fusion
  160.5 2.1 pad_maximum_fusion.1.projected_ref
  162.6 16.3 %attention_forward.1 = bf16[2,577,512]{2,1,0:T(8,128)(2,1)} custom-call(bf16[2,577,1536]{2,1,0:T(8,128)(2,1)} %pad_maximum_fusion.1.projected_ref), custom_call_target="tpu_custom_call" | custom-call | tf_op jit(solution)/shard_map/attention_forward/pallas_call | solution.py:373
  179.1 6.0 %fusion.32 = (bf16[1,4,2,2,64,2048]{5,4,3,2,1,0:T(8,128)(2,1)}, bf16[1,4,2,2,64,2048]{5,4,3,2,1,0:T(8,128)(2,1)}) fusion(bf16[2,4,2,2,64,2048]{5,4,3,2,1,0:T(8,128)(2,1)} %get-tuple-element.26), kind=kLoop, calls=%fused_computation.124 | loop fusion | bytes 16777216 | tf_op jit(solution)/shard_map/slice | solution.py:926
  185.2 1.9 fusion.22
  187.1 2.7 fusion.30
  190.3 8.4 %multiply_convert_fusion.3 = (bf16[577,2048]{1,0:T(8,128)(2,1)S(1)}, f32[577,2048]{1,0:T(8,128)}) fusion(f32[2048]{0:T(1024)S(1)} %bitcast.188, bf16[577,1024]{1,0:T(8,128)(2,1)S(1)} %add_convert_fusion.3, bf16[1024,2048]{1,0:T(8,128)(2,1)} %bitcast.154), kind=kOutput, calls=%fused_computation.5 | convolution fusion | flops 2428385280 | bytes 12474368 | tf_op jit(solution)/shard_map/dot_general | solution.py:810
  198.7 2.7 fusion.41
  201.4 7.3 %convolution_convert_fusion.3 = bf16[1024,2048]{1,0:T(8,128)(2,1)} fusion(bf16[577,2048]{1,0:T(8,128)(2,1)S(1)} %get-tuple-element.85, bf16[577,512]{1,0:T(8,128)(2,1)} %collective-permute-done.1, bf16[577,512]{1,0:T(8,128)(2,1)S(1)} %copy-done.6, pred[]{:T(512)S(6)} %eq.4), kind=kOutput, calls=%fused_computation.14 | convolution fusion | flops 2427528192 | bytes 7739393 | tf_op jit(solution)/shard_map/dot_general | solution.py:810
  208.7 6.6 %convolution_convert_fusion.2 = bf16[1024,2048]{1,0:T(8,128)(2,1)} fusion(f32[577,2048]{1,0:T(8,128)S(1)} %fusion.41, f32[2048]{0:T(1024)S(1)} %bitcast.190, bf16[577,512]{1,0:T(8,128)(2,1)} %collective-permute-done.1, bf16[577,512]{1,0:T(8,128)(2,1)S(1)} %copy-done.6, pred[]{:T(512)S(6)} %eq.4), kind=kOutput, calls=%fused_computation.13 | convolution fusion | flops 2435800064 | bytes 10110977 | tf_op jit(solution)/shard_map/dot_general | solution.py:810
  215.3 7.5 %pad_maximum_fusion = bf16[16,2,64,2048]{3,2,0,1:T(8,128)(2,1)} fusion(bf16[16,1,64,2048]{3,2,0,1:T(8,128)(2,1)} %bitcast.163, bf16[16,1,64,2048]{3,2,0,1:T(8,128)(2,1)} %bitcast.162), kind=kLoop, calls=%fused_computation | loop fusion | flops 4194304 | bytes 16777216 | tf_op jit(solution)/shard_map/stack | solution.py:935
  222.7 8.3 %copy.49 = bf16[16,2,64,2048]{3,2,1,0:T(8,128)(2,1)} copy(bf16[16,2,64,2048]{3,2,0,1:T(8,128)(2,1)} %pad_maximum_fusion) | data formatting | bytes 16777216 | tf_op jit(solution)/shard_map/stack | solution.py:935
  231.1 4.6 fusion.33
  235.8 2.7 fusion.40
  238.5 2.8 add_convert_fusion.2
  241.3 1.2 constant_dynamic-slice_fusion.3
  242.5 1.5 collective-permute-start
  244.0 5.4 fusion.39
  249.4 2.7 fusion.42
  252.1 5.6 %fusion.38 = (bf16[2048]{0:T(1024)(128)(2,1)S(1)}, bf16[577,2048]{1,0:T(8,128)(2,1)S(1)}) fusion(f32[577,2048]{1,0:T(8,128)S(1)} %bitcast.196, f32[2048]{0:T(1024)S(1)} %bitcast.192, bf16[1024,2048]{1,0:T(8,128)(2,1)S(1)} %bitcast.157, bf16[577,512]{1,0:T(8,128)(2,1)} %collective-permute-done.1, bf16[577,512]{1,0:T(8,128)(2,1)S(1)} %copy-done.7, pred[]{:T(512)S(6)} %eq.4), kind=kOutput, calls=%fused_computation.130 | convolution fusion | flops 2439609344 | bytes 12478465 | tf_op jit(solution)/shard_map/dot_general | solution.py:810
  257.6 3.3 multiply_reduce_fusion
  260.9 3.3 fusion.31
  264.5 1.3 copy-done.21
  265.8 0.8 fusion.21
  267.0 0.8 fusion.20
  267.8 1.1 pad_maximum_fusion.5.upstream_ref
  268.9 28.4 %attention_back.1 = bf16[2,577,1536]{2,1,0:T(8,128)(2,1)} custom-call(bf16[2,577,1536]{2,1,0:T(8,128)(2,1)} %pad_maximum_fusion.1.projected_ref, bf16[2,577,512]{2,1,0:T(8,128)(2,1)} %pad_maximum_fusion.5.upstream_ref), custom_call_target="tpu_custom_call" | custom-call | tf_op jit(solution)/shard_map/attention_back/pallas_call | solution.py:386
  297.3 4.7 fusion.2
  302.0 5.8 %fusion.12 = (f32[577]{0:T(1024)S(1)}, bf16[1024]{0:T(1024)(128)(2,1)S(1)}, f32[577]{0:T(1024)S(1)}, bf16[1024]{0:T(1024)(128)(2,1)S(1)}, f32[577,1024]{1,0:T(8,128)}) fusion(f32[1024]{0:T(1024)S(1)} %mul.160, f32[577]{0:T(1024)S(1)} %get-tuple-element.83, f32[577]{0:T(1024)S(1)} %get-tuple-element.82, bf16[577,512]{1,0:T(8,128)(2,1)S(1)} %copy-done.4, ...), kind=kOutput, calls=%fused_computation.36 | convolution fusion | flops 1823353600 | bytes 10912264 | tf_op jit(solution)/shard_map/dot_general | solution.py:810
  308.0 2.6 reduce.3
  311.1 2.0 fusion.25
  313.7 3.6 convolution_convert_fusion.7
  317.3 3.4 convolution_convert_fusion.1
  320.6 2.0 pad_maximum_fusion.2.refs_4_
  322.7 3.3 convolution_convert_fusion
  326.0 2.1 pad_maximum_fusion.3.refs_5_
  328.1 0.6 copy-done.14
  328.7 2.0 fusion.16.refs_6_
  331.2 5.1 convolution_convert_fusion.5
  336.3 5.3 convolution_convert_fusion.4
  341.6 2.0 convolution_convert_fusion.6
  343.6 176.3 %scatter_grads.1 = (f32[64,2048]{1,0:T(8,128)}, f32[64,512]{1,0:T(8,128)}, f32[64,1664]{1,0:T(8,128)}, bf16[2,577,512]{2,1,0:T(8,128)(2,1)}) custom-call(bf16[4,2,2,64,2048]{4,3,2,1,0:T(8,128)(2,1)} %bitcast.160, bf16[4,2,2,64,2048]{4,3,2,1,0:T(8,128)(2,1)} %bitcast.161, bf16[4,2,2,64,512]{4,3,2,1,0:T(8,128)(2,1)} %bitcast.174, ...), custom_call_target="tpu_custom_call" | custom-call | tf_op jit(solution)/shard_map/scatter_grads/pallas_call | solution.py:765
  519.9 0.7 slice.214
  520.5 1.0 slice.217
  521.6 3.0 reshape.249
  525.0 0.9 reshape.247
  526.0 0.6 slice.218
  526.5 1.2 slice_bitcast_fusion.25
  528.2 2.7 maximum_select_fusion.1
  531.0 1.8 convert_bitcast_fusion
  532.7 0.7 copy.63
  533.4 0.8 copy.64
  (178 shorter events, 6.1 us)
Async XLA Ops:
  7.2 4.4 copy-start.20
  7.2 523.8 %reduce-scatter.2.cloned.1.call-start = ((), (), s32[]{:S(2)}) async-start(), calls=%async_computation.1 | async-start | bytes 8650752 | tf_op jit(solution)/shard_map/reduce_scatter | solution.py:934
  7.2 5.5 %copy-start.37 = (f32[128]{0:T(128)S(1)}, f32[128]{0:T(128)}, u32[]{:S(2)}) copy-start(f32[128]{0:T(128)} %param.24) | copy-start | bytes 1540
  7.3 5.5 %copy-start.36 = (f32[2,32]{1,0:T(2,128)S(1)}, f32[2,32]{1,0:T(2,128)}, u32[]{:S(2)}) copy-start(f32[2,32]{1,0:T(2,128)} %param.18) | copy-start | bytes 772
  7.3 5.6 %copy-start.30 = (f32[32]{0:T(128)S(1)}, f32[32]{0:T(128)}, u32[]{:S(2)}) copy-start(f32[32]{0:T(128)} %param.16) | copy-start | bytes 388
  7.3 5.6 %copy-start.31 = (f32[32]{0:T(128)S(1)}, f32[32]{0:T(128)}, u32[]{:S(2)}) copy-start(f32[32]{0:T(128)} %param.15) | copy-start | bytes 388
  7.3 5.6 %copy-start.32 = (f32[32]{0:T(128)S(1)}, f32[32]{0:T(128)}, u32[]{:S(2)}) copy-start(f32[32]{0:T(128)} %param.21) | copy-start | bytes 388
  7.3 5.6 %copy-start.33 = (f32[32]{0:T(128)S(1)}, f32[32]{0:T(128)}, u32[]{:S(2)}) copy-start(f32[32]{0:T(128)} %param.20) | copy-start | bytes 388
  7.3 5.6 %copy-start.34 = (f32[32]{0:T(128)S(1)}, f32[32]{0:T(128)}, u32[]{:S(2)}) copy-start(f32[32]{0:T(128)} %param.26) | copy-start | bytes 388
  7.3 5.6 %copy-start.35 = (f32[32]{0:T(128)S(1)}, f32[32]{0:T(128)}, u32[]{:S(2)}) copy-start(f32[32]{0:T(128)} %param.22) | copy-start | bytes 388
  7.3 5.7 %copy-start.25 = (f32[64,3,512]{2,0,1:T(8,128)S(1)}, f32[64,3,512]{2,0,1:T(8,128)}, u32[]{:S(2)}) copy-start(f32[64,3,512]{2,0,1:T(8,128)} %param.17) | copy-start | bytes 1179652
  10.0 3.5 copy-start.26
  10.0 4.2 copy-start.22
  10.0 4.9 copy-start.23
  10.0 191.4 %collective-permute-start.1 = (bf16[577,512]{1,0:T(8,128)(2,1)}, bf16[577,512]{1,0:T(8,128)(2,1)}, u32[]{:S(2)}, u32[]{:S(2)}) collective-permute-start(bf16[577,512]{1,0:T(8,128)(2,1)} %get-tuple-element.59), channel_id=1, source_target_pairs={{0,1},{1,0},{2,3},{3,2},{4,5},{5,4},{6,7},{7,6},{8,9},{9,8},{10,11... | collective-permute-start | bytes 1772552 | tf_op jit(solution)/shard_map/ppermute | solution.py:792
  149.7 35.5 %copy-start.11 = (bf16[1,4,2,2,64,512]{5,4,3,2,1,0:T(8,128)(2,1)}, bf16[1,4,2,2,64,512]{5,4,3,2,1,0:T(8,128)(2,1)S(1)}, u32[]{:S(2)}) copy-start(bf16[1,4,2,2,64,512]{5,4,3,2,1,0:T(8,128)(2,1)S(1)} %get-tuple-element.53) | copy-start | bytes 3145732
  150.1 6.1 %copy-start.28 = (f32[1024]{0:T(1024)}, f32[1024]{0:T(1024)S(1)}, u32[]{:S(2)}) copy-start(f32[1024]{0:T(1024)S(1)} %add.153) | copy-start | bytes 12292
  151.6 4.7 copy-start.3
  189.8 67.8 %copy-start.2 = (f32[577,1024]{1,0:T(8,128)}, f32[577,1024]{1,0:T(8,128)S(1)}, u32[]{:S(2)}) copy-start(f32[577,1024]{1,0:T(8,128)S(1)} %get-tuple-element.84) | copy-start | bytes 7090180
  190.3 8.4 %copy-start.16 = (bf16[577,1024]{1,0:T(8,128)(2,1)}, bf16[577,1024]{1,0:T(8,128)(2,1)S(1)}, u32[]{:S(2)}) copy-start(bf16[577,1024]{1,0:T(8,128)(2,1)S(1)} %add_convert_fusion.3) | copy-start | bytes 3545092
  190.3 8.4 %copy-start.8 = (bf16[1,4,2,2,64,2048]{5,4,3,2,1,0:T(8,128)(2,1)S(1)}, bf16[1,4,2,2,64,2048]{5,4,3,2,1,0:T(8,128)(2,1)}, u32[]{:S(2)}) copy-start(bf16[1,4,2,2,64,2048]{5,4,3,2,1,0:T(8,128)(2,1)} %get-tuple-element.48) | copy-start | bytes 12582916
  198.6 2.7 copy-start.39
  198.7 2.7 copy-start.6
  201.4 7.3 %copy-start.38 = (f32[577,2048]{1,0:T(8,128)}, f32[577,2048]{1,0:T(8,128)S(1)}, u32[]{:S(2)}) copy-start(f32[577,2048]{1,0:T(8,128)S(1)} %fusion.41) | copy-start | bytes 14180356
  231.1 4.6 copy-start.40
  231.1 7.3 %slice-start = ((s8[4784128]{0:T(1024)(128)(4,1)}), s8[4194304]{0:T(1024)(128)(4,1)S(1)}, s32[]{:S(2)}) async-start(s8[4784128]{0:T(1024)(128)(4,1)} %bitcast.195), calls=%async_computation.2 | async-start | bytes 8388608
  235.7 2.7 slice-start.1
  235.7 8.2 %slice-start.2 = ((s8[4784128]{0:T(1024)(128)(4,1)}), s8[4194304]{0:T(1024)(128)(4,1)S(1)}, s32[]{:S(2)}) async-start(s8[4784128]{0:T(1024)(128)(4,1)} %bitcast.197), calls=%async_computation.4 | async-start | bytes 8388608
  238.5 5.5 %slice-start.3 = ((s8[4784128]{0:T(1024)(128)(4,1)}), s8[589824]{0:T(1024)(128)(4,1)S(1)}, s32[]{:S(2)}) async-start(s8[4784128]{0:T(1024)(128)(4,1)} %bitcast.197), calls=%async_computation.5 | async-start | bytes 1179648
  241.2 2.7 copy-start.7
  242.5 285.8 %collective-permute-start = (bf16[577,512]{1,0:T(8,128)(2,1)}, bf16[577,512]{1,0:T(8,128)(2,1)}, u32[]{:S(2)}, u32[]{:S(2)}) collective-permute-start(bf16[577,512]{1,0:T(8,128)(2,1)} %get-tuple-element.55), channel_id=1, source_target_pairs={{0,1},{1,0},{2,3},{3,2},{4,5},{5,4},{6,7},{7,6},{8,9},{9,8},{10,11... | collective-permute-start | bytes 1772552 | tf_op jit(solution)/shard_map/ppermute | solution.py:803
  244.0 5.4 copy-start.10
  249.3 2.7 copy-start.41
  252.0 5.6 %copy-start.9 = (bf16[1,4,2,2,64,2048]{5,4,3,2,1,0:T(8,128)(2,1)S(1)}, bf16[1,4,2,2,64,2048]{5,4,3,2,1,0:T(8,128)(2,1)}, u32[]{:S(2)}) copy-start(bf16[1,4,2,2,64,2048]{5,4,3,2,1,0:T(8,128)(2,1)} %get-tuple-element.48) | copy-start | bytes 12582916
  257.6 3.3 copy-start.43
  264.2 1.5 copy-start.21
  264.4 2.1 copy-start.18
  265.8 1.2 copy-start.12
  297.3 4.7 copy-start
  297.3 4.7 copy-start.4
  313.5 3.7 copy-start.1
  313.5 3.7 copy-start.5
  313.5 3.7 copy-start.29
  326.0 2.6 copy-start.14
  328.7 2.0 copy-start.17
  328.7 2.5 copy-start.42
  331.2 5.1 copy-start.44
  336.3 5.3 copy-start.13
  336.3 5.3 copy-start.19
  521.6 6.7 %copy-start.15 = (bf16[577,512]{1,0:T(8,128)(2,1)S(1)}, bf16[577,512]{1,0:T(8,128)(2,1)}, u32[]{:S(2)}) copy-start(bf16[577,512]{1,0:T(8,128)(2,1)} %get-tuple-element.54) | copy-start | bytes 1772548
  524.9 7.8 %copy-start.27 = (f32[64,512]{1,0:T(8,128)S(1)}, f32[64,512]{1,0:T(8,128)}, u32[]{:S(2)}) copy-start(f32[64,512]{1,0:T(8,128)} %get-tuple-element.30) | copy-start | bytes 393220
  524.9 8.5 %copy-start.24 = (f32[64,2048]{1,0:T(8,128)S(1)}, f32[64,2048]{1,0:T(8,128)}, u32[]{:S(2)}) copy-start(f32[64,2048]{1,0:T(8,128)} %get-tuple-element.123) | copy-start | bytes 1572868
Sparse Core Ops, SparseCore 0:
  231.2 279.0 reduce-scatter.1

commit v4 on v3

--- a/solution.py
+++ b/solution.py
@@ -930,13 +930,6 @@
 
     upstream = upstream_low.astype(jnp.float32)
     reducer_grad = [product(upstream_low, activated[h], 0, 0).astype(low) for h in range(cols)]
-    reducer_parts = [part.reshape(rows, block_rows, -1) for part in reducer_grad]
-    reduce_total = lax.psum_scatter(
-        jnp.stack(reducer_parts, 1).reshape(rows * cols * block_rows, -1),
-        ("row", "col"),
-        scatter_dimension=0,
-        tiled=True,
-    ).astype(jnp.float32)
     expanded_grad = [
         (product(upstream_low, reducer[h], 1, 0) * gelu_slope(expanded[h])).astype(low)
         for h in range(cols)
@@ -982,9 +975,9 @@
     mixed_grad = [jnp.concatenate([mixer_grad[h], vector_grads[h]], 1) for h in range(cols)]
     grads = [
         [part.reshape(depth, 2, 2, block_rows, -1) for part in halves]
-        for halves in (expander_grad, merger_grad, mixed_grad)
+        for halves in (reducer_grad, expander_grad, merger_grad, mixed_grad)
     ]
-    expand_total, merge_total, mixed_total, tokens_gradient = (
+    reduce_total, expand_total, merge_total, mixed_total, tokens_gradient = (
         scatter_grads(grads, [input_grad.astype(low)], depth)
     )
     tokens_gradient = tokens_gradient.reshape(tokens.shape).astype(jnp.float32)

time: 552 us -> 487 us (0.88)
  Pallas kernels: 350 us -> 307 us
  between operations: 15.3 us -> 1.94 us
  other arithmetic: 33.3 us -> 26.2 us
    pallas_call x1, Pallas kernels: 176 us -> 133 us  [scatter_grads(): pl.pallas_call(functools.partial(scatter_kernel, depth, len(grads), len(w...]
    another operation x2 -> x1, local copies, waits for them, and re-layouts: 8.32 us -> 0.01 us  [the longest x1 8.3 us: image_shards(): jnp.stack(reducer_parts, 1).reshape(rows * cols * block_rows, -1)]
    another operation x3 -> x2, other arithmetic: 7.5 us -> 0.01 us  [the longest x1 7.49 us: image_shards(): jnp.stack(reducer_parts, 1).reshape(rows * cols * block_rows, -1)]
  transfers between devices with their start and end apart: 3 -> 2, of which waited for: 0 -> 0; matrix products, arithmetic and copies ran while one was open for 25% -> 32% of each run, Pallas kernels for 65% -> 64%
where the time goes in v4:
time: 487 us; the launch traced here: 478 us
  Pallas kernels  307 us (63%)
  matrix products  96.5 us (20%)
  local copies, waits for them, and re-layouts  43.4 us (9%)
  other arithmetic  26.2 us (5%)
    pallas_call x1, Pallas kernels, scatter_grads(): pl.pallas_call(functools.partial(scatter_kernel, depth, len(grads), len(w...  133 us
    pallas_call x1, Pallas kernels, gather_weights(): pl.pallas_call(functools.partial(gather_kernel, depth, len(pieces)), in_s...  129 us
    dot_general x24, matrix products, product(): lax.dot_general(left, right, (((left_at,), (right_at,)), ((), ())), prefe...  96.5 us
    pallas_call x1, Pallas kernels, attention_back(): pl.pallas_call(attention_back_kernel, grid=(halves, groups), in_specs=[pl...  28.2 us
    pallas_call x1, Pallas kernels, attention_forward(): pl.pallas_call(attention_forward_kernel, grid=(halves, groups), in_specs=...  16.3 us
  transfers between devices with their start and end apart: 2, of which 0 were waited for; matrix products, arithmetic and copies ran while one was open for 32% of the time, Pallas kernels for 64%

profile of v4, /device:TPU:28, one launch (start us, length us, event | category | flops | bytes accessed | tf_op | source)
XLA Modules:
  0.0 478.2 jit_solution(12627675551813714947)
XLA Ops:
  0.8 2.7 constant_dynamic-slice_fusion.1
  3.4 1.5 collective-permute-start.1
  5.7 1.3 reshape.237.refs_0_
  6.9 0.7 convert_bitcast_fusion.refs_4_
  7.6 0.7 convert_element_type.128.refs_3_
  8.4 0.6 convert_bitcast_fusion.1.refs_2_
  9.0 0.7 fusion.24.refs_1_
  9.7 129.1 %gather_weights.1 = (bf16[2,577,512]{2,1,0:T(8,128)(2,1)}, bf16[2,4,2,2,64,1664]{5,4,3,2,1,0:T(8,128)(2,1)}, bf16[2,4,2,2,64,512]{5,4,3,2,1,0:T(8,128)(2,1)}, bf...) custom-call(bf16[2,577,512]{2,1,0:T(8,128)(2,1)} %reshape.237.refs_0_, ...), custom_call_target="tpu_custom_call" | custom-call | tf_op jit(solution)/shard_map/gather_weights/pallas_call | solution.py:592
  138.9 1.1 slice.225
  140.0 1.3 slice_bitcast_fusion.19
  142.6 4.2 fusion
  146.8 4.2 fusion.1
  151.1 2.1 pad_maximum_fusion.projected_ref
  153.2 16.3 %attention_forward.1 = bf16[2,577,512]{2,1,0:T(8,128)(2,1)} custom-call(bf16[2,577,1536]{2,1,0:T(8,128)(2,1)} %pad_maximum_fusion.projected_ref), custom_call_target="tpu_custom_call" | custom-call | tf_op jit(solution)/shard_map/attention_forward/pallas_call | solution.py:373
  169.5 2.7 fusion.34
  172.5 6.1 %fusion.32 = (bf16[1,4,2,2,64,2048]{5,4,3,2,1,0:T(8,128)(2,1)}, bf16[1,4,2,2,64,2048]{5,4,3,2,1,0:T(8,128)(2,1)}) fusion(bf16[2,4,2,2,64,2048]{5,4,3,2,1,0:T(8,128)(2,1)} %get-tuple-element.27), kind=kLoop, calls=%fused_computation.122 | loop fusion | bytes 16777216 | tf_op jit(solution)/shard_map/slice | solution.py:926
  178.6 6.2 %fusion.33 = (bf16[1,4,2,2,64,2048]{5,4,3,2,1,0:T(8,128)(2,1)}, bf16[1,4,2,2,64,2048]{5,4,3,2,1,0:T(8,128)(2,1)}) fusion(bf16[2,4,2,2,64,2048]{5,4,3,2,1,0:T(8,128)(2,1)} %get-tuple-element.28), kind=kLoop, calls=%fused_computation.123 | loop fusion | bytes 16777216 | tf_op jit(solution)/shard_map/slice | solution.py:928
  184.9 0.8 fusion.22
  186.5 2.4 fusion.30
  189.4 2.7 fusion.41
  192.3 5.3 %multiply_convert_fusion.3 = (bf16[577,2048]{1,0:T(8,128)(2,1)S(1)}, f32[577,2048]{1,0:T(8,128)}) fusion(f32[2048]{0:T(1024)S(1)} %bitcast.189, bf16[577,1024]{1,0:T(8,128)(2,1)S(1)} %add_convert_fusion.3, bf16[1024,2048]{1,0:T(8,128)(2,1)S(1)} %bitcast.153), kind=kOutput, calls=%fused_computation.4 | convolution fusion | flops 2428385280 | bytes 12474368 | tf_op jit(solution)/shard_map/dot_general | solution.py:810
  197.7 2.7 fusion.40
  200.8 4.0 add_convert_fusion.2
  204.7 2.4 constant_dynamic-slice_fusion.3
  207.1 1.5 collective-permute-start
  208.6 8.4 %fusion.39 = (bf16[2048]{0:T(1024)(128)(2,1)S(1)}, bf16[577,2048]{1,0:T(8,128)(2,1)S(1)}) fusion(f32[577,2048]{1,0:T(8,128)} %get-tuple-element.88, f32[2048]{0:T(1024)S(1)} %bitcast.190, bf16[1024,2048]{1,0:T(8,128)(2,1)} %bitcast.157, bf16[577,512]{1,0:T(8,128)(2,1)} %collective-permute-done.1, bf16[577,512]{1,0:T(8,128)(2,1)} %get-tuple-element.60, ...), kind=kOutput, calls=%fused_computation.129 | convolution fusion | flops 2439609344 | bytes 12478465 | tf_op jit(solution)/shard_map/dot_general | solution.py:810
  217.0 2.7 fusion.42
  220.2 1.4 copy-done.47
  221.6 5.5 %fusion.38 = (bf16[2048]{0:T(1024)(128)(2,1)S(1)}, bf16[577,2048]{1,0:T(8,128)(2,1)S(1)}) fusion(f32[577,2048]{1,0:T(8,128)S(1)} %copy-done.47, f32[2048]{0:T(1024)S(1)} %bitcast.187, bf16[1024,2048]{1,0:T(8,128)(2,1)S(1)} %bitcast.156, bf16[577,512]{1,0:T(8,128)(2,1)} %collective-permute-done.1, bf16[577,512]{1,0:T(8,128)(2,1)S(1)} %copy-done.5, pred[]{:T(512)S(6)} %eq.4), kind=kOutput, calls=%fused_computation.128 | convolution fusion | flops 2439609344 | bytes 12478465 | tf_op jit(solution)/shard_map/dot_general | solution.py:810
  227.2 3.3 multiply_reduce_fusion
  230.5 3.2 fusion.31
  233.9 1.0 copy-done.15
  234.9 0.8 fusion.20
  236.0 0.6 copy-done.30
  236.6 0.8 fusion.21
  237.4 1.2 pad_maximum_fusion.4.upstream_ref
  238.6 28.2 %attention_back.1 = bf16[2,577,1536]{2,1,0:T(8,128)(2,1)} custom-call(bf16[2,577,1536]{2,1,0:T(8,128)(2,1)} %pad_maximum_fusion.projected_ref, bf16[2,577,512]{2,1,0:T(8,128)(2,1)} %pad_maximum_fusion.4.upstream_ref), custom_call_target="tpu_custom_call" | custom-call | tf_op jit(solution)/shard_map/attention_back/pallas_call | solution.py:386
  266.8 4.6 fusion.2
  271.4 4.8 %convolution_convert_fusion = bf16[1024,1536]{1,0:T(8,128)(2,1)} fusion(bf16[2,577,1536]{2,1,0:T(8,128)(2,1)S(1)} %copy-done, f32[1024]{0:T(1024)S(1)} %add.151, f32[1024]{0:T(1024)S(1)} %mul.160, f32[577]{0:T(1024)S(1)} %get-tuple-element.85, f32[577]{0:T(1024)S(1)} %get-tuple-element.84, bf16[577,512]{1,0:T(8,128)(2,1)S(1)} %copy-done.3, ...), kind=kOutput, calls=%fused_computation.10 | convolution fusion | flops 1821975552 | bytes 6152192 | tf_op jit(solution)/shard_map/dot_general | solution.py:810
  276.2 4.5 convolution_convert_fusion.1
  280.8 2.0 convolution_convert_fusion.6
  282.9 5.1 %convolution_convert_fusion.2 = bf16[1024,2048]{1,0:T(8,128)(2,1)} fusion(bf16[577,1024]{1,0:T(8,128)(2,1)S(1)} %copy-done.27, bf16[577,2048]{1,0:T(8,128)(2,1)S(1)} %copy-done.53), kind=kOutput, calls=%fused_computation.12 | convolution fusion | flops 2422210560 | bytes 7739392 | tf_op jit(solution)/shard_map/dot_general | solution.py:810
  288.0 5.1 %convolution_convert_fusion.3 = bf16[1024,2048]{1,0:T(8,128)(2,1)} fusion(bf16[577,1024]{1,0:T(8,128)(2,1)S(1)} %copy-done.27, bf16[577,2048]{1,0:T(8,128)(2,1)S(1)} %copy-done.51), kind=kOutput, calls=%fused_computation.13 | convolution fusion | flops 2422210560 | bytes 7739392 | tf_op jit(solution)/shard_map/dot_general | solution.py:810
  293.1 5.8 %fusion.12 = (f32[577]{0:T(1024)S(1)}, bf16[1024]{0:T(1024)(128)(2,1)S(1)}, f32[577]{0:T(1024)S(1)}, bf16[1024]{0:T(1024)(128)(2,1)S(1)}, f32[577,1024]{1,0:T(8,128)}) fusion(f32[1024]{0:T(1024)S(1)} %mul.160, f32[577]{0:T(1024)S(1)} %get-tuple-element.85, f32[577]{0:T(1024)S(1)} %get-tuple-element.84, bf16[577,512]{1,0:T(8,128)(2,1)S(1)} %copy-done.3, ...), kind=kOutput, calls=%fused_computation.35 | convolution fusion | flops 1823353600 | bytes 10912264 | tf_op jit(solution)/shard_map/dot_general | solution.py:810
  299.1 2.6 reduce.3
  302.1 2.0 fusion.25
  304.6 4.1 pad_maximum_fusion.2.refs_7_
  308.7 2.1 pad_maximum_fusion.1.refs_6_
  310.8 1.0 copy-done.21
  311.8 2.1 fusion.16.refs_8_
  314.0 8.4 %convolution_convert_fusion.4 = bf16[1024,2048]{1,0:T(8,128)(2,1)} fusion(f32[577,2048]{1,0:T(8,128)} %copy-done.46, f32[2048]{0:T(1024)S(1)} %bitcast.188, bf16[577,512]{1,0:T(8,128)(2,1)} %collective-permute-done.1, bf16[577,512]{1,0:T(8,128)(2,1)S(1)} %copy-done.6, pred[]{:T(512)S(6)} %eq.4), kind=kOutput, calls=%fused_computation.14 | convolution fusion | flops 2435800064 | bytes 10110977 | tf_op jit(solution)/shard_map/dot_general | solution.py:810
  322.4 6.5 %convolution_convert_fusion.5 = bf16[1024,2048]{1,0:T(8,128)(2,1)} fusion(bf16[577,2048]{1,0:T(8,128)(2,1)S(1)} %copy-done.49, bf16[577,512]{1,0:T(8,128)(2,1)} %collective-permute-done.1, bf16[577,512]{1,0:T(8,128)(2,1)S(1)} %copy-done.6, pred[]{:T(512)S(6)} %eq.4), kind=kOutput, calls=%fused_computation.15 | convolution fusion | flops 2427528192 | bytes 7739393 | tf_op jit(solution)/shard_map/dot_general | solution.py:810
  328.9 2.0 convolution_convert_fusion.7
  330.9 133.5 %scatter_grads.1 = (f32[64,2048]{1,0:T(8,128)}, f32[64,2048]{1,0:T(8,128)}, f32[64,512]{1,0:T(8,128)}, f32[64,1664]{1,0:T(8,128)}, bf16[2,577,512]{2,1,0:T(8,128)(2,1)}) custom-call(bf16[4,2,2,64,2048]{4,3,2,1,0:T(8,128)(2,1)} %bitcast.160, bf16[4,2,2,64,2048]{4,3,2,1,0:T(8,128)(2,1)} %bitcast.159, bf16[4,2,2,64,2048]{4,3,2,1,0:T(8,128)(2,1)} %bitcast.150, ...), custom_call_target="tpu_custom_call" | custom-call | tf_op jit(solution)/shard_map/scatter_grads/pallas_call | solution.py:765
  464.4 1.0 slice.217
  465.4 0.7 slice.214
  466.1 3.0 reshape.253
  469.5 0.9 reshape.252
  470.5 0.6 slice.218
  471.0 1.2 slice_bitcast_fusion.25
  472.8 2.7 maximum_select_fusion.1
  475.5 0.7 copy.61
  476.1 0.8 copy.62
  476.9 0.8 copy.63
  (181 shorter events, 7.2 us)
Async XLA Ops:
  0.6 4.3 copy-start.44
  0.7 4.3 copy-start.39
  0.7 4.3 copy-start.38
  0.7 4.3 copy-start.41
  0.7 4.3 copy-start.40
  0.7 4.3 copy-start.43
  0.7 4.3 copy-start.42
  0.7 4.4 copy-start.45
  0.7 4.4 copy-start.35
  0.7 4.9 %copy-start.28 = (bf16[1154,512]{1,0:T(8,128)(2,1)S(1)}, bf16[1154,512]{1,0:T(8,128)(2,1)}, u32[]{:S(2)}) copy-start(bf16[1154,512]{1,0:T(8,128)(2,1)} %param.14) | copy-start | bytes 3545092
  3.4 3.5 copy-start.31
  3.4 205.1 %collective-permute-start.1 = (bf16[577,512]{1,0:T(8,128)(2,1)}, bf16[577,512]{1,0:T(8,128)(2,1)}, u32[]{:S(2)}, u32[]{:S(2)}) collective-permute-start(bf16[577,512]{1,0:T(8,128)(2,1)} %get-tuple-element.61), channel_id=1, source_target_pairs={{0,1},{1,0},{2,3},{3,2},{4,5},{5,4},{6,7},{7,6},{8,9},{9,8},{10,11... | collective-permute-start | bytes 1772552 | tf_op jit(solution)/shard_map/ppermute | solution.py:792
  5.2 2.5 copy-start.32
  5.3 3.1 copy-start.36
  141.4 5.5 %copy-start.2 = (bf16[577,512]{1,0:T(8,128)(2,1)}, bf16[577,512]{1,0:T(8,128)(2,1)S(1)}, u32[]{:S(2)}) copy-start(bf16[577,512]{1,0:T(8,128)(2,1)S(1)} %get-tuple-element.59) | copy-start | bytes 1772548
  172.2 12.7 %copy-start.14 = (bf16[1,4,2,2,64,512]{5,4,3,2,1,0:T(8,128)(2,1)}, bf16[1,4,2,2,64,512]{5,4,3,2,1,0:T(8,128)(2,1)S(1)}, u32[]{:S(2)}) copy-start(bf16[1,4,2,2,64,512]{5,4,3,2,1,0:T(8,128)(2,1)S(1)} %get-tuple-element.55) | copy-start | bytes 3145732
  178.6 6.3 %copy-start.17 = (bf16[2,577,512]{2,1,0:T(8,128)(2,1)S(1)}, bf16[2,577,512]{2,1,0:T(8,128)(2,1)}, u32[]{:S(2)}) copy-start(bf16[2,577,512]{2,1,0:T(8,128)(2,1)} %attention_forward.1) | copy-start | bytes 3545092
  184.9 1.3 copy-start.18
  184.9 1.6 copy-start.29
  186.5 2.8 copy-start.7
  188.9 38.3 %copy-start.1 = (f32[577,1024]{1,0:T(8,128)}, f32[577,1024]{1,0:T(8,128)S(1)}, u32[]{:S(2)}) copy-start(f32[577,1024]{1,0:T(8,128)S(1)} %get-tuple-element.86) | copy-start | bytes 7090180
  189.4 2.7 copy-start.26
  189.4 3.0 copy-start.9
  192.1 8.3 %copy-start.46 = (f32[577,2048]{1,0:T(8,128)}, f32[577,2048]{1,0:T(8,128)S(1)}, u32[]{:S(2)}) copy-start(f32[577,2048]{1,0:T(8,128)S(1)} %fusion.41) | copy-start | bytes 14180356
  192.3 5.4 %copy-start.13 = (bf16[1,4,2,2,64,2048]{5,4,3,2,1,0:T(8,128)(2,1)S(1)}, bf16[1,4,2,2,64,2048]{5,4,3,2,1,0:T(8,128)(2,1)}, u32[]{:S(2)}) copy-start(bf16[1,4,2,2,64,2048]{5,4,3,2,1,0:T(8,128)(2,1)} %get-tuple-element.53) | copy-start | bytes 12582916
  197.7 2.7 copy-start.48
  197.7 3.1 copy-start.11
  207.1 265.7 %collective-permute-start = (bf16[577,512]{1,0:T(8,128)(2,1)}, bf16[577,512]{1,0:T(8,128)(2,1)}, u32[]{:S(2)}, u32[]{:S(2)}) collective-permute-start(bf16[577,512]{1,0:T(8,128)(2,1)} %get-tuple-element.57), channel_id=1, source_target_pairs={{0,1},{1,0},{2,3},{3,2},{4,5},{5,4},{6,7},{7,6},{8,9},{9,8},{10,11... | collective-permute-start | bytes 1772552 | tf_op jit(solution)/shard_map/ppermute | solution.py:803
  208.6 8.4 %copy-start.10 = (bf16[1,4,2,2,64,2048]{5,4,3,2,1,0:T(8,128)(2,1)S(1)}, bf16[1,4,2,2,64,2048]{5,4,3,2,1,0:T(8,128)(2,1)}, u32[]{:S(2)}) copy-start(bf16[1,4,2,2,64,2048]{5,4,3,2,1,0:T(8,128)(2,1)} %get-tuple-element.51) | copy-start | bytes 12582916
  217.0 2.7 copy-start.50
  217.0 2.7 copy-start.5
  217.0 3.2 copy-start.12
  217.0 4.6 copy-start.47
  221.6 5.6 %copy-start.8 = (bf16[1,4,2,2,64,2048]{5,4,3,2,1,0:T(8,128)(2,1)S(1)}, bf16[1,4,2,2,64,2048]{5,4,3,2,1,0:T(8,128)(2,1)}, u32[]{:S(2)}) copy-start(bf16[1,4,2,2,64,2048]{5,4,3,2,1,0:T(8,128)(2,1)} %get-tuple-element.50) | copy-start | bytes 12582916
  227.2 3.3 copy-start.52
  233.7 1.2 copy-start.15
  234.9 1.0 copy-start.23
  234.9 1.7 copy-start.30
  266.8 4.6 copy-start
  266.8 4.7 copy-start.3
  276.2 4.5 copy-start.19
  276.2 4.5 copy-start.24
  280.8 2.0 copy-start.27
  280.8 2.1 copy-start.53
  282.9 5.1 %copy-start.51 = (bf16[577,2048]{1,0:T(8,128)(2,1)S(1)}, bf16[577,2048]{1,0:T(8,128)(2,1)}, u32[]{:S(2)}) copy-start(bf16[577,2048]{1,0:T(8,128)(2,1)} %copy-done.50) | copy-start | bytes 7090180
  304.6 4.1 copy-start.16
  308.7 2.1 copy-start.4
  308.7 3.1 copy-start.21
  311.8 2.2 copy-start.6
  314.0 8.4 %copy-start.49 = (bf16[577,2048]{1,0:T(8,128)(2,1)S(1)}, bf16[577,2048]{1,0:T(8,128)(2,1)}, u32[]{:S(2)}) copy-start(bf16[577,2048]{1,0:T(8,128)(2,1)} %copy-done.48) | copy-start | bytes 7090180
  322.4 6.5 %copy-start.20 = (bf16[2,577,512]{2,1,0:T(8,128)(2,1)S(1)}, bf16[2,577,512]{2,1,0:T(8,128)(2,1)}, u32[]{:S(2)}) copy-start(bf16[2,577,512]{2,1,0:T(8,128)(2,1)} %attention_forward.1) | copy-start | bytes 3545092
  322.4 6.5 %copy-start.25 = (bf16[577,1024]{1,0:T(8,128)(2,1)S(1)}, bf16[577,1024]{1,0:T(8,128)(2,1)}, u32[]{:S(2)}) copy-start(bf16[577,1024]{1,0:T(8,128)(2,1)} %copy-done.23) | copy-start | bytes 3545092
  466.1 6.7 %copy-start.22 = (bf16[577,512]{1,0:T(8,128)(2,1)S(1)}, bf16[577,512]{1,0:T(8,128)(2,1)}, u32[]{:S(2)}) copy-start(bf16[577,512]{1,0:T(8,128)(2,1)} %get-tuple-element.56) | copy-start | bytes 1772548
  469.1 6.4 %copy-start.37 = (f32[64,512]{1,0:T(8,128)S(1)}, f32[64,512]{1,0:T(8,128)}, u32[]{:S(2)}) copy-start(f32[64,512]{1,0:T(8,128)} %get-tuple-element.31) | copy-start | bytes 393220
  469.3 6.8 %copy-start.34 = (f32[64,2048]{1,0:T(8,128)S(1)}, f32[64,2048]{1,0:T(8,128)}, u32[]{:S(2)}) copy-start(f32[64,2048]{1,0:T(8,128)} %get-tuple-element.125) | copy-start | bytes 1572868
  469.5 7.5 %copy-start.33 = (f32[64,2048]{1,0:T(8,128)S(1)}, f32[64,2048]{1,0:T(8,128)}, u32[]{:S(2)}) copy-start(f32[64,2048]{1,0:T(8,128)} %get-tuple-element.33) | copy-start | bytes 1572868

commit v5 on v4

--- a/solution.py
+++ b/solution.py
@@ -401,6 +401,7 @@
 IN_VMEM = pl.BlockSpec(memory_space=pltpu.VMEM)
 SIDES = 2
 BUFFERS = 6
+SLOTS = 4
 CHUNK = 4
 AHEAD = 12
 SPACING = 2
@@ -448,7 +449,7 @@
         self.count += 1
         return self.count - 1
 
-    def send(self, slot, source, target, device):
+    def send(self, slot, source, target, device, keep=True):
         copy = pltpu.make_async_remote_copy(
             src_ref=source,
             dst_ref=target,
@@ -458,7 +459,9 @@
             device_id_type=MESH,
         )
         copy.start()
-        self.sent.append(copy)
+        if keep:
+            self.sent.append(copy)
+        return copy
 
     def arrived(self, slot, target, device):
         pltpu.make_async_remote_copy(
@@ -475,14 +478,14 @@
             copy.wait_send()
 
 
-def run_waves(chains):
+def run_waves(chains, ahead):
     stages = len(chains[0])
     count = len(chains)
-    for at in range(min(AHEAD, count)):
+    for at in range(min(ahead, count)):
         chains[at][0]()
     for wave in range(1, count + SPACING * (stages - 1)):
-        if wave + AHEAD - 1 < count:
-            chains[wave + AHEAD - 1][0]()
+        if wave + ahead - 1 < count:
+            chains[wave + ahead - 1][0]()
         for stage in range(stages - 1, 0, -1):
             at = wave - 1 - SPACING * (stage - 1)
             if 0 <= at < count:
@@ -579,7 +582,7 @@
     for at in range(pieces_count):
         slots.append(copies.slot())
         copies.send(slots[at], pieces[at].at[1 - x], images[at].at[x], x_peer)
-    run_waves(chains)
+    run_waves(chains, AHEAD)
     for at in range(pieces_count):
         copies.arrived(slots[at], images[at].at[1 - x], x_peer)
         kept[at].wait()
@@ -615,9 +618,74 @@
         target(at)[...] = total.astype(jnp.bfloat16)
 
 
-def scatter_chain(copies, where, depth, grad, total, buffers, load_sems, start, width):
+class Loaded:
+    def __init__(self, copies, core, grad, own, sems, start, width):
+        self.copies, self.core, self.grad, self.own_ref = copies, core, grad, own
+        self.every = pl.ds(start, width)
+        self.loads = [
+            pltpu.make_async_copy(
+                grad[side].at[:, :, core, :, self.every],
+                own.at[side, :, :, :, self.every],
+                sems[side],
+            )
+            for side in range(SIDES)
+        ]
+
+    def prepare(self):
+        for load in self.loads:
+            load.start()
+
+    def give(self, slot, side, target, partner):
+        source = self.grad[side].at[:, :, 1 - self.core, :, self.every]
+        self.copies.send(slot, source, target, partner)
+
+    def ready(self):
+        for load in self.loads:
+            load.wait()
+
+    def own(self, side, z, y):
+        return self.own_ref.at[side, z, y, :, self.every]
+
+
+class Computed:
+    def __init__(self, copies, core, left, right, ring, flying, order, start, width):
+        self.copies, self.core, self.left, self.right = copies, core, left, right
+        self.ring, self.flying, self.slot = ring, flying, order % SLOTS
+        self.every = pl.ds(start, width)
+
+    def prepare(self):
+        for copy in self.flying.pop(self.slot, ()):
+            copy.wait_send()
+        depth, rows, width = self.ring.shape[3], self.ring.shape[5], self.ring.shape[6]
+        span = depth // 2
+        block = span * 2 * rows
+
+        @pl.loop(0, SIDES * 2 * 2)
+        def _(at):
+            who, side, half = lax.div(at, 4), lax.rem(lax.div(at, 2), 2), lax.rem(at, 2)
+            left = self.left[
+                lax.rem(self.core + who, 2), pl.ds(pl.multiple_of(half * block, block), block), :
+            ]
+            right = self.right[side, :, self.every]
+            result = jnp.dot(left, right, preferred_element_type=jnp.float32)
+            self.ring[self.slot, who, side, pl.ds(half * span, span)] = result.astype(
+                jnp.bfloat16
+            ).reshape(span, 2, rows, width)
+
+    def give(self, slot, side, target, partner):
+        copy = self.copies.send(slot, self.ring.at[self.slot, 1, side], target, partner, False)
+        self.flying.setdefault(self.slot, []).append(copy)
+
+    def ready(self):
+        pass
+
+    def own(self, side, z, y):
+        return self.ring.at[self.slot, 0, side, z, y]
+
+
+def scatter_chain(copies, where, depth, source, total, buffers, start, width):
     x, z, y, core = where
-    own, halves, ax_in, by_in, along, along_in = buffers
+    halves, ax_in, by_in, along, along_in = buffers
     first = split_width(width)
     every = pl.ds(start, width)
     a, b = pl.ds(start, first), pl.ds(start + first, width - first)
@@ -629,63 +697,50 @@
     z_peers = [device_of(x, at, y, core) for at in z_to]
     pair = [copies.slot() for _ in range(SIDES)]
     ax, ay, bx, by = [copies.slot() for _ in range(4)]
+    ca, cb = pl.ds(start // 2, first), pl.ds(start // 2, width - first)
     hops = [copies.slot() for _ in steps]
-    load = [
-        pltpu.make_async_copy(
-            grad[side].at[:, :, core, :, every],
-            own.at[side, :, :, :, every],
-            load_sems[side],
+    def begin():
+        source.prepare()
+        for side in range(SIDES):
+            source.give(pair[side], side, halves.at[side, :, :, :, every], partner)
+
+    def second():
+        source.ready()
+        for side in range(SIDES):
+            copies.arrived(pair[side], halves.at[side, :, :, :, every], partner)
+
+        def block_at(at):
+            return lax.div(at, depth * 2), lax.rem(lax.div(at, 2), depth), lax.rem(at, 2)
+
+        add_blocks(
+            SIDES * depth * 2,
+            lambda at: halves.at[block_at(at) + (slice(None), every)],
+            lambda at: source.own(*block_at(at)),
         )
-        for side in range(SIDES)
-    ]
-
-    def begin():
-        for side in range(SIDES):
-            load[side].start()
-            copies.send(
-                pair[side],
-                grad[side].at[:, :, 1 - core, :, every],
-                halves.at[side, :, :, :, every],
-                partner,
-            )
-
-    def second():
-        for side in range(SIDES):
-            load[side].wait()
-            copies.arrived(pair[side], halves.at[side, :, :, :, every], partner)
-
-        def at_block(ref, at):
-            return ref.at[
-                lax.div(at, depth * 2), lax.rem(lax.div(at, 2), depth), lax.rem(at, 2), :, every
-            ]
-
-        add_blocks(
-            SIDES * depth * 2, lambda at: at_block(halves, at), lambda at: at_block(own, at)
-        )
-        copies.send(ax, halves.at[1 - x, :, :, :, a], ax_in.at[:, :, :, a], x_peer)
-        copies.send(by, halves.at[:, :, 1 - y, :, b], by_in.at[:, :, :, b], y_peer)
+        copies.send(ax, halves.at[1 - x, :, :, :, a], ax_in.at[:, :, :, ca], x_peer)
+        copies.send(by, halves.at[:, :, 1 - y, :, b], by_in.at[:, :, :, cb], y_peer)
 
     def third():
-        copies.arrived(ax, ax_in.at[:, :, :, a], x_peer)
+        copies.arrived(ax, ax_in.at[:, :, :, ca], x_peer)
         add_blocks(
             depth * 2,
-            lambda at: ax_in.at[lax.div(at, 2), lax.rem(at, 2), :, a],
+            lambda at: ax_in.at[lax.div(at, 2), lax.rem(at, 2), :, ca],
             lambda at: halves.at[x, lax.div(at, 2), lax.rem(at, 2), :, a],
         )
-        copies.send(ay, ax_in.at[:, 1 - y, :, a], along.at[:, :, a], y_peer)
-        copies.arrived(by, by_in.at[:, :, :, b], y_peer)
+        copies.send(ay, ax_in.at[:, 1 - y, :, ca], along.at[:, :, a], y_peer)
+        copies.arrived(by, by_in.at[:, :, :, cb], y_peer)
         add_blocks(
             SIDES * depth,
-            lambda at: by_in.at[lax.div(at, depth), lax.rem(at, depth), :, b],
+            lambda at: by_in.at[lax.div(at, depth), lax.rem(at, depth), :, cb],
             lambda at: halves.at[lax.div(at, depth), lax.rem(at, depth), y, :, b],
         )
-        copies.send(bx, by_in.at[1 - x, :, :, b], along.at[:, :, b], x_peer)
+        copies.send(bx, by_in.at[1 - x, :, :, cb], along.at[:, :, b], x_peer)
 
     def fourth():
         copies.arrived(ay, along.at[:, :, a], y_peer)
-        add_blocks(depth, lambda at: along.at[at, :, a], lambda at: ax_in.at[at, y, :, a])
+        add_blocks(depth, lambda at: along.at[at, :, a], lambda at: ax_in.at[at, y, :, ca])
         copies.arrived(bx, along.at[:, :, b], x_peer)
-        add_blocks(depth, lambda at: along.at[at, :, b], lambda at: by_in.at[x, at, :, b])
+        add_blocks(depth, lambda at: along.at[at, :, b], lambda at: by_in.at[x, at, :, cb])
         for k in range(depth - 1):
             copies.send(
                 hops[k], along.at[z_to[k], :, every], along_in.at[k, :, every], z_peers[k]
@@ -702,13 +757,20 @@
     return begin, second, third, fourth, last
 
 
-def scatter_kernel(depth, count, wholes_count, *refs):
-    grads = [refs[SIDES * at : SIDES * at + SIDES] for at in range(count)]
-    refs = refs[SIDES * count :]
-    wholes, refs = refs[:wholes_count], refs[wholes_count:]
-    totals, pieces = refs[:count], refs[count : count + wholes_count]
-    refs = refs[count + wholes_count :]
-    send_sems, recv_sems, own_sems = refs[-3:]
+def scatter_kernel(depth, count, pairs_count, wholes_count, *refs):
+    def take(number):
+        nonlocal refs
+        taken, refs = refs[:number], refs[number:]
+        return taken
+
+    grads = [take(SIDES) for _ in range(count)]
+    pairs = [take(2) for _ in range(pairs_count)]
+    wholes = take(wholes_count)
+    totals = take(count + pairs_count)
+    pieces = take(wholes_count)
+    owns = take(count)
+    buffers = [take(BUFFERS - 1) for _ in totals]
+    ring, send_sems, recv_sems, own_sems = refs
     where = place()
     x, z, y, core = where
     copies = Copies(send_sems, recv_sems)
@@ -720,53 +782,64 @@
         width = pieces[at].shape[2]
         mine = pl.ds(pl.multiple_of(x * width, width), width)
         theirs = pl.ds(pl.multiple_of((1 - x) * width, width), width)
-        copy = pltpu.make_async_copy(
-            wholes[at].at[:, mine], pieces[at].at[x], own_sems.at[at]
-        )
+        copy = pltpu.make_async_copy(wholes[at].at[:, mine], pieces[at].at[x], own_sems.at[at])
         copy.start()
         kept.append(copy)
         copies.send(slots[at], wholes[at].at[:, theirs], pieces[at].at[x], x_peer)
-    chains = []
+    chains, flying, order = [], {}, 0
     loads = iter(range(own_sems.shape[0] - wholes_count))
-    for at in range(count):
-        buffers = refs[BUFFERS * at : BUFFERS * at + BUFFERS]
-        for start, width in chunks_of(totals[at].shape[1]):
-            load_sems = [own_sems.at[wholes_count + next(loads)] for _ in range(SIDES)]
+    for at, total in enumerate(totals):
+        for start, width in chunks_of(total.shape[1]):
+            if at < count:
+                sems = [own_sems.at[wholes_count + next(loads)] for _ in range(SIDES)]
+                source = Loaded(copies, core, grads[at], owns[at], sems, start, width)
+            else:
+                source = Computed(
+                    copies, core, *pairs[at - count], ring, flying, order, start, width
+                )
+                order += 1
             chains.append(
-                scatter_chain(
-                    copies, where, depth, grads[at], totals[at], buffers, load_sems, start, width
-                )
+                scatter_chain(copies, where, depth, source, total, buffers[at], start, width)
             )
-    run_waves(chains)
+    run_waves(chains, SLOTS - 1)
     for at in range(wholes_count):
         copies.arrived(slots[at], pieces[at].at[1 - x], x_peer)
         kept[at].wait()
+    for flight in flying.values():
+        for copy in flight:
+            copy.wait_send()
     copies.finish()
 
 
 def scatter_buffers(depth, rows, width):
+    part = -(-width // (2 * GROUP)) * GROUP
     shapes = [
         (SIDES, depth, 2, rows, width),
-        (SIDES, depth, 2, rows, width),
-        (depth, 2, rows, width),
-        (SIDES, depth, rows, width),
+        (depth, 2, rows, part),
+        (SIDES, depth, rows, part),
         (depth, rows, width),
         (depth - 1, rows, width),
     ]
     return [pltpu.VMEM(shape, jnp.bfloat16) for shape in shapes]
 
 
-def scatter_grads(grads, wholes, depth):
-    chunks = sum(len(chunks_of(grad[0].shape[4])) for grad in grads)
+def scatter_grads(grads, pairs, wholes, depth):
+    rows = grads[0][0].shape[3]
+    widths = [grad[0].shape[4] for grad in grads] + [pair[1].shape[2] for pair in pairs]
+    loaded = sum(len(chunks_of(width)) for width in widths[: len(grads)])
+    chunks = sum(len(chunks_of(width)) for width in widths)
     copies = (depth + 5) * chunks + len(wholes)
-    scratch = []
-    for grad in grads:
-        scratch += scatter_buffers(depth, grad[0].shape[3], grad[0].shape[4])
+    scratch = [
+        pltpu.VMEM((SIDES, depth, 2, rows, width), jnp.bfloat16) for width in widths[: len(grads)]
+    ]
+    for width in widths:
+        scratch += scatter_buffers(depth, rows, width)
+    scratch.append(pltpu.VMEM((SLOTS, 2, SIDES, depth, 2, rows, CHUNK * GROUP), jnp.bfloat16))
     return pl.pallas_call(
-        functools.partial(scatter_kernel, depth, len(grads), len(wholes)),
-        in_specs=[ANY] * SIDES * len(grads) + [IN_VMEM] * len(wholes),
-        out_specs=[IN_VMEM] * len(grads) + [ANY] * len(wholes),
-        out_shape=[jax.ShapeDtypeStruct(grad[0].shape[3:], jnp.float32) for grad in grads]
+        functools.partial(scatter_kernel, depth, len(grads), len(pairs), len(wholes)),
+        in_specs=[ANY] * SIDES * len(grads) + [IN_VMEM] * (2 * len(pairs) + len(wholes)),
+        out_specs=[IN_VMEM] * len(widths) + [ANY] * len(wholes),
+        out_shape=[jax.ShapeDtypeStruct((rows, width), jnp.float32) for width in widths]
         + [
             jax.ShapeDtypeStruct((SIDES, whole.shape[0], whole.shape[1] // SIDES), whole.dtype)
             for whole in wholes
@@ -775,13 +848,17 @@
         + [
             pltpu.SemaphoreType.DMA((copies,)),
             pltpu.SemaphoreType.DMA((copies,)),
-            pltpu.SemaphoreType.DMA((SIDES * chunks + len(wholes),)),
+            pltpu.SemaphoreType.DMA((SIDES * loaded + len(wholes),)),
         ],
         compiler_params=pltpu.CompilerParams(
-            collective_id=2, has_side_effects=True, vmem_limit_bytes=60 * 2**20
+            collective_id=2, has_side_effects=True, vmem_limit_bytes=62 * 2**20
         ),
         name="scatter_grads",
-    )(*[half for grad in grads for half in grad], *wholes)
+    )(
+        *[half for grad in grads for half in grad],
+        *[part for pair in pairs for part in pair],
+        *wholes,
+    )
 
 
 def to_image(piece):
@@ -817,6 +894,11 @@
     first_mean = jnp.mean(scaled_grad, -1, keepdims=True)
     second_mean = jnp.mean(scaled_grad * scaled, -1, keepdims=True)
     return inverse * (scaled_grad - first_mean - scaled * second_mean)
+
+
+def core_order(left, rows, block_rows):
+    turned = left.T.reshape(rows // 2, 2, block_rows, -1).transpose(1, 0, 2, 3)
+    return turned.reshape(2, rows // 2 * block_rows, -1)
 
 
 def group_order(block):
@@ -929,12 +1011,10 @@
     layer_output = from_image((hidden + reduced + reduce_shift).astype(low))
 
     upstream = upstream_low.astype(jnp.float32)
-    reducer_grad = [product(upstream_low, activated[h], 0, 0).astype(low) for h in range(cols)]
     expanded_grad = [
         (product(upstream_low, reducer[h], 1, 0) * gelu_slope(expanded[h])).astype(low)
         for h in range(cols)
     ]
-    expander_grad = [product(second_low, expanded_grad[h], 0, 0).astype(low) for h in range(cols)]
     expand_shift_grad = [jnp.sum(part.astype(jnp.float32), 0) for part in expanded_grad]
     second_grad = sum(product(expanded_grad[h], expander[h], 1, 1) for h in range(cols))
     hidden_grad = upstream + norm_back(
@@ -975,10 +1055,14 @@
     mixed_grad = [jnp.concatenate([mixer_grad[h], vector_grads[h]], 1) for h in range(cols)]
     grads = [
         [part.reshape(depth, 2, 2, block_rows, -1) for part in halves]
-        for halves in (reducer_grad, expander_grad, merger_grad, mixed_grad)
+        for halves in (merger_grad, mixed_grad)
     ]
-    reduce_total, expand_total, merge_total, mixed_total, tokens_gradient = (
-        scatter_grads(grads, [input_grad.astype(low)], depth)
+    pairs = [
+        (core_order(left, rows, block_rows), jnp.stack(right))
+        for left, right in ((upstream_low, activated), (second_low, expanded_grad))
+    ]
+    merge_total, mixed_total, reduce_total, expand_total, tokens_gradient = scatter_grads(
+        grads, pairs, [input_grad.astype(low)], depth
     )
     tokens_gradient = tokens_gradient.reshape(tokens.shape).astype(jnp.float32)
     mixer_total = part_order(mixed_total[:, :mixer_width])

time: 487 us -> 486 us (level)
  matrix products: 96.5 us -> 76.2 us
  other arithmetic: 26.2 us -> 36 us
  local copies, waits for them, and re-layouts: 43.4 us -> 49.5 us
    dot_general x24 -> x20, matrix products: 96.5 us -> 76.2 us  [product(): lax.dot_general(left, right, (((left_at,), (right_at,)), ((), ())), prefe...]
    another operation x2 -> x4, other arithmetic: 0.01 us -> 9.91 us  [the longest x2 9.9 us: image_shards(): jnp.stack(right)]
    transpose x0 -> x4, local copies, waits for them, and re-layouts: none -> 7.16 us  [core_order(): turned = left.T.reshape(rows // 2, 2, block_rows, -1).transpose(1, 0, 2, 3)]
  transfers between devices with their start and end apart: 2 -> 2, of which waited for: 0 -> 0; matrix products, arithmetic and copies ran while one was open for 32% -> 31% of each run, Pallas kernels for 64% -> 65%
where the time goes in v5:
time: 486 us; the launch traced here: 477 us
  Pallas kernels  311 us (64%)
  matrix products  76.2 us (16%)
  local copies, waits for them, and re-layouts  49.5 us (10%)
  other arithmetic  36 us (7%)
    pallas_call x1, Pallas kernels, scatter_grads(): pl.pallas_call(functools.partial(scatter_kernel, depth, len(grads), len(p...  137 us
    pallas_call x1, Pallas kernels, gather_weights(): pl.pallas_call(functools.partial(gather_kernel, depth, len(pieces)), in_s...  129 us
    dot_general x20, matrix products, product(): lax.dot_general(left, right, (((left_at,), (right_at,)), ((), ())), prefe...  76.2 us
    pallas_call x1, Pallas kernels, attention_back(): pl.pallas_call(attention_back_kernel, grid=(halves, groups), in_specs=[pl...  28.1 us
    pallas_call x1, Pallas kernels, attention_forward(): pl.pallas_call(attention_forward_kernel, grid=(halves, groups), in_specs=...  16.6 us
    another operation x2, other arithmetic, image_shards(): jnp.stack(right)  9.9 us
  transfers between devices with their start and end apart: 2, of which 0 were waited for; matrix products, arithmetic and copies ran while one was open for 31% of the time, Pallas kernels for 65%

profile of v5, /device:TPU:28, one launch (start us, length us, event | category | flops | bytes accessed | tf_op | source)
XLA Modules:
  0.0 477.4 jit_solution(2114102199363513689)
XLA Ops:
  0.8 2.7 constant_dynamic-slice_fusion.1
  3.4 1.5 collective-permute-start.1
  5.6 1.3 reshape.237.refs_0_
  6.9 0.7 convert_bitcast_fusion.refs_4_
  7.6 0.7 convert_element_type.116.refs_3_
  9.0 0.7 fusion.24.refs_1_
  9.7 129.1 %gather_weights.1 = (bf16[2,577,512]{2,1,0:T(8,128)(2,1)}, bf16[2,4,2,2,64,1664]{5,4,3,2,1,0:T(8,128)(2,1)}, bf16[2,4,2,2,64,512]{5,4,3,2,1,0:T(8,128)(2,1)}, bf...) custom-call(bf16[2,577,512]{2,1,0:T(8,128)(2,1)} %reshape.237.refs_0_, ...), custom_call_target="tpu_custom_call" | custom-call | tf_op jit(solution)/shard_map/gather_weights/pallas_call | solution.py:595
  138.9 1.1 slice.225
  140.0 1.3 slice_bitcast_fusion.19
  142.6 4.2 fusion
  146.8 4.2 fusion.1
  151.1 2.1 pad_maximum_fusion.2.projected_ref
  153.1 16.6 %attention_forward.1 = bf16[2,577,512]{2,1,0:T(8,128)(2,1)} custom-call(bf16[2,577,1536]{2,1,0:T(8,128)(2,1)} %pad_maximum_fusion.2.projected_ref), custom_call_target="tpu_custom_call" | custom-call | tf_op jit(solution)/shard_map/attention_forward/pallas_call | solution.py:373
  169.8 2.7 fusion.35
  172.7 6.1 %fusion.34 = (bf16[1,4,2,2,64,2048]{5,4,3,2,1,0:T(8,128)(2,1)}, bf16[1,4,2,2,64,2048]{5,4,3,2,1,0:T(8,128)(2,1)}) fusion(bf16[2,4,2,2,64,2048]{5,4,3,2,1,0:T(8,128)(2,1)} %get-tuple-element.27), kind=kLoop, calls=%fused_computation.122 | loop fusion | bytes 16777216 | tf_op jit(solution)/shard_map/slice | solution.py:1008
  178.9 6.2 %fusion.33 = (bf16[1,4,2,2,64,2048]{5,4,3,2,1,0:T(8,128)(2,1)}, bf16[1,4,2,2,64,2048]{5,4,3,2,1,0:T(8,128)(2,1)}) fusion(bf16[2,4,2,2,64,2048]{5,4,3,2,1,0:T(8,128)(2,1)} %get-tuple-element.28), kind=kLoop, calls=%fused_computation.121 | loop fusion | bytes 16777216 | tf_op jit(solution)/shard_map/slice | solution.py:1010
  185.2 0.8 fusion.22
  186.8 2.3 fusion.31
  189.1 5.9 %multiply_convert_fusion.2 = (bf16[577,2048]{1,0:T(8,128)(2,1)}, f32[577,2048]{1,0:T(8,128)}) fusion(f32[2048]{0:T(1024)S(1)} %bitcast.198, bf16[1024,2048]{1,0:T(8,128)(2,1)S(1)} %bitcast.161, f32[577,1024]{1,0:T(8,128)S(1)} %get-tuple-element.88, f32[1024]{0:T(1024)S(1)} %add.166, f32[1024]{0:T(1024)S(1)} %mul.167, f32[577]{0:T(1024)S(1)} %get-tuple-element.85, ...), kind=kOutput, calls=%fused_computation.4 | convolution fusion | flops 2431339520 | bytes 13668872 | tf_op jit(solution)/shard_map/dot_general | solution.py:887
  195.0 5.3 %multiply_convert_fusion.3 = (bf16[577,2048]{1,0:T(8,128)(2,1)S(1)}, f32[577,2048]{1,0:T(8,128)}) fusion(f32[2048]{0:T(1024)S(1)} %bitcast.200, bf16[1024,2048]{1,0:T(8,128)(2,1)S(1)} %bitcast.163, f32[577,1024]{1,0:T(8,128)S(1)} %get-tuple-element.88, f32[1024]{0:T(1024)S(1)} %add.166, f32[1024]{0:T(1024)S(1)} %mul.167, f32[577]{0:T(1024)S(1)} %get-tuple-element.85, ...), kind=kOutput, calls=%fused_computation.6 | convolution fusion | flops 2431339520 | bytes 13668872 | tf_op jit(solution)/shard_map/dot_general | solution.py:887
  200.4 1.5 copy-done.26
  201.9 4.1 fusion.41
  205.9 6.3 %add_convert_fusion.2 = bf16[577,1024]{1,0:T(8,128)(2,1)S(1)} fusion(f32[577,1024]{1,0:T(8,128)S(1)} %get-tuple-element.88, f32[577,1024]{1,0:T(8,128)} %fusion.41, bf16[577,2048]{1,0:T(8,128)(2,1)} %get-tuple-element.91, bf16[1024,2048]{1,0:T(8,128)(2,1)} %bitcast.165, f32[1024]{0:T(1024)S(1)} %add.179), kind=kOutput, calls=%fused_computation.43 | convolution fusion | flops 2422476800 | bytes 12470272 | tf_op jit(solution)/shard_map/dot_general | solution.py:887
  212.2 1.2 constant_dynamic-slice_fusion.3
  213.4 1.5 collective-permute-start
  214.9 1.5 fusion.65
  216.4 2.5 copy.54
  219.0 2.7 copy.55
  221.7 4.7 pad_maximum_fusion.refs_5_
  226.5 6.0 %fusion.40 = (bf16[2048]{0:T(1024)(128)(2,1)S(1)}, bf16[577,2048]{1,0:T(8,128)(2,1)S(1)}) fusion(f32[577,2048]{1,0:T(8,128)S(1)} %copy-done.49, f32[2048]{0:T(1024)S(1)} %bitcast.201, bf16[1024,2048]{1,0:T(8,128)(2,1)S(1)} %bitcast.168, bf16[577,512]{1,0:T(8,128)(2,1)} %collective-permute-done.1, bf16[577,512]{1,0:T(8,128)(2,1)S(1)} %copy-done.5, pred[]{:T(512)S(6)} %eq.4), kind=kOutput, calls=%fused_computation.128 | convolution fusion | flops 2439609344 | bytes 12478465 | tf_op jit(solution)/shard_map/dot_general | solution.py:887
  232.5 2.7 fusion.42
  235.6 5.4 %fusion.39 = (bf16[2048]{0:T(1024)(128)(2,1)S(1)}, bf16[577,2048]{1,0:T(8,128)(2,1)S(1)}) fusion(f32[577,2048]{1,0:T(8,128)S(1)} %bitcast.205, f32[2048]{0:T(1024)S(1)} %bitcast.199, bf16[1024,2048]{1,0:T(8,128)(2,1)S(1)} %bitcast.166, bf16[577,512]{1,0:T(8,128)(2,1)} %collective-permute-done.1, bf16[577,512]{1,0:T(8,128)(2,1)S(1)} %copy-done.5, pred[]{:T(512)S(6)} %eq.4), kind=kOutput, calls=%fused_computation.127 | convolution fusion | flops 2439609344 | bytes 12478465 | tf_op jit(solution)/shard_map/dot_general | solution.py:887
  241.0 3.6 multiply_reduce_fusion
  244.6 3.2 fusion.32
  248.0 1.0 copy-done.15
  249.1 0.8 fusion.20
  250.7 0.8 fusion.21
  251.5 1.1 pad_maximum_fusion.6.upstream_ref
  252.7 28.1 %attention_back.1 = bf16[2,577,1536]{2,1,0:T(8,128)(2,1)} custom-call(bf16[2,577,1536]{2,1,0:T(8,128)(2,1)} %pad_maximum_fusion.2.projected_ref, bf16[2,577,512]{2,1,0:T(8,128)(2,1)} %pad_maximum_fusion.6.upstream_ref), custom_call_target="tpu_custom_call" | custom-call | tf_op jit(solution)/shard_map/attention_back/pallas_call | solution.py:386
  280.8 4.6 fusion.2
  285.5 4.5 convolution_convert_fusion
  290.0 4.8 %convolution_convert_fusion.1 = bf16[1024,1536]{1,0:T(8,128)(2,1)} fusion(bf16[2,577,1536]{2,1,0:T(8,128)(2,1)S(1)} %copy-done, f32[1024]{0:T(1024)S(1)} %add.151, f32[1024]{0:T(1024)S(1)} %mul.160, f32[577]{0:T(1024)S(1)} %get-tuple-element.87, f32[577]{0:T(1024)S(1)} %get-tuple-element.86, bf16[577,512]{1,0:T(8,128)(2,1)S(1)} %copy-done.3, ...), kind=kOutput, calls=%fused_computation.13 | convolution fusion | flops 1821975552 | bytes 6152192 | tf_op jit(solution)/shard_map/dot_general | solution.py:887
  294.8 2.0 convolution_convert_fusion.2
  296.8 5.8 %fusion.12 = (f32[577]{0:T(1024)S(1)}, bf16[1024]{0:T(1024)(128)(2,1)S(1)}, f32[577]{0:T(1024)S(1)}, bf16[1024]{0:T(1024)(128)(2,1)S(1)}, f32[577,1024]{1,0:T(8,128)}) fusion(f32[1024]{0:T(1024)S(1)} %mul.160, f32[577]{0:T(1024)S(1)} %get-tuple-element.87, f32[577]{0:T(1024)S(1)} %get-tuple-element.86, bf16[577,512]{1,0:T(8,128)(2,1)S(1)} %copy-done.3, ...), kind=kOutput, calls=%fused_computation.33 | convolution fusion | flops 1823353600 | bytes 10912264 | tf_op jit(solution)/shard_map/dot_general | solution.py:887
  302.8 2.6 reduce.3
  305.8 3.1 fusion.26
  309.4 5.2 %pad_maximum_fusion.1.refs_7_ = bf16[2,577,2048]{2,1,0:T(8,128)(2,1)} fusion(bf16[1,577,2048]{2,1,0:T(8,128)(2,1)} %bitcast.174, bf16[1,577,2048]{2,1,0:T(8,128)(2,1)} %bitcast.173), kind=kLoop, calls=%fused_computation.1 | loop fusion | flops 2363392 | bytes 9453568 | tf_op jit(solution)/shard_map/stack | solution.py:1061
  314.6 2.1 pad_maximum_fusion.4.refs_3_
  316.7 1.0 copy-done.16
  317.7 2.1 pad_maximum_fusion.3.refs_2_
  319.8 1.0 copy-done.22
  320.8 1.9 fusion.16.refs_8_
  322.8 2.0 convolution_convert_fusion.3
  324.8 0.7 copy.52
  325.5 1.2 copy.53
  326.7 136.9 %scatter_grads.1 = (f32[64,512]{1,0:T(8,128)}, f32[64,1664]{1,0:T(8,128)}, f32[64,2048]{1,0:T(8,128)}, f32[64,2048]{1,0:T(8,128)}, bf16[2,577,512]{2,1,0:T(8,128)(2,1)}) custom-call(bf16[4,2,2,64,512]{4,3,2,1,0:T(8,128)(2,1)} %bitcast.179, bf16[4,2,2,64,512]{4,3,2,1,0:T(8,128)(2,1)} %bitcast.178, bf16[4,2,2,64,1664]{4,3,2,1,0:T(8,128)(2,1)} %pad_maximum_fusion.3.refs_2_, ...), custom_call_target="tpu_custom_call" | custom-call | tf_op jit(solution)/shard_map/scatter_grads/pallas_call | solution.py:838
  463.6 1.0 slice.217
  464.6 0.7 slice.214
  465.3 3.0 reshape.253
  468.7 0.9 reshape.252
  470.2 1.2 slice_bitcast_fusion.25
  471.9 2.7 maximum_select_fusion.1
  475.3 0.8 copy.72
  476.1 0.8 copy.73
  (180 shorter events, 8.4 us)
Async XLA Ops:
  0.6 4.3 copy-start.47
  0.7 4.3 copy-start.42
  0.7 4.3 copy-start.41
  0.7 4.3 copy-start.44
  0.7 4.3 copy-start.43
  0.7 4.3 copy-start.46
  0.7 4.3 copy-start.45
  0.7 4.4 copy-start.48
  0.7 4.4 copy-start.38
  0.7 4.9 %copy-start.31 = (bf16[1154,512]{1,0:T(8,128)(2,1)S(1)}, bf16[1154,512]{1,0:T(8,128)(2,1)}, u32[]{:S(2)}) copy-start(bf16[1154,512]{1,0:T(8,128)(2,1)} %param.14) | copy-start | bytes 3545092
  3.4 3.5 copy-start.34
  3.4 223.0 %collective-permute-start.1 = (bf16[577,512]{1,0:T(8,128)(2,1)}, bf16[577,512]{1,0:T(8,128)(2,1)}, u32[]{:S(2)}, u32[]{:S(2)}) collective-permute-start(bf16[577,512]{1,0:T(8,128)(2,1)} %get-tuple-element.63), channel_id=1, source_target_pairs={{0,1},{1,0},{2,3},{3,2},{4,5},{5,4},{6,7},{7,6},{8,9},{9,8},{10,11... | collective-permute-start | bytes 1772552 | tf_op jit(solution)/shard_map/ppermute | solution.py:869
  5.2 2.5 copy-start.35
  5.3 3.1 copy-start.39
  141.4 5.5 %copy-start.2 = (bf16[577,512]{1,0:T(8,128)(2,1)}, bf16[577,512]{1,0:T(8,128)(2,1)S(1)}, u32[]{:S(2)}) copy-start(bf16[577,512]{1,0:T(8,128)(2,1)S(1)} %get-tuple-element.61) | copy-start | bytes 1772548
  172.5 12.7 %copy-start.14 = (bf16[1,4,2,2,64,512]{5,4,3,2,1,0:T(8,128)(2,1)}, bf16[1,4,2,2,64,512]{5,4,3,2,1,0:T(8,128)(2,1)S(1)}, u32[]{:S(2)}) copy-start(bf16[1,4,2,2,64,512]{5,4,3,2,1,0:T(8,128)(2,1)S(1)} %get-tuple-element.55) | copy-start | bytes 3145732
  178.9 6.3 %copy-start.18 = (bf16[2,577,512]{2,1,0:T(8,128)(2,1)S(1)}, bf16[2,577,512]{2,1,0:T(8,128)(2,1)}, u32[]{:S(2)}) copy-start(bf16[2,577,512]{2,1,0:T(8,128)(2,1)} %attention_forward.1) | copy-start | bytes 3545092
  185.2 1.3 copy-start.19
  185.2 1.6 copy-start.32
  186.7 2.4 copy-start.7
  189.1 51.9 %copy-start.1 = (f32[577,1024]{1,0:T(8,128)}, f32[577,1024]{1,0:T(8,128)S(1)}, u32[]{:S(2)}) copy-start(f32[577,1024]{1,0:T(8,128)S(1)} %get-tuple-element.88) | copy-start | bytes 7090180
  189.1 5.9 %copy-start.9 = (bf16[1,4,2,2,64,2048]{5,4,3,2,1,0:T(8,128)(2,1)S(1)}, bf16[1,4,2,2,64,2048]{5,4,3,2,1,0:T(8,128)(2,1)}, u32[]{:S(2)}) copy-start(bf16[1,4,2,2,64,2048]{5,4,3,2,1,0:T(8,128)(2,1)} %get-tuple-element.53) | copy-start | bytes 12582916
  195.0 6.8 %copy-start.12 = (bf16[1,4,2,2,64,2048]{5,4,3,2,1,0:T(8,128)(2,1)S(1)}, bf16[1,4,2,2,64,2048]{5,4,3,2,1,0:T(8,128)(2,1)}, u32[]{:S(2)}) copy-start(bf16[1,4,2,2,64,2048]{5,4,3,2,1,0:T(8,128)(2,1)} %get-tuple-element.51) | copy-start | bytes 12582916
  200.4 1.5 copy-start.26
  213.4 258.5 %collective-permute-start = (bf16[577,512]{1,0:T(8,128)(2,1)}, bf16[577,512]{1,0:T(8,128)(2,1)}, u32[]{:S(2)}, u32[]{:S(2)}) collective-permute-start(bf16[577,512]{1,0:T(8,128)(2,1)} %get-tuple-element.59), channel_id=1, source_target_pairs={{0,1},{1,0},{2,3},{3,2},{4,5},{5,4},{6,7},{7,6},{8,9},{9,8},{10,11... | collective-permute-start | bytes 1772552 | tf_op jit(solution)/shard_map/ppermute | solution.py:880
  219.0 2.7 copy-start.25
  219.0 7.5 %copy-start.49 = (f32[577,2048]{1,0:T(8,128)S(1)}, f32[577,2048]{1,0:T(8,128)}, u32[]{:S(2)}) copy-start(f32[577,2048]{1,0:T(8,128)} %get-tuple-element.90) | copy-start | bytes 14180356
  221.7 4.8 copy-start.5
  221.7 4.8 copy-start.13
  221.7 13.5 %slice-start = ((s8[4784128]{0:T(1024)(128)(4,1)}), s8[4194304]{0:T(1024)(128)(4,1)S(1)}, s32[]{:S(2)}) async-start(s8[4784128]{0:T(1024)(128)(4,1)} %bitcast.204), calls=%async_computation | async-start | bytes 8388608
  226.5 6.0 %copy-start.10 = (bf16[1,4,2,2,64,2048]{5,4,3,2,1,0:T(8,128)(2,1)S(1)}, bf16[1,4,2,2,64,2048]{5,4,3,2,1,0:T(8,128)(2,1)}, u32[]{:S(2)}) copy-start(bf16[1,4,2,2,64,2048]{5,4,3,2,1,0:T(8,128)(2,1)} %get-tuple-element.53) | copy-start | bytes 12582916
  226.5 8.7 %slice-start.1 = ((s8[4784128]{0:T(1024)(128)(4,1)}), s8[589824]{0:T(1024)(128)(4,1)S(1)}, s32[]{:S(2)}) async-start(s8[4784128]{0:T(1024)(128)(4,1)} %bitcast.204), calls=%async_computation.1 | async-start | bytes 1179648
  232.5 2.7 copy-start.23
  232.5 3.1 copy-start.11
  235.6 5.4 %copy-start.8 = (bf16[1,4,2,2,64,2048]{5,4,3,2,1,0:T(8,128)(2,1)S(1)}, bf16[1,4,2,2,64,2048]{5,4,3,2,1,0:T(8,128)(2,1)}, u32[]{:S(2)}) copy-start(bf16[1,4,2,2,64,2048]{5,4,3,2,1,0:T(8,128)(2,1)} %get-tuple-element.52) | copy-start | bytes 12582916
  241.0 3.6 copy-start.24
  247.9 1.2 copy-start.15
  249.1 1.0 copy-start.28
  249.1 1.7 copy-start.33
  280.8 4.6 copy-start
  280.8 4.7 copy-start.3
  290.0 4.8 %copy-start.20 = (bf16[2,577,512]{2,1,0:T(8,128)(2,1)S(1)}, bf16[2,577,512]{2,1,0:T(8,128)(2,1)}, u32[]{:S(2)}) copy-start(bf16[2,577,512]{2,1,0:T(8,128)(2,1)} %attention_forward.1) | copy-start | bytes 3545092
  290.0 4.8 %copy-start.29 = (bf16[577,1024]{1,0:T(8,128)(2,1)S(1)}, bf16[577,1024]{1,0:T(8,128)(2,1)}, u32[]{:S(2)}) copy-start(bf16[577,1024]{1,0:T(8,128)(2,1)} %copy-done.28) | copy-start | bytes 3545092
  309.4 5.2 %copy-start.17 = (bf16[1024,1536]{1,0:T(8,128)(2,1)S(1)}, bf16[1024,1536]{1,0:T(8,128)(2,1)}, u32[]{:S(2)}) copy-start(bf16[1024,1536]{1,0:T(8,128)(2,1)} %convolution_convert_fusion) | copy-start | bytes 9437188
  314.6 3.1 copy-start.16
  317.7 2.1 copy-start.4
  317.7 3.1 copy-start.22
  320.8 2.0 copy-start.21
  320.8 2.0 copy-start.30
  322.8 2.0 copy-start.6
  465.3 6.7 %copy-start.27 = (bf16[577,512]{1,0:T(8,128)(2,1)S(1)}, bf16[577,512]{1,0:T(8,128)(2,1)}, u32[]{:S(2)}) copy-start(bf16[577,512]{1,0:T(8,128)(2,1)} %get-tuple-element.58) | copy-start | bytes 1772548
  468.3 6.4 %copy-start.40 = (f32[64,512]{1,0:T(8,128)S(1)}, f32[64,512]{1,0:T(8,128)}, u32[]{:S(2)}) copy-start(f32[64,512]{1,0:T(8,128)} %get-tuple-element.31) | copy-start | bytes 393220
  468.5 6.8 %copy-start.37 = (f32[64,2048]{1,0:T(8,128)S(1)}, f32[64,2048]{1,0:T(8,128)}, u32[]{:S(2)}) copy-start(f32[64,2048]{1,0:T(8,128)} %get-tuple-element.129) | copy-start | bytes 1572868
  468.7 7.5 %copy-start.36 = (f32[64,2048]{1,0:T(8,128)S(1)}, f32[64,2048]{1,0:T(8,128)}, u32[]{:S(2)}) copy-start(f32[64,2048]{1,0:T(8,128)} %get-tuple-element.33) | copy-start | bytes 1572868
